TPU v7x, 32 devices: a whole 2x2x4 slice. The times are simulated.
32 devices in a mesh: row: 8 (over z, y), col: 2 (over core), layer: 2 (over x).
Axes of the slice: x: 2, y: 2, z: 4, core: 2. Of those that a mesh axis runs over, the one named last changes fastest.
Arguments:
- matrix: float32 [1, 8, 256, 4, 2, 256], P(None, 'row', None, None, 'col'), may hold values from -8 to 113.137085, as said below
Outputs:
- factored: float32 [1, 8, 256, 4, 2, 256], P(None, 'row', None, 'layer', 'col')
Inputs may be any that keep to these rules, and one draw needn't show every extreme that they name: `matrix`: viewed as in the first step it is symmetric, its leading 2 * 256 x 2 * 256 block is positive definite, and its diagonal entries lie between 2.5 and 5 times the square root of 512.
All inputs are finite; a program needn't handle non-finite values.
Results may differ from a plain program's by a relative error of at most 0.000059.
Values sent between devices are 32-bit elements; how exact they have to be, the bound alone decides.
No kernel may reach another device: no remote copies, remote signals or barrier semaphores. Data moves between devices by JAX's collectives and lax.ppermute only.
A program may use at most 128 MiB of HBM per device.

v0:
```python
import jax
import jax.numpy as jnp
from jax import lax
from jax.sharding import PartitionSpec as P

HIGH = lax.Precision.HIGHEST


def from_root(shard, axis, root):
    mine = lax.axis_index(axis) == root
    return lax.psum(jnp.where(mine, shard, jnp.zeros_like(shard)), axis)


def factor_block(diag_block):
    lower_fac = jnp.linalg.cholesky(diag_block)
    identity = jnp.eye(diag_block.shape[0], dtype=jnp.float32)
    inverse = lax.linalg.triangular_solve(lower_fac, identity, left_side=True, lower=True)
    return (lower_fac, inverse)


def on_device(matrix):
    row_total = lax.axis_size("row")
    col_total = lax.axis_size("col")
    layer_total = lax.axis_size("layer")
    grid_row = lax.axis_index("row")
    grid_col = lax.axis_index("col")
    grid_layer = lax.axis_index("layer")
    row_blocks = matrix.shape[0]
    block_size = matrix.shape[2]
    col_blocks = matrix.shape[3]
    half = block_size // layer_total
    owned = col_blocks // layer_total
    rows = row_blocks * block_size
    tile = matrix.reshape(rows, col_blocks * block_size)
    row_ids = jnp.arange(rows) // block_size * row_total + grid_row
    column = tile[:, :block_size]
    pending = None
    total = None
    panels = []
    for section in range(2):
        diag_block = from_root(column, "row", section % row_total)
        lower_fac, inverse = factor_block(diag_block)
        solved = jnp.dot(column, inverse.T, precision=HIGH, preferred_element_type=jnp.float32)
        repeated = jnp.tile(lower_fac, (row_blocks, 1))
        complete = jnp.where(
            row_ids[:, None] > section,
            solved,
            jnp.where(row_ids[:, None] == section, repeated, 0.0),
        )
        panels.append(complete)
        share = lax.dynamic_slice_in_dim(complete, grid_layer * half, half, 1)
        share = from_root(share, "col", section % col_total)
        gathered = lax.all_gather(
            share.reshape(row_blocks, 1, block_size, half), "row", axis=1, tiled=True
        )
        grouped = gathered.reshape(col_blocks, col_total, block_size, half)
        picked = lax.dynamic_index_in_dim(grouped, grid_col, 1, keepdims=False).reshape(
            col_blocks * block_size, half
        )
        update = lax.dot_general(
            share,
            picked,
            (((1,), (1,)), ((), ())),
            precision=HIGH,
            preferred_element_type=jnp.float32,
        )
        if section == 0:
            head = lax.psum(update[:, :block_size], "layer")
            column = tile[:, :block_size] - head
            pending = update
        else:
            total = pending + update
    reduced = lax.psum_scatter(
        total.reshape(rows, col_blocks, block_size), "layer", scatter_dimension=1, tiled=True
    )
    own_part = (
        lax.dynamic_slice_in_dim(
            tile.reshape(rows, col_blocks, block_size), grid_layer * owned, owned, 1
        )
        - reduced
    )
    replacement = jnp.where(grid_col == 0, panels[0], panels[1])
    global_ids = (grid_layer * owned + jnp.arange(owned)) * col_total + grid_col
    result = jnp.where((global_ids < 2)[None, :, None], replacement[:, None, :], own_part)
    return result.reshape(row_blocks, 1, block_size, owned, 1, block_size)


def solution(mesh):
    in_specs = (P(None, "row", None, None, "col", None),)
    out_specs = P(None, "row", None, "layer", "col", None)
    return jax.shard_map(
        on_device, mesh=mesh, in_specs=in_specs, out_specs=out_specs, check_vma=False
    )
```

profile of v0, /device:TPU:0, one launch (start us, length us, event | category | flops | bytes accessed | tf_op | source)
XLA Modules:
  0.0 472.4 jit_solution(6674159370767984335)
XLA Ops:
  6.5 2.3 copy.16
  9.8 74.7 %all-reduce.7.cloned.1.call-done = f32[256,256]{0,1:T(8,128)} async-done(((f32[256,256]{0,1:T(8,128)}), f32[256,256]{0,1:T(8,128)}) %all-reduce.7.cloned.1.call-update) | async-done | bytes 262160 | tf_op jit(solution)/shard_map/psum | solution.py:11
  84.4 1.1 copy.17
  85.7 11.7 %cholesky.130 = f32[128,128]{1,0:T(8,128)S(1)} custom-call(f32[128,128]{1,0:T(8,128)S(1)} %cholesky.194), custom_call_target="Cholesky" | custom-call | tf_op jit(solution)/shard_map/jit(cholesky)/cholesky | solution.py:15
  97.4 9.8 %custom-call.13 = f32[1,128,128]{1,2,0:T(8,128)S(1)} custom-call(f32[1,128,128]{2,1,0:T(8,128)S(1)} %get-tuple-element.62), custom_call_target="InvertDiagBlocksLowerTriangular" | custom-call | tf_op jit(solution)/shard_map/jit(cholesky)/cholesky | solution.py:15
  107.7 11.7 %cholesky.147 = f32[128,128]{1,0:T(8,128)S(1)} custom-call(f32[128,128]{1,0:T(8,128)S(1)} %convolution_subtract_fusion.3), custom_call_target="Cholesky" | custom-call | tf_op jit(solution)/shard_map/jit(cholesky)/cholesky | solution.py:15
  122.0 4.5 while.4
  122.8 1.4 dynamic-slice.13
  125.0 1.4 dynamic-slice.13
  126.5 19.7 %custom-call.14 = f32[2,128,128]{1,2,0:T(8,128)S(1)} custom-call(f32[2,128,128]{2,1,0:T(8,128)S(1)} %get-tuple-element.21), custom_call_target="InvertDiagBlocksLowerTriangular" | custom-call | tf_op jit(solution)/shard_map/triangular_solve/custom-call.0 | solution.py:17
  148.3 17.2 %all-reduce.9.cloned.1.call-done = f32[256,128]{0,1:T(8,128)} async-done(((f32[256,128]{0,1:T(8,128)}), f32[256,128]{0,1:T(8,128)}) %all-reduce.9.cloned.1.call-update) | async-done | bytes 131088 | tf_op jit(solution)/shard_map/psum | solution.py:11
  165.6 42.6 %all-gather.5.cloned.1.call-done = f32[2048,128]{0,1:T(8,128)} async-done(((f32[256,128]{0,1:T(8,128)}), f32[2048,128]{0,1:T(8,128)}) %all-gather.5.cloned.1.call-update) | async-done | bytes 1048592 | tf_op jit(solution)/shard_map/all_gather | solution.py:53
  208.2 2.1 reshape.86
  210.3 1.6 dynamic-slice_reduce_fusion.1
  214.8 22.4 %all-reduce.11.cloned.1.call-done = f32[256,256]{0,1:T(8,128)} async-done(((f32[256,256]{0,1:T(8,128)}), f32[256,256]{0,1:T(8,128)}) %all-reduce.11.cloned.1.call-update) | async-done | bytes 262160 | tf_op jit(solution)/shard_map/psum | solution.py:68
  237.2 1.7 broadcast_select_fusion
  239.2 72.3 %all-reduce.13.cloned.1.call-done = f32[256,256]{0,1:T(8,128)} async-done(((f32[256,256]{0,1:T(8,128)}), f32[256,256]{0,1:T(8,128)}) %all-reduce.13.cloned.1.call-update) | async-done | bytes 262160 | tf_op jit(solution)/shard_map/psum | solution.py:11
  312.7 11.7 %cholesky.164 = f32[128,128]{1,0:T(8,128)S(1)} custom-call(f32[128,128]{1,0:T(8,128)S(1)} %cholesky.197), custom_call_target="Cholesky" | custom-call | tf_op jit(solution)/shard_map/jit(cholesky)/cholesky | solution.py:15
  324.5 9.8 %custom-call.15 = f32[1,128,128]{1,2,0:T(8,128)S(1)} custom-call(f32[1,128,128]{2,1,0:T(8,128)S(1)} %get-tuple-element.60), custom_call_target="InvertDiagBlocksLowerTriangular" | custom-call | tf_op jit(solution)/shard_map/jit(cholesky)/cholesky | solution.py:15
  334.8 11.7 %cholesky.181 = f32[128,128]{1,0:T(8,128)S(1)} custom-call(f32[128,128]{1,0:T(8,128)S(1)} %convolution_subtract_fusion.2), custom_call_target="Cholesky" | custom-call | tf_op jit(solution)/shard_map/jit(cholesky)/cholesky | solution.py:15
  349.5 4.4 while.5
  350.4 1.4 dynamic-slice.15
  352.5 1.4 dynamic-slice.15
  354.0 19.7 %custom-call.16 = f32[2,128,128]{1,2,0:T(8,128)S(1)} custom-call(f32[2,128,128]{2,1,0:T(8,128)S(1)} %get-tuple-element.22), custom_call_target="InvertDiagBlocksLowerTriangular" | custom-call | tf_op jit(solution)/shard_map/triangular_solve/custom-call.0 | solution.py:17
  376.4 17.2 %all-reduce.15.cloned.1.call-done = f32[256,128]{0,1:T(8,128)} async-done(((f32[256,128]{0,1:T(8,128)}), f32[256,128]{0,1:T(8,128)}) %all-reduce.15.cloned.1.call-update) | async-done | bytes 131088 | tf_op jit(solution)/shard_map/psum | solution.py:11
  393.7 42.6 %all-gather.7.cloned.1.call-done = f32[2048,128]{0,1:T(8,128)} async-done(((f32[256,128]{0,1:T(8,128)}), f32[2048,128]{0,1:T(8,128)}) %all-gather.7.cloned.1.call-update) | async-done | bytes 1048592 | tf_op jit(solution)/shard_map/all_gather | solution.py:53
  436.3 2.1 reshape.89
  438.4 1.6 dynamic-slice_reduce_fusion
  443.1 1.2 copy-done
  444.8 17.9 %reduce-scatter.2.cloned.1.call-done = f32[256,2,256]{2,0,1:T(8,128)} async-done(((f32[256,4,256]{2,0,1:T(8,128)}), f32[256,2,256]{2,0,1:T(8,128)}) %reduce-scatter.2.cloned.1.call-update) | async-done | bytes 524304 | tf_op jit(solution)/shard_map/reduce_scatter | solution.py:73
  462.6 1.2 fusion.2
  463.8 1.3 copy.32
  (101 shorter events, 20.2 us)
Async XLA Ops:
  6.5 77.9 %all-reduce.7.cloned.1.call-start = ((), (), s32[]{:S(2)}) async-start(), calls=%async_computation.1 | async-start | bytes 524288 | tf_op jit(solution)/shard_map/psum | solution.py:11
  9.6 155.9 %all-reduce.9.cloned.1.call-start = ((), (), s32[]{:S(2)}) async-start(), calls=%async_computation.2 | async-start | bytes 262144 | tf_op jit(solution)/shard_map/psum | solution.py:11
  84.4 1.2 copy-start.1
  148.2 59.9 %all-gather.5.cloned.1.call-start = ((), (), s32[]{:S(2)}) async-start(), calls=%async_computation.7 | async-start | bytes 1179648 | tf_op jit(solution)/shard_map/all_gather | solution.py:53
  165.5 71.7 %all-reduce.11.cloned.1.call-start = ((), (), s32[]{:S(2)}) async-start(), calls=%async_computation.3 | async-start | bytes 524288 | tf_op jit(solution)/shard_map/psum | solution.py:68
  211.9 0.9 copy-start.4
  214.7 96.7 %all-reduce.13.cloned.1.call-start = ((), (), s32[]{:S(2)}) async-start(), calls=%async_computation.4 | async-start | bytes 524288 | tf_op jit(solution)/shard_map/psum | solution.py:11
  238.9 154.7 %all-reduce.15.cloned.1.call-start = ((), (), s32[]{:S(2)}) async-start(), calls=%async_computation.5 | async-start | bytes 262144 | tf_op jit(solution)/shard_map/psum | solution.py:11
  311.5 1.2 copy-start.2
  374.3 1.0 copy-start.3
  376.4 59.9 %all-gather.7.cloned.1.call-start = ((), (), s32[]{:S(2)}) async-start(), calls=%async_computation.8 | async-start | bytes 1179648 | tf_op jit(solution)/shard_map/all_gather | solution.py:53
  393.6 69.0 %reduce-scatter.2.cloned.1.call-start = ((), (), s32[]{:S(2)}) async-start(), calls=%async_computation.6 | async-start | bytes 1572864 | tf_op jit(solution)/shard_map/reduce_scatter | solution.py:73
  440.0 0.9 copy-start.5
  443.1 1.2 copy-start
Sparse Core Ops, SparseCore 0:
  10.7 73.7 all-reduce.6
  148.4 17.0 all-reduce.8
  167.6 40.5 all-gather.4
  214.9 22.2 all-reduce.10
  240.4 71.0 all-reduce.12
  376.5 17.0 all-reduce.14
  395.7 40.5 all-gather.6
  443.2 19.3 reduce-scatter.1
where the time goes:
time: 481 us; the launch traced here: 472 us
  waiting for transfers between devices  307 us (64%)
  other arithmetic  113 us (23%)
  local copies, waits for them, and re-layouts  28.5 us (6%)
  between operations  17 us (4%)
  matrix products  5.65 us (1%)
    psum x4, waiting for transfers between devices, from_root(): return lax.psum(jnp.where(mine, shard, jnp.zeros_like(shard)), axis)  181 us
    all_gather x2, waiting for transfers between devices, on_device(): lax.all_gather(share.reshape(row_blocks, 1, block_size, half), 'row', axi...  85.2 us
    another operation x13, other arithmetic, factor_block(): lower_fac = jnp.linalg.cholesky(diag_block)  68.7 us
    another operation x5, other arithmetic, factor_block(): lax.linalg.triangular_solve(lower_fac, identity, left_side=True, lower=True)  39.4 us
    psum x1, waiting for transfers between devices, on_device(): head = lax.psum(update[:, :block_size], 'layer')  22.4 us
    reduce_scatter x1, waiting for transfers between devices, on_device(): lax.psum_scatter(total.reshape(rows, col_blocks, block_size), 'layer', sc...  17.9 us
  transfers between devices with their start and end apart: 8, of which 8 were waited for; matrix products, arithmetic and copies ran while one was open for 0% of the time, Pallas kernels for 0%

commit v1 on v0

v1 whole, which is shorter than its diff:
```python
import functools

import jax
import jax.numpy as jnp
from jax import lax
from jax.experimental import pallas as pl
from jax.experimental.pallas import tpu as pltpu
from jax.sharding import PartitionSpec as P

HIGH = lax.Precision.HIGHEST
F32 = jnp.float32
AXES = ("row", "col", "layer")
VMEM = pl.BlockSpec(memory_space=pltpu.VMEM)
SMEM = pl.BlockSpec(memory_space=pltpu.SMEM)
LANES = 128
SUB = 8


def contract(left, right, ldim, rdim):
    return lax.dot_general(
        left,
        right,
        (((ldim,), (rdim,)), ((), ())),
        precision=HIGH,
        preferred_element_type=F32,
    )


def nn(a, b):
    return contract(a, b, 1, 0)


def nt(a, b):
    return contract(a, b, 1, 1)


def tn(a, b):
    return contract(a, b, 0, 0)


def row_of(tile, k):
    return jnp.broadcast_to(tile[k : k + 1, :], tile.shape)


def small_inverse(block):
    size = block.shape[0]
    tiles = size // SUB
    width = 2 * size
    rows = lax.broadcasted_iota(jnp.int32, (size, size), 0)
    cols = lax.broadcasted_iota(jnp.int32, (size, size), 1)
    eye = jnp.where(rows == cols, 1.0, 0.0).astype(F32)
    full = jnp.concatenate([block, eye], axis=1)
    v = [full[SUB * t : SUB * (t + 1)] for t in range(tiles)]
    sub = lax.broadcasted_iota(jnp.int32, (SUB, width), 0)
    for s in range(tiles):
        c = {
            (j, t): jnp.broadcast_to(v[t][:, SUB * s + j : SUB * s + j + 1], (SUB, width))
            for j in range(SUB)
            for t in range(s, tiles)
        }
        pivots = jnp.ones((SUB, width), F32)
        for k in range(0, SUB, 2):
            p = row_of(c[k, s], k)
            q = row_of(c[k, s], k + 1)
            w = row_of(c[k + 1, s], k + 1)
            det = p * w - q * q
            over_det = 1.0 / det
            over_p = 1.0 / p
            v0, v1 = row_of(v[s], k), row_of(v[s], k + 1)
            c0 = {j: row_of(c[j, s], k) for j in range(k + 2, SUB)}
            c1 = {j: row_of(c[j, s], k + 1) for j in range(k + 2, SUB)}
            pivots = jnp.where(sub == k, p, jnp.where(sub == k + 1, det * over_p, pivots))
            for t in range(s, tiles):
                m0 = (w * c[k, t] - q * c[k + 1, t]) * over_det
                m1 = (p * c[k + 1, t] - q * c[k, t]) * over_det
                if t == s:
                    m0 = jnp.where(sub > k + 1, m0, jnp.where(sub == k + 1, q * over_p, 0.0))
                    m1 = jnp.where(sub > k + 1, m1, 0.0)
                v[t] = v[t] - m0 * v0 - m1 * v1
                for j in range(k + 2, SUB):
                    c[j, t] = c[j, t] - m0 * c0[j] - m1 * c1[j]
        v[s] = v[s] * lax.rsqrt(pivots)
    return jnp.concatenate(v, axis=0)[:, size:]


def inverse_factor(a, x):
    n = a.shape[0]
    base = min(n, LANES // 2)
    x[...] = jnp.zeros((n, n), F32)
    for lo in range(0, n, base):
        hi = lo + base
        inv = small_inverse(a[lo:hi, lo:hi])
        if lo:
            x[lo:hi, :lo] = nn(inv, x[lo:hi, :lo])
        x[lo:hi, lo:hi] = inv
        if hi < n:
            upper = nn(inv, a[lo:hi, hi:])
            a[hi:, hi:] = a[hi:, hi:] - tn(upper, upper)
            x[hi:, :hi] = x[hi:, :hi] - tn(upper, x[lo:hi, :hi])


def first_kernel(row, w00, w01, inv, q, a):
    @pl.when(row[0] == 0)
    def _():
        a[...] = w00[...]
        inverse_factor(a, inv)
        q[...] = nn(inv[...], w01[...])


def second_kernel(row, w11, q, inv, a):
    @pl.when(row[0] == 0)
    def _():
        a[...] = w11[...] - tn(q[...], q[...])
        inverse_factor(a, inv)


def call_first(row, w00, w01):
    n = w00.shape[0]
    block = jax.ShapeDtypeStruct((n, n), F32)
    return pl.pallas_call(
        first_kernel,
        out_shape=(block, block),
        in_specs=[SMEM, VMEM, VMEM],
        out_specs=(VMEM, VMEM),
        scratch_shapes=[pltpu.VMEM((n, n), F32)],
    )(row, w00, w01)


def call_second(row, w11, q):
    n = w11.shape[0]
    return pl.pallas_call(
        second_kernel,
        out_shape=jax.ShapeDtypeStruct((n, n), F32),
        in_specs=[SMEM, VMEM, VMEM],
        out_specs=VMEM,
        scratch_shapes=[pltpu.VMEM((n, n), F32)],
    )(row, w11, q)


def lower_part(x):
    rows = lax.broadcasted_iota(jnp.int32, x.shape, 0)
    cols = lax.broadcasted_iota(jnp.int32, x.shape, 1)
    return jnp.where(rows >= cols, x, 0.0)


def early_kernel(row, wr, tile, wg, inv0, q, p0, t1r, t1g, acc):
    step = pl.program_id(0)

    @pl.when(step == 0)
    def _():
        solved = nt(wr[0], inv0[...])
        solved = jnp.where(row[0] == 0, lower_part(solved), solved)
        p0[...] = solved
        t1r[...] = wr[1] - nn(solved, q[...])

    first, second = wg[0, 0], wg[0, 1]
    p0g = nt(first, inv0[...])
    t1g[0] = second - nn(p0g, q[...])
    acc[0] = tile[0] - nt(p0[...], p0g)


def late_kernel(ids, p0, t1r, t1g, acc, inv1, out, p1):
    step = pl.program_id(0)

    @pl.when(step == 0)
    def _():
        solved = nt(t1r[...], inv1[...])
        solved = jnp.where(ids[0] == 1, lower_part(solved), solved)
        p1[...] = jnp.where(ids[0] == 0, 0.0, solved)

    p1g = nt(t1g[0], inv1[...])
    rest = acc[0] - nt(p1[...], p1g)
    block = ids[1] + step * ids[2]
    out[0] = jnp.where(block == 0, p0[...], jnp.where(block == 1, p1[...], rest))


def whole_spec(shape):
    return pl.BlockSpec(shape, lambda i: (0,) * len(shape))


def step_spec(shape):
    return pl.BlockSpec((1,) + shape, lambda i: (i,) + (0,) * len(shape))


def call_early(row, wr, tiles, wg, inv0, q):
    count, n, _ = tiles.shape
    block = jax.ShapeDtypeStruct((n, n), F32)
    stack = jax.ShapeDtypeStruct((count, n, n), F32)
    return pl.pallas_call(
        early_kernel,
        grid=(count,),
        out_shape=(block, block, stack, stack),
        in_specs=[
            SMEM,
            whole_spec((2, n, n)),
            step_spec((n, n)),
            step_spec((2, n, n)),
            whole_spec((n, n)),
            whole_spec((n, n)),
        ],
        out_specs=(whole_spec((n, n)), whole_spec((n, n)), step_spec((n, n)), step_spec((n, n))),
    )(row, wr, tiles, wg, inv0, q)


def call_late(ids, p0, t1r, t1g, acc, inv1):
    count, n, _ = acc.shape
    return pl.pallas_call(
        late_kernel,
        grid=(count,),
        out_shape=jax.ShapeDtypeStruct((count, n, n), F32),
        in_specs=[
            SMEM,
            whole_spec((n, n)),
            whole_spec((n, n)),
            step_spec((n, n)),
            step_spec((n, n)),
            whole_spec((n, n)),
        ],
        out_specs=step_spec((n, n)),
        scratch_shapes=[pltpu.VMEM((n, n), F32)],
    )(ids, p0, t1r, t1g, acc, inv1)


def rounds_of(edges):
    rounds = []
    for source, target in edges:
        for taken in rounds:
            if all(source != s and target != t for s, t in taken):
                taken.append((source, target))
                break
        else:
            rounds.append([(source, target)])
    return rounds


def spread(x, row, row_total):
    gap = row_total // 2
    while gap:
        pairs = [(r, r + gap) for r in range(0, row_total, 2 * gap)]
        got = lax.ppermute(x, "row", pairs)
        x = jnp.where(row % (2 * gap) == gap, got, x)
        gap //= 2
    return x


def on_device(matrix):
    row_total = lax.axis_size("row")
    col_total = lax.axis_size("col")
    layer_total = lax.axis_size("layer")
    row = lax.axis_index("row")
    col = lax.axis_index("col")
    layer = lax.axis_index("layer")
    n = matrix.shape[2]
    col_blocks = matrix.shape[3]
    owned = col_blocks // layer_total
    levels = row_total // 2
    near = levels // layer_total
    half = n // 2
    swap = [(0, 1), (1, 0)]
    rowid = row[None].astype(jnp.int32)

    def device(r, c, l):
        return (r * col_total + c) * layer_total + l

    def permute(x, triples):
        return lax.ppermute(
            x,
            AXES,
            [(device(a, c, l), device(b, c, l)) for a, b, l in triples for c in range(col_total)],
        )

    tile = matrix.reshape(n, col_blocks, n)
    mine = tile[:, 0]
    other = lax.ppermute(mine, "col", swap)
    wr = jnp.where(col == 0, jnp.stack([mine, other]), jnp.stack([other, mine]))

    edges = []
    for l in range(layer_total):
        for gap in range(1, levels):
            for h in range(max(1, l * near), (l + 1) * near):
                for target in (h + gap, h - gap):
                    if 1 <= target < levels:
                        edges.append(((h, l), (target, l)))
    rounds = rounds_of(edges)
    level = row // 2
    got = []
    for taken in rounds:
        triples = [(2 * s + y, 2 * t + y, l) for (s, l), (t, _) in taken for y in range(2)]
        got.append(permute(mine, triples))
    pieces = jnp.stack(got + [mine])
    table = []
    for l in range(layer_total):
        for t in range(levels):
            line = []
            for h in range(l * near, (l + 1) * near):
                slot = len(rounds)
                for i, taken in enumerate(rounds):
                    if ((h, l), (t, l)) in taken:
                        slot = i
                line.append(slot)
            table.append(line)
    slots = jnp.array(table, jnp.int32)[layer * levels + level]
    held = jnp.take(pieces, slots, axis=0)
    own_tiles = lax.dynamic_slice_in_dim(tile, layer * owned, owned, 1).transpose(1, 0, 2)

    w11 = permute(wr[1], [(1, 0, l) for l in range(layer_total)])

    inv0, q = call_first(rowid, wr[0], wr[1])

    first = spread(jnp.where(col == 0, inv0, q), row, row_total)
    second = lax.ppermute(first, "col", swap)
    inv1 = call_second(rowid, w11, q)

    send = jnp.where(row == 0, own_tiles, held) if near == owned else None
    pair = permute(send, [(r, r ^ 1, l) for r in range(row_total) for l in range(layer_total)])
    even = jnp.where(row % 2 == 0, held, pair)
    odd = jnp.where(row % 2 == 0, pair, held)
    keep = jnp.where(col == 0, even, odd)
    give = jnp.where(col == 0, odd, even)
    taken = lax.ppermute(give, "col", swap)
    wg = jnp.where(col == 0, jnp.stack([keep, taken], 1), jnp.stack([taken, keep], 1))
    top = jnp.where(row == 0, own_tiles, pair)
    bottom = jnp.where(row == 0, 0.0, own_tiles)
    flipped = jnp.stack([top, bottom], 1).transpose(0, 1, 3, 2)
    wg = jnp.where(row < 2, flipped, wg)

    inv0_all = jnp.where(col == 0, first, second)
    q_all = jnp.where(col == 0, second, first)
    p0, t1r, t1g, acc = call_early(rowid, wr, own_tiles, wg, inv0_all, q_all)

    part = jnp.where(col == 0, inv1[:half], inv1[half:])
    part = spread(part, row, row_total)
    rest = lax.ppermute(part, "col", swap)
    inv1_all = jnp.where(
        col == 0, jnp.concatenate([part, rest]), jnp.concatenate([rest, part])
    )
    start = layer * owned * col_total + col
    ids = jnp.stack([row, start, jnp.full_like(row, col_total)]).astype(jnp.int32)
    out = call_late(ids, p0, t1r, t1g, acc, inv1_all)
    return out.transpose(1, 0, 2).reshape(1, 1, n, owned, 1, n)


def solution(mesh):
    in_specs = (P(None, "row", None, None, "col", None),)
    out_specs = P(None, "row", None, "layer", "col", None)
    return jax.shard_map(
        on_device, mesh=mesh, in_specs=in_specs, out_specs=out_specs, check_vma=False
    )
```

time: 481 us -> 90.4 us (0.19); the launches traced: 472 us -> 89.6 us
  waiting for transfers between devices: 307 us -> 5.89 us
  other arithmetic: 113 us -> 14.1 us
  Pallas kernels: 0 us -> 33.2 us
  starting transfers between devices: 0.5 us -> 20.7 us
  between operations: 17 us -> 0.44 us
  local copies, waits for them, and re-layouts: 28.5 us -> 15.2 us
  matrix products: 5.65 us -> 0 us
    psum x5 -> x0, waiting for transfers between devices: 204 us -> none  [the longest x4 181 us: from_root(): return lax.psum(jnp.where(mine, shard, jnp.zeros_like(shard)), axis)]
    another operation x18 -> x4, other arithmetic: 108 us -> 3.05 us  [the longest x2 1.3 us: on_device(): jnp.stack([keep, taken], 1)]
    all_gather x2 -> x0, waiting for transfers between devices: 85.2 us -> none  [on_device(): lax.all_gather(share.reshape(row_blocks, 1, block_size, half), 'row', axi...]
    pallas_call x0 -> x4, Pallas kernels: none -> 33.2 us  [the longest x1 11.4 us: call_second(): pl.pallas_call(second_kernel, out_shape=jax.ShapeDtypeStruct((n, n), F32)...]
    ppermute x0 -> x15, starting transfers between devices: none -> 20.7 us  [the longest x6 16.3 us: spread(): got = lax.ppermute(x, 'row', pairs)]
    reduce_scatter x1 -> x0, waiting for transfers between devices: 17.9 us -> none  [on_device(): lax.psum_scatter(total.reshape(rows, col_blocks, block_size), 'layer', sc...]
    another operation x37 -> x4, local copies, waits for them, and re-layouts: 9.08 us -> 1.57 us  [the longest x3 1.53 us: on_device(): jnp.stack([keep, taken], 1)]
    select_n x4 -> x17, other arithmetic: 3.76 us -> 10.4 us  [the longest x6 2.55 us: spread(): x = jnp.where(row % (2 * gap) == gap, got, x)]
  transfers between devices with their start and end apart: 8 -> 15, of which waited for: 8 -> 4; matrix products, arithmetic and copies ran while one was open for 0% -> 22% of each run, Pallas kernels for 0% -> 25%
where the time goes in v1:
time: 90.4 us; the launch traced here: 89.6 us
  Pallas kernels  33.2 us (37%)
  starting transfers between devices  20.7 us (23%)
  local copies, waits for them, and re-layouts  15.2 us (17%)
  other arithmetic  14.1 us (16%)
  waiting for transfers between devices  5.89 us (7%)
    ppermute x6, starting transfers between devices, spread(): got = lax.ppermute(x, 'row', pairs)  16.3 us
    pallas_call x1, Pallas kernels, call_second(): pl.pallas_call(second_kernel, out_shape=jax.ShapeDtypeStruct((n, n), F32)...  11.4 us
    pallas_call x1, Pallas kernels, call_first(): pl.pallas_call(first_kernel, out_shape=(block, block), in_specs=[SMEM, VM...  11.3 us
    pallas_call x1, Pallas kernels, call_early(): pl.pallas_call(early_kernel, grid=(count,), out_shape=(block, block, stac...  5.81 us
    ppermute x6, waiting for transfers between devices, spread(): got = lax.ppermute(x, 'row', pairs)  5.76 us
    pallas_call x1, Pallas kernels, call_late(): pl.pallas_call(late_kernel, grid=(count,), out_shape=jax.ShapeDtypeStruct...  4.69 us
    unnamed x21, local copies, waits for them, and re-layouts  4.44 us
    ppermute x5, starting transfers between devices, permute(): lax.ppermute(x, AXES, [(device(a, c, l), device(b, c, l)) for a, b, l in...  3.37 us
  transfers between devices with their start and end apart: 15, of which 4 were waited for; matrix products, arithmetic and copies ran while one was open for 22% of the time, Pallas kernels for 25%

profile of v1, /device:TPU:0, one launch (start us, length us, event | category | flops | bytes accessed | tf_op | source)
XLA Modules:
  0.0 89.6 jit_solution(3013001495665279080)
XLA Ops:
  0.0 1.5 %copy.22 = f32[1,1,256,4,1,256]{5,2,3,4,1,0:T(8,128)S(1)} copy(f32[1,1,256,4,1,256]{5,4,3,2,1,0:T(1,128)} %param.2) | data formatting | bytes 2097152 | tf_op args[0]
  6.0 0.9 copy.23
  8.8 1.2 %pad_maximum_fusion = f32[4,256,256]{2,1,0:T(8,128)S(1)} fusion(f32[1,256,256]{2,1,0:T(8,128)S(1)} %get-tuple-element.19, f32[1,256,256]{2,1,0:T(8,128)} %bitcast.56, f32[1,256,256]{2,1,0:T(8,128)} %bitcast.57, f32[1,256,256]{2,1,0:T(8,128)} %bitcast.58), kind=kLoop, calls=%fused_computation.1 | loop fusion | flops 786432 | bytes 2097152 | tf_op jit(solution)/shard_map/stack | solution.py:290
  11.0 0.8 slice_bitcast_fusion
  11.9 1.3 %collective-permute-start.10 = (f32[256,256]{1,0:T(8,128)S(1)}, f32[256,256]{1,0:T(8,128)S(1)}, u32[]{:S(2)}, u32[]{:S(2)}) collective-permute-start(f32[256,256]{1,0:T(8,128)S(1)} %get-tuple-element.23.w01), channel_id=1, source_target_pairs={{4,0},{6,2},{5,1},{7,3}} | collective-permute-start | bytes 786440 | tf_op jit(solution)/shard_map/ppermute | solution.py:266
  13.2 11.3 %shard_map.28 = (f32[256,256]{1,0:T(8,128)}, f32[256,256]{1,0:T(8,128)}) custom-call(s32[1]{0:T(128)} %bitcast.row, f32[256,256]{1,0:T(8,128)} %get-tuple-element.24.w00, f32[256,256]{1,0:T(8,128)} %copy-done.5), custom_call_target="tpu_custom_call" | custom-call | tf_op jit(solution)/shard_map/pallas_call | solution.py:120
  24.5 1.0 %broadcast_select_fusion.9 = f32[256,256]{1,0:T(8,128)S(1)} fusion(f32[256,256]{1,0:T(8,128)} %get-tuple-element.11, f32[256,256]{1,0:T(8,128)} %get-tuple-element.12.q, pred[]{:T(512)S(6)} %eq.21), kind=kLoop, calls=%fused_computation.30 | loop fusion | flops 65536 | bytes 786433 | tf_op jit(solution)/shard_map/jit(_where)/select_n | solution.py:310
  25.5 8.1 %collective-permute-start.6 = (f32[256,256]{1,0:T(8,128)S(1)}, f32[256,256]{1,0:T(8,128)}, u32[]{:S(2)}, u32[]{:S(2)}) collective-permute-start(f32[256,256]{1,0:T(8,128)S(1)} %broadcast_select_fusion.9), channel_id=1, source_target_pairs={{0,16},{1,17},{2,18},{3,19}} | collective-permute-start | bytes 786440 | tf_op jit(solution)/shard_map/ppermute | solution.py:240
  33.7 0.7 copy-done.6
  34.4 11.4 %shard_map.30 = f32[256,256]{1,0:T(8,128)} custom-call(s32[1]{0:T(128)} %bitcast.row, f32[256,256]{1,0:T(8,128)} %copy-done.6, f32[256,256]{1,0:T(8,128)} %get-tuple-element.12.q), custom_call_target="tpu_custom_call" | custom-call | tf_op jit(solution)/shard_map/pallas_call | solution.py:131
  45.8 1.0 %slice_select_fusion = f32[128,256]{1,0:T(8,128)S(1)} fusion(f32[256,256]{1,0:T(8,128)} %shard_map.30, pred[]{:T(512)S(6)} %eq.21), kind=kLoop, calls=%fused_computation.24 | loop fusion | flops 32768 | bytes 393217 | tf_op jit(solution)/shard_map/jit(_where)/select_n | solution.py:331
  46.8 1.4 %collective-permute-start.11 = (f32[128,256]{1,0:T(8,128)S(1)}, f32[128,256]{1,0:T(8,128)S(1)}, u32[]{:S(2)}, u32[]{:S(2)}) collective-permute-start(f32[128,256]{1,0:T(8,128)S(1)} %slice_select_fusion), channel_id=1, source_target_pairs={{0,16},{1,17},{2,18},{3,19}} | collective-permute-start | bytes 393224 | tf_op jit(solution)/shard_map/ppermute | solution.py:240
  48.2 0.8 broadcast_select_fusion.4
  49.0 2.0 %collective-permute-start.7 = (f32[256,256]{1,0:T(8,128)}, f32[256,256]{1,0:T(8,128)}, u32[]{:S(2)}, u32[]{:S(2)}) collective-permute-start(f32[256,256]{1,0:T(8,128)} %broadcast_select_fusion.4), channel_id=1, source_target_pairs={{0,8},{16,24},{1,9},{17,25},{2,10},{18,26},{3,11},{19,27}} | collective-permute-start | bytes 786440 | tf_op jit(solution)/shard_map/ppermute | solution.py:240
  51.3 1.9 %collective-permute-start.12 = (f32[128,256]{1,0:T(8,128)S(1)}, f32[128,256]{1,0:T(8,128)}, u32[]{:S(2)}, u32[]{:S(2)}) collective-permute-start(f32[128,256]{1,0:T(8,128)S(1)} %broadcast_select_fusion.10), channel_id=1, source_target_pairs={{0,8},{16,24},{1,9},{17,25},{2,10},{18,26},{3,11},{19,27}} | collective-permute-start | bytes 393224 | tf_op jit(solution)/shard_map/ppermute | solution.py:240
  53.6 1.0 %copy.10 = f32[2,256,256]{1,2,0:T(8,128)} copy(f32[2,256,256]{2,1,0:T(8,128)S(1)} %broadcast_select_fusion.1) | data formatting | bytes 1048576 | tf_op jit(solution)/shard_map/jit(_where)/select_n | solution.py:317
  54.6 1.2 %select_bitcast_fusion = (f32[2,1,256,256]{2,3,0,1:T(8,128)S(1)}, f32[2,256,256]{1,2,0:T(8,128)}, f32[2,1,256,256]{2,3,0,1:T(8,128)S(1)}, f32[2,1,256,256]{2,3,0,1:T(8,128)}) fusion(f32[2,256,256]{1,2,0:T(8,128)} %copy.10, pred[]{:T(512)S(6)} %eq.21, f32[2,256,256]{1,2,0:T(8,128)S(1)} %copy.6, f32[2,256,256]{1,2,0:T(8,128)S(1)} %collective-permute-done.4, ...), kind=kLoop, calls=%fused_computation.14 | loop fusion | flops 524288 | bytes 4194307 | tf_op jit(solution)/shard_map/stack | solution.py:321
  55.8 1.2 %copy.12 = f32[2,256,256]{2,1,0:T(8,128)S(1)} copy(f32[2,256,256]{1,2,0:T(8,128)} %get-tuple-element.18) | data formatting | bytes 1048576 | tf_op jit(solution)/shard_map/jit(_where)/select_n | solution.py:316
  57.3 1.0 %broadcast_select_fusion.5 = f32[256,256]{1,0:T(8,128)S(1)} fusion(f32[256,256]{1,0:T(8,128)} %collective-permute-done.7, f32[256,256]{1,0:T(8,128)} %broadcast_select_fusion.4, pred[]{:T(512)S(6)} %eq.45), kind=kLoop, calls=%fused_computation.26 | loop fusion | flops 65536 | bytes 786433 | tf_op jit(solution)/shard_map/jit(_where)/select_n | solution.py:241
  58.3 1.3 %collective-permute-start.8 = (f32[256,256]{1,0:T(8,128)S(1)}, f32[256,256]{1,0:T(8,128)S(1)}, u32[]{:S(2)}, u32[]{:S(2)}) collective-permute-start(f32[256,256]{1,0:T(8,128)S(1)} %broadcast_select_fusion.5), channel_id=1, source_target_pairs={{0,4},{8,12},{16,20},{24,28},{1,5},{9,13},{17,21},{25,29},{2,6},{1... | collective-permute-start | bytes 786440 | tf_op jit(solution)/shard_map/ppermute | solution.py:240
  59.6 1.5 %collective-permute-start.13 = (f32[128,256]{1,0:T(8,128)S(1)}, f32[128,256]{1,0:T(8,128)S(1)}, u32[]{:S(2)}, u32[]{:S(2)}) collective-permute-start(f32[128,256]{1,0:T(8,128)S(1)} %broadcast_select_fusion.11), channel_id=1, source_target_pairs={{0,4},{8,12},{16,20},{24,28},{1,5},{9,13},{17,21},{25,29},{2,6},{1... | collective-permute-start | bytes 393224 | tf_op jit(solution)/shard_map/ppermute | solution.py:240
  61.2 0.9 broadcast_select_fusion.2
  62.0 1.0 %copy.14 = f32[2,1,256,256]{3,2,0,1:T(8,128)} copy(f32[2,1,256,256]{2,3,0,1:T(8,128)S(1)} %get-tuple-element.17) | data formatting | bytes 1048576 | tf_op jit(solution)/shard_map/stack | solution.py:321
  63.0 5.3 %collective-permute-done.13 = f32[128,256]{1,0:T(8,128)S(1)} collective-permute-done((f32[128,256]{1,0:T(8,128)S(1)}, f32[128,256]{1,0:T(8,128)S(1)}, u32[]{:S(2)}, u32[]{:S(2)}) %collective-permute-start.13) | collective-permute-done | bytes 131104 | tf_op jit(solution)/shard_map/ppermute | solution.py:240
  68.4 0.7 broadcast_select_fusion.6
  69.7 0.7 maximum_select_fusion.2.inv1
  72.4 1.4 %fusion = f32[2,2,256,256]{3,2,0,1:T(8,128)S(1)} fusion(f32[2,1,256,256]{2,3,0,1:T(8,128)S(1)} %copy-done.3, f32[2,1,256,256]{2,3,0,1:T(8,128)S(1)} %get-tuple-element.25, f32[2,2,256,256]{3,2,0,1:T(8,128)S(1)} %copy.15, f32[2,1,256,256]{3,2,0,1:T(8,128)} %copy.14, f32[2,1,256,256]{3,2,0,1:T(8,128)} %bitcast.51, pred[]{:T(512)S(6)} %eq.21, pred[]{:T(512)S(6)} %lt.49), kind=kLoop, calls=%fused_computation.3 | loop fusion | flops 1048576 | bytes 4194306 | tf_op jit(solution)/shard_map/jit(_where)/select_n | solution.py:325
  73.8 1.1 %copy.17.wg = f32[2,2,256,256]{3,2,1,0:T(8,128)} copy(f32[2,2,256,256]{3,2,0,1:T(8,128)S(1)} %fusion) | data formatting | bytes 2097152 | tf_op jit(solution)/shard_map/jit(_where)/select_n | solution.py:325
  74.9 1.8 %broadcast_select_fusion.7 = (f32[256,256]{1,0:T(8,128)}, f32[256,256]{1,0:T(8,128)}) fusion(f32[256,256]{1,0:T(8,128)S(1)} %collective-permute-done.9, f32[256,256]{1,0:T(8,128)} %broadcast_select_fusion.6, pred[]{:T(512)S(6)} %eq.21), kind=kLoop, calls=%fused_computation.28 | loop fusion | flops 131072 | bytes 1048577 | tf_op jit(solution)/shard_map/jit(_where)/select_n | solution.py:328
  76.7 5.8 %shard_map.29 = (f32[256,256]{1,0:T(8,128)}, f32[256,256]{1,0:T(8,128)}, f32[2,256,256]{2,1,0:T(8,128)}, f32[2,256,256]{2,1,0:T(8,128)}) custom-call(s32[1]{0:T(128)} %bitcast.row, f32[2,256,256]{2,1,0:T(8,128)} %copy-done, f32[2,256,256]{2,1,0:T(8,128)} %bitcast.53, f32[2,2,256,256]{3,2,1,0:T(8,128)} %copy.17.wg, f32[256,256]{1,0:T(8,128)} %get-tuple-element.22.inv0, ...), custom_call_target="tpu_custom_call" | custom-call | tf_op jit(solution)/shard_map/pallas_call | solution.py:189
  82.5 4.7 %shard_map.31 = f32[2,256,256]{2,1,0:T(8,128)} custom-call(s32[3]{0:T(128)} %pad_add_fusion.ids, f32[256,256]{1,0:T(8,128)} %get-tuple-element.13.p0, f32[256,256]{1,0:T(8,128)} %get-tuple-element.14.t1r, f32[2,256,256]{2,1,0:T(8,128)} %get-tuple-element.15.t1g, f32[2,256,256]{2,1,0:T(8,128)} %get-tuple-element.16.acc, f32[256,256]{1,0:T(8,128)} %maximum_select_fusion.2.inv1), custom_call_target="tpu_custom_call" | custom-call | tf_op jit(solution)/shard_map/pallas_call | solution.py:207
  87.2 2.4 %copy.18 = f32[1,1,256,2,1,256]{5,4,3,2,1,0:T(1,128)} copy(f32[1,1,256,2,1,256]{5,2,3,4,1,0:T(8,128)} %bitcast.52) | data formatting | bytes 1048576 | tf_op jit(solution)/shard_map/reshape | solution.py:340
  (61 shorter events, 10.9 us)
Async XLA Ops:
  0.0 4.2 %copy-start.1 = (f32[1,1,256,4,1,256]{5,4,3,2,1,0:T(1,128)S(1)}, f32[1,1,256,4,1,256]{5,4,3,2,1,0:T(1,128)}, u32[]{:S(2)}) copy-start(f32[1,1,256,4,1,256]{5,4,3,2,1,0:T(1,128)} %param.2) | copy-start | bytes 3145732
  1.6 9.4 %collective-permute-start = (f32[256,256]{1,0:T(8,128)S(1)}, f32[256,256]{1,0:T(8,128)S(1)}, u32[]{:S(2)}, u32[]{:S(2)}) collective-permute-start(f32[256,256]{1,0:T(8,128)S(1)} %get-tuple-element.20), channel_id=1, source_target_pairs={{0,2},{2,0},{1,3},{3,1},{4,6},{6,4},{5,7},{7,5},{8,10},{10,8},{9,1... | collective-permute-start | bytes 786440 | tf_op jit(solution)/shard_map/ppermute | solution.py:274
  2.1 5.8 %collective-permute-start.3 = (f32[256,256]{1,0:T(8,128)S(1)}, f32[256,256]{1,0:T(8,128)S(1)}, u32[]{:S(2)}, u32[]{:S(2)}) collective-permute-start(f32[256,256]{1,0:T(8,128)S(1)} %get-tuple-element.20), channel_id=1, source_target_pairs={{25,9},{27,11},{29,13},{31,15}} | collective-permute-start | bytes 786440 | tf_op jit(solution)/shard_map/ppermute | solution.py:266
  2.8 5.2 %collective-permute-start.2 = (f32[256,256]{1,0:T(8,128)S(1)}, f32[256,256]{1,0:T(8,128)S(1)}, u32[]{:S(2)}, u32[]{:S(2)}) collective-permute-start(f32[256,256]{1,0:T(8,128)S(1)} %get-tuple-element.20), channel_id=1, source_target_pairs={{8,24},{10,26},{12,28},{14,30},{17,9},{19,11},{21,13},{23,15}} | collective-permute-start | bytes 786440 | tf_op jit(solution)/shard_map/ppermute | solution.py:266
  3.5 4.5 %collective-permute-start.1 = (f32[256,256]{1,0:T(8,128)S(1)}, f32[256,256]{1,0:T(8,128)S(1)}, u32[]{:S(2)}, u32[]{:S(2)}) collective-permute-start(f32[256,256]{1,0:T(8,128)S(1)} %get-tuple-element.20), channel_id=1, source_target_pairs={{8,16},{10,18},{12,20},{14,22},{17,25},{19,27},{21,29},{23,31},{25... | collective-permute-start | bytes 786440 | tf_op jit(solution)/shard_map/ppermute | solution.py:266
  8.0 0.7 copy-start.7
  8.0 0.8 copy-start.8
  8.0 0.8 copy-start.9
  11.0 0.9 copy-start
  11.9 1.3 %copy-start.5 = (f32[256,256]{1,0:T(8,128)}, f32[256,256]{1,0:T(8,128)S(1)}, u32[]{:S(2)}) copy-start(f32[256,256]{1,0:T(8,128)S(1)} %get-tuple-element.23.w01) | copy-start | bytes 786436
  11.9 21.8 %collective-permute-start.10 = (f32[256,256]{1,0:T(8,128)S(1)}, f32[256,256]{1,0:T(8,128)S(1)}, u32[]{:S(2)}, u32[]{:S(2)}) collective-permute-start(f32[256,256]{1,0:T(8,128)S(1)} %get-tuple-element.23.w01), channel_id=1, source_target_pairs={{4,0},{6,2},{5,1},{7,3}} | collective-permute-start | bytes 786440 | tf_op jit(solution)/shard_map/ppermute | solution.py:266
  25.5 22.8 %collective-permute-start.6 = (f32[256,256]{1,0:T(8,128)S(1)}, f32[256,256]{1,0:T(8,128)}, u32[]{:S(2)}, u32[]{:S(2)}) collective-permute-start(f32[256,256]{1,0:T(8,128)S(1)} %broadcast_select_fusion.9), channel_id=1, source_target_pairs={{0,16},{1,17},{2,18},{3,19}} | collective-permute-start | bytes 786440 | tf_op jit(solution)/shard_map/ppermute | solution.py:240
  33.6 19.7 %collective-permute-start.4 = (f32[2,256,256]{1,2,0:T(8,128)S(1)}, f32[2,256,256]{1,2,0:T(8,128)S(1)}, u32[]{:S(2)}, u32[]{:S(2)}) collective-permute-start(f32[2,256,256]{1,2,0:T(8,128)S(1)} %bitcast_select_fusion.2), channel_id=1, source_target_pairs={{0,4},{2,6},{1,5},{3,7},{4,0},{6,2},{5,1},{7,3},{8,12},{10,14},{9,... | collective-permute-start | bytes 1572872 | tf_op jit(solution)/shard_map/ppermute | solution.py:266
  33.7 0.7 copy-start.6
  46.8 4.5 %copy-start.2 = (f32[256,256]{1,0:T(8,128)S(1)}, f32[256,256]{1,0:T(8,128)}, u32[]{:S(2)}) copy-start(f32[256,256]{1,0:T(8,128)} %shard_map.30) | copy-start | bytes 786436
  46.8 4.5 %collective-permute-start.11 = (f32[128,256]{1,0:T(8,128)S(1)}, f32[128,256]{1,0:T(8,128)S(1)}, u32[]{:S(2)}, u32[]{:S(2)}) collective-permute-start(f32[128,256]{1,0:T(8,128)S(1)} %slice_select_fusion), channel_id=1, source_target_pairs={{0,16},{1,17},{2,18},{3,19}} | collective-permute-start | bytes 393224 | tf_op jit(solution)/shard_map/ppermute | solution.py:240
  49.0 8.3 %collective-permute-start.7 = (f32[256,256]{1,0:T(8,128)}, f32[256,256]{1,0:T(8,128)}, u32[]{:S(2)}, u32[]{:S(2)}) collective-permute-start(f32[256,256]{1,0:T(8,128)} %broadcast_select_fusion.4), channel_id=1, source_target_pairs={{0,8},{16,24},{1,9},{17,25},{2,10},{18,26},{3,11},{19,27}} | collective-permute-start | bytes 786440 | tf_op jit(solution)/shard_map/ppermute | solution.py:240
  51.3 8.3 %collective-permute-start.12 = (f32[128,256]{1,0:T(8,128)S(1)}, f32[128,256]{1,0:T(8,128)}, u32[]{:S(2)}, u32[]{:S(2)}) collective-permute-start(f32[128,256]{1,0:T(8,128)S(1)} %broadcast_select_fusion.10), channel_id=1, source_target_pairs={{0,8},{16,24},{1,9},{17,25},{2,10},{18,26},{3,11},{19,27}} | collective-permute-start | bytes 393224 | tf_op jit(solution)/shard_map/ppermute | solution.py:240
  58.3 10.1 %collective-permute-start.8 = (f32[256,256]{1,0:T(8,128)S(1)}, f32[256,256]{1,0:T(8,128)S(1)}, u32[]{:S(2)}, u32[]{:S(2)}) collective-permute-start(f32[256,256]{1,0:T(8,128)S(1)} %broadcast_select_fusion.5), channel_id=1, source_target_pairs={{0,4},{8,12},{16,20},{24,28},{1,5},{9,13},{17,21},{25,29},{2,6},{1... | collective-permute-start | bytes 786440 | tf_op jit(solution)/shard_map/ppermute | solution.py:240
  59.6 8.7 %collective-permute-start.13 = (f32[128,256]{1,0:T(8,128)S(1)}, f32[128,256]{1,0:T(8,128)S(1)}, u32[]{:S(2)}, u32[]{:S(2)}) collective-permute-start(f32[128,256]{1,0:T(8,128)S(1)} %broadcast_select_fusion.11), channel_id=1, source_target_pairs={{0,4},{8,12},{16,20},{24,28},{1,5},{9,13},{17,21},{25,29},{2,6},{1... | collective-permute-start | bytes 393224 | tf_op jit(solution)/shard_map/ppermute | solution.py:240
  62.0 8.4 %collective-permute-start.5 = (f32[2,256,256]{2,1,0:T(8,128)}, f32[2,256,256]{2,1,0:T(8,128)S(1)}, u32[]{:S(2)}, u32[]{:S(2)}) collective-permute-start(f32[2,256,256]{2,1,0:T(8,128)} %broadcast_select_fusion.2), channel_id=1, source_target_pairs={{0,2},{2,0},{1,3},{3,1},{4,6},{6,4},{5,7},{7,5},{8,10},{10,8},{9,1... | collective-permute-start | bytes 1572872 | tf_op jit(solution)/shard_map/ppermute | solution.py:320
  68.3 1.4 %collective-permute-start.14 = (f32[128,256]{1,0:T(8,128)S(1)}, f32[128,256]{1,0:T(8,128)S(1)}, u32[]{:S(2)}, u32[]{:S(2)}) collective-permute-start(f32[128,256]{1,0:T(8,128)S(1)} %broadcast_select_fusion.12), channel_id=1, source_target_pairs={{0,2},{2,0},{1,3},{3,1},{4,6},{6,4},{5,7},{7,5},{8,10},{10,8},{9,1... | collective-permute-start | bytes 393224 | tf_op jit(solution)/shard_map/ppermute | solution.py:333
  69.1 5.7 %collective-permute-start.9 = (f32[256,256]{1,0:T(8,128)}, f32[256,256]{1,0:T(8,128)S(1)}, u32[]{:S(2)}, u32[]{:S(2)}) collective-permute-start(f32[256,256]{1,0:T(8,128)} %broadcast_select_fusion.6), channel_id=1, source_target_pairs={{0,2},{2,0},{1,3},{3,1},{4,6},{6,4},{5,7},{7,5},{8,10},{10,8},{9,1... | collective-permute-start | bytes 786440 | tf_op jit(solution)/shard_map/ppermute | solution.py:311
  70.5 0.8 copy-start.4
  71.4 1.0 %copy-start.3 = (f32[2,1,256,256]{2,3,0,1:T(8,128)S(1)}, f32[2,1,256,256]{2,3,0,1:T(8,128)}, u32[]{:S(2)}) copy-start(f32[2,1,256,256]{2,3,0,1:T(8,128)} %get-tuple-element.26) | copy-start | bytes 1572868

commit v2 on v0

v2 whole, which is shorter than its diff:
```python
import functools

import jax
import jax.numpy as jnp
from jax import lax
from jax.experimental import pallas as pl
from jax.experimental.pallas import tpu as pltpu
from jax.sharding import PartitionSpec as P

HIGH = lax.Precision.HIGHEST
F32 = jnp.float32
AXES = ("row", "col", "layer")
VMEM = pl.BlockSpec(memory_space=pltpu.VMEM)
SMEM = pl.BlockSpec(memory_space=pltpu.SMEM)
ANY = pl.BlockSpec(memory_space=pl.ANY)
LANES = 128
SUB = 8


def contract(left, right, ldim, rdim):
    return lax.dot_general(
        left,
        right,
        (((ldim,), (rdim,)), ((), ())),
        precision=HIGH,
        preferred_element_type=F32,
    )


def nn(a, b):
    return contract(a, b, 1, 0)


def nt(a, b):
    return contract(a, b, 1, 1)


def tn(a, b):
    return contract(a, b, 0, 0)


def row_of(tile, k):
    return jnp.broadcast_to(tile[k : k + 1, :], tile.shape)


def small_inverse(block):
    size = block.shape[0]
    tiles = size // SUB
    width = 2 * size
    rows = lax.broadcasted_iota(jnp.int32, (size, size), 0)
    cols = lax.broadcasted_iota(jnp.int32, (size, size), 1)
    eye = jnp.where(rows == cols, 1.0, 0.0).astype(F32)
    full = jnp.concatenate([block, eye], axis=1)
    v = [full[SUB * t : SUB * (t + 1)] for t in range(tiles)]
    sub = lax.broadcasted_iota(jnp.int32, (SUB, width), 0)
    for s in range(tiles):
        c = {
            (j, t): jnp.broadcast_to(v[t][:, SUB * s + j : SUB * s + j + 1], (SUB, width))
            for j in range(SUB)
            for t in range(s, tiles)
        }
        pivots = jnp.ones((SUB, width), F32)
        for k in range(0, SUB, 2):
            p = row_of(c[k, s], k)
            q = row_of(c[k, s], k + 1)
            w = row_of(c[k + 1, s], k + 1)
            det = p * w - q * q
            over_det = 1.0 / det
            over_p = 1.0 / p
            v0, v1 = row_of(v[s], k), row_of(v[s], k + 1)
            c0 = {j: row_of(c[j, s], k) for j in range(k + 2, SUB)}
            c1 = {j: row_of(c[j, s], k + 1) for j in range(k + 2, SUB)}
            pivots = jnp.where(sub == k, p, jnp.where(sub == k + 1, det * over_p, pivots))
            for t in range(s, tiles):
                m0 = (w * c[k, t] - q * c[k + 1, t]) * over_det
                m1 = (p * c[k + 1, t] - q * c[k, t]) * over_det
                if t == s:
                    m0 = jnp.where(sub > k + 1, m0, jnp.where(sub == k + 1, q * over_p, 0.0))
                    m1 = jnp.where(sub > k + 1, m1, 0.0)
                v[t] = v[t] - m0 * v0 - m1 * v1
                for j in range(k + 2, SUB):
                    c[j, t] = c[j, t] - m0 * c0[j] - m1 * c1[j]
        v[s] = v[s] * lax.rsqrt(pivots)
    return jnp.concatenate(v, axis=0)[:, size:]


def inverse_factor(a, x):
    n = a.shape[0]
    base = min(n, LANES // 2)
    x[...] = jnp.zeros((n, n), F32)
    for lo in range(0, n, base):
        hi = lo + base
        inv = small_inverse(a[lo:hi, lo:hi])
        if lo:
            x[lo:hi, :lo] = nn(inv, x[lo:hi, :lo])
        x[lo:hi, lo:hi] = inv
        if hi < n:
            upper = nn(inv, a[lo:hi, hi:])
            a[hi:, hi:] = a[hi:, hi:] - tn(upper, upper)
            x[hi:, :hi] = x[hi:, :hi] - tn(upper, x[lo:hi, :hi])


def split(x):
    high = x.astype(jnp.bfloat16)
    return high, (x - high.astype(F32)).astype(jnp.bfloat16)


def three(left, right, ldim, rdim):
    def part(a, b):
        return lax.dot_general(
            a, b, (((ldim,), (rdim,)), ((), ())), preferred_element_type=F32
        )

    return part(left[0], right[0]) + (part(left[0], right[1]) + part(left[1], right[0]))


def lower_part(x):
    rows = lax.broadcasted_iota(jnp.int32, x.shape, 0)
    cols = lax.broadcasted_iota(jnp.int32, x.shape, 1)
    return jnp.where(rows >= cols, x, 0.0)


def place():
    return lax.axis_index("row"), lax.axis_index("col"), lax.axis_index("layer")


def is_owner():
    row, col, _ = place()
    return (row == 0) & (col == 0)


def move(source, target, sem):
    copy = pltpu.make_async_copy(source, target, sem)
    copy.start()
    copy.wait()


def first_kernel(matrix, inv, a, x, sem):
    @pl.when(is_owner())
    def _():
        move(matrix.at[0, 0, :, 0, 0, :], a, sem.at[0])
        inverse_factor(a, x)
        move(x, inv, sem.at[0])


def second_kernel(inv0, w01, w11, inv1, a, x, b, sem):
    @pl.when(is_owner())
    def _():
        one = pltpu.make_async_copy(inv0, x, sem.at[0])
        two = pltpu.make_async_copy(w01, b, sem.at[1])
        three_ = pltpu.make_async_copy(w11, a, sem.at[2])
        one.start()
        two.start()
        three_.start()
        one.wait()
        two.wait()
        three_.wait()
        q = nn(x[...], b[...])
        a[...] = a[...] - tn(q, q)
        inverse_factor(a, x)
        move(x, inv1, sem.at[0])


def factor_cost(n):
    return pl.CostEstimate(flops=40 * n**3, transcendentals=0, bytes_accessed=64 * n * n * 4)


def call_first(matrix, n):
    return pl.pallas_call(
        first_kernel,
        out_shape=jax.ShapeDtypeStruct((n, n), F32),
        in_specs=[ANY],
        out_specs=ANY,
        scratch_shapes=[pltpu.VMEM((n, n), F32)] * 2 + [pltpu.SemaphoreType.DMA((1,))],
        cost_estimate=factor_cost(n),
        name="first",
    )(matrix)


def call_second(inv0, w01, w11):
    n = w11.shape[0]
    return pl.pallas_call(
        second_kernel,
        out_shape=jax.ShapeDtypeStruct((n, n), F32),
        in_specs=[ANY] * 3,
        out_specs=ANY,
        scratch_shapes=[pltpu.VMEM((n, n), F32)] * 3 + [pltpu.SemaphoreType.DMA((3,))],
        cost_estimate=factor_cost(n),
        name="second",
    )(inv0, w01, w11)


def early_kernel(dims, table, matrix, *refs):
    count, owned, near, levels = dims
    own, sib = refs[:count], refs[count : 2 * count]
    inv_own, inv_sib = refs[2 * count : 2 * count + 2]
    p0, t1r, t1g, acc = refs[2 * count + 2 : 2 * count + 6]
    inv, w01, wr, wg, tiles, sem, sems = refs[2 * count + 6 :]
    row, col, layer = place()
    level, odd = row // 2, row % 2

    def fetch(slot, from_own, target, s):
        for i in range(count):

            @pl.when((slot == i) & from_own)
            def _():
                pltpu.make_async_copy(own[i], target, s).start()

            @pl.when((slot == i) & jnp.logical_not(from_own))
            def _():
                pltpu.make_async_copy(sib[i], target, s).start()

    def wait(target, s):
        pltpu.make_async_copy(own[0], target, s).wait()

    @pl.when(col == 0)
    def _():
        pltpu.make_async_copy(inv_own, inv, sem.at[0]).start()

    @pl.when(col != 0)
    def _():
        pltpu.make_async_copy(inv_sib, inv, sem.at[0]).start()

    line = (layer * levels + level) * (2 * near + 1)
    fetch(table[line + 2 * near], col != odd, w01, sem.at[1])
    pltpu.make_async_copy(own[0], wr.at[col], sem.at[2]).start()
    pltpu.make_async_copy(sib[0], wr.at[1 - col], sem.at[3]).start()

    def start(k, _):
        pltpu.make_async_copy(
            matrix.at[0, 0, :, layer * owned + k, 0, :], tiles.at[k], sems.at[0, k]
        ).start()
        slot = jnp.where((odd == col) & (row > 1), table[line + k], table[line + near + k])

        @pl.when(row > 0)
        def _():
            for i in range(count):

                @pl.when(slot == i)
                def _():
                    at = jnp.where(row == 1, 0, col)
                    pltpu.make_async_copy(own[i], wg.at[k, at], sems.at[1, k]).start()
                    pltpu.make_async_copy(sib[i], wg.at[k, 1 - at], sems.at[2, k]).start()

        return 0

    lax.fori_loop(0, owned, start, 0)
    wait(inv, sem.at[0])
    wait(w01, sem.at[1])
    wait(wr.at[0], sem.at[2])
    wait(wr.at[1], sem.at[3])

    def end(k, _):
        wait(tiles.at[k], sems.at[0, k])

        @pl.when(row > 0)
        def _():
            wait(wg.at[k, 0], sems.at[1, k])
            wait(wg.at[k, 1], sems.at[2, k])

        return 0

    lax.fori_loop(0, owned, end, 0)
    inverse = split(inv[...])
    cross = split(w01[...])

    @pl.when(odd == 0)
    def _():
        w01[...] = three(inverse, cross, 1, 0).T

    @pl.when(odd != 0)
    def _():
        w01[...] = three(cross, inverse, 1, 1)

    p01 = split(w01[...])
    solved = three(split(wr[0]), inverse, 1, 1)
    p0[...] = jnp.where(row == 0, lower_part(solved), solved)
    mine = split(p0[...])
    t1r[...] = wr[1] - three(mine, p01, 1, 1)

    def body(k, _):
        @pl.when(row > 1)
        def _():
            g = three(split(wg[k, 0]), inverse, 1, 1)
            parts = split(g)
            t1g[k] = wg[k, 1] - three(parts, p01, 1, 1)
            acc[k] = tiles[k] - three(mine, parts, 1, 1)

        @pl.when(row == 1)
        def _():
            g = split(three(inverse, split(wg[k, 0]), 1, 0))
            t1g[k] = (tiles[k] - three(p01, g, 1, 0)).T
            acc[k] = tiles[k] - three(mine, g, 1, 0)

        @pl.when(row == 0)
        def _():
            g = split(three(inverse, split(tiles[k]), 1, 0))
            t1g[k] = jnp.zeros_like(tiles[k])
            acc[k] = tiles[k] - three(mine, g, 1, 0)

        return 0

    lax.fori_loop(0, owned, body, 0, unroll=2)


def late_kernel(owned, col_total, p0, t1r, t1g, acc, inv_own, inv_sib, out, inv, p1, res, sem, sems):
    row, col, layer = place()

    @pl.when(col == 0)
    def _():
        pltpu.make_async_copy(inv_own, inv, sem.at[0]).start()

    @pl.when(col != 0)
    def _():
        pltpu.make_async_copy(inv_sib, inv, sem.at[0]).start()

    pltpu.make_async_copy(inv_own, inv, sem.at[0]).wait()
    inverse = split(inv[...])
    solved = three(split(t1r[...]), inverse, 1, 1)
    solved = jnp.where(row == 1, lower_part(solved), solved)
    p1[...] = jnp.where(row == 0, 0.0, solved)
    mine = split(p1[...])

    def out_copy(k):
        return pltpu.make_async_copy(
            res.at[k], out.at[0, 0, :, k, 0, :], sems.at[k]
        )

    def body(k, _):
        block = (layer * owned + k) * col_total + col

        @pl.when(block == 0)
        def _():
            res[k] = p0[...]

        @pl.when(block == 1)
        def _():
            res[k] = p1[...]

        @pl.when(block > 1)
        def _():
            g = three(split(t1g[k]), inverse, 1, 1)
            res[k] = acc[k] - three(mine, split(g), 1, 1)

        out_copy(k).start()
        return 0

    lax.fori_loop(0, owned, body, 0, unroll=2)

    def end(k, _):
        out_copy(k).wait()
        return 0

    lax.fori_loop(0, owned, end, 0)


def call_early(dims, table, matrix, own, sib, inv_own, inv_sib):
    owned = dims[1]
    n = matrix.shape[2]
    block = jax.ShapeDtypeStruct((n, n), F32)
    stack = jax.ShapeDtypeStruct((owned, n, n), F32)
    dma = pltpu.SemaphoreType.DMA
    return pl.pallas_call(
        functools.partial(early_kernel, dims),
        out_shape=(block, block, stack, stack),
        in_specs=[SMEM] + [ANY] * (2 * len(own) + 3),
        out_specs=(VMEM,) * 4,
        scratch_shapes=[
            pltpu.VMEM((n, n), F32),
            pltpu.VMEM((n, n), F32),
            pltpu.VMEM((2, n, n), F32),
            pltpu.VMEM((owned, 2, n, n), F32),
            pltpu.VMEM((owned, n, n), F32),
            dma((4,)),
            dma((3, owned)),
        ],
        cost_estimate=pl.CostEstimate(flops=60 * n**3, transcendentals=0, bytes_accessed=32 * n * n * 4),
        name="early",
    )(table, matrix, *own, *sib, inv_own, inv_sib)


def call_late(col_total, p0, t1r, t1g, acc, inv_own, inv_sib):
    owned, n, _ = acc.shape
    dma = pltpu.SemaphoreType.DMA
    return pl.pallas_call(
        functools.partial(late_kernel, owned, col_total),
        out_shape=jax.ShapeDtypeStruct((1, 1, n, owned, 1, n), F32),
        in_specs=[VMEM] * 4 + [ANY] * 2,
        out_specs=ANY,
        scratch_shapes=[
            pltpu.VMEM((n, n), F32),
            pltpu.VMEM((n, n), F32),
            pltpu.VMEM((owned, n, n), F32),
            dma((1,)),
            dma((owned,)),
        ],
        cost_estimate=pl.CostEstimate(flops=30 * n**3, transcendentals=0, bytes_accessed=16 * n * n * 4),
        name="late",
    )(p0, t1r, t1g, acc, inv_own, inv_sib)


def put(rounds, pairs):
    for i, taken in enumerate(rounds):
        if all(s != a and t != b for s, t in pairs for a, b in taken):
            taken.extend(pairs)
            return i
    rounds.append(list(pairs))
    return len(rounds) - 1


def gather_plan(levels, near, layer_total, col_total):
    cores = range(col_total)
    rounds = [[((1, 1, l), (0, 0, l)) for l in range(layer_total)]]
    arrived = {}
    for l in range(layer_total):
        for gap in range(1, levels):
            for h in range(max(1, l * near), (l + 1) * near):
                for t in (h + gap, h - gap):
                    if 1 <= t < levels:
                        pairs = [
                            ((2 * h + y, c, l), (2 * t + y, c, l)) for y in range(2) for c in cores
                        ]
                        arrived[l, t, h] = put(rounds, pairs)
    for t in range(levels - 1, 0, -1):
        for l in range(layer_total):
            pairs = [((y, 1 - y, l), (2 * t + y, 1 - y, l)) for y in range(2)]
            arrived[l, t, "cross"] = put(rounds, pairs)
    return rounds, arrived


def pair_plan(levels, near, layer_total, count, arrived):
    plan = {}
    for l in range(layer_total):
        for t in range(levels):
            line = []
            for h in range(l * near, (l + 1) * near):
                if t == h and h > 0:
                    line.append((0, 0, h))
                elif (l, t, h) in arrived:
                    line.append((1, 1 + arrived[l, t, h], h))
            line.sort()
            step = {}
            for order, slot, h in line:
                j = max(0, slot - 1 - (count - near)) if order else 0
                while j in step:
                    j += 1
                step[j % near if j >= near else j] = (slot, h)
            plan[l, t] = step
    return plan


def on_device(matrix):
    row_total = lax.axis_size("row")
    col_total = lax.axis_size("col")
    layer_total = lax.axis_size("layer")
    row, col, layer = place()
    n = matrix.shape[2]
    col_blocks = matrix.shape[3]
    owned = col_blocks // layer_total
    levels = row_total // 2
    near = levels // layer_total
    swap = [(0, 1), (1, 0)]
    level = row // 2

    def device(r, c, l):
        return (r * col_total + c) * layer_total + l

    def permute(x, pairs):
        return lax.ppermute(x, AXES, [(device(*s), device(*t)) for s, t in pairs])

    def permute_rows(x, pairs, cores):
        return permute(
            x,
            [((a, c, l), (b, c, l)) for a, b in pairs for c in cores for l in range(layer_total)],
        )

    def sibling(x):
        return lax.ppermute(x, "col", swap)

    rounds, arrived = gather_plan(levels, near, layer_total, col_total)
    plan = pair_plan(levels, near, layer_total, len(rounds), arrived)

    mine = matrix[0, 0, :, 0, 0, :]
    inv0 = call_first(matrix, n)
    other = sibling(mine)
    got = [permute(mine, pairs) for pairs in rounds]
    inv1 = call_second(inv0, other, got[0])

    first = [0]
    hop = permute_rows(inv0, [(0, 1)], first)
    flat = [permute_rows(hop, [(1, 2 * t + 1)], first) for t in range(levels - 1, 0, -1)]
    odd_rows = sum(flat[1:], flat[0])
    back = permute_rows(odd_rows, [(2 * t + 1, 2 * t) for t in range(1, levels)], first)
    inv0_own = jnp.where(row == 0, inv0, jnp.where(row == 1, hop, jnp.where(row % 2 == 1, odd_rows, back)))
    inv0_sib = sibling(inv0_own)

    flat = [permute_rows(inv1, [(0, 2 * t)], first) for t in range(levels - 1, 0, -1)]
    hop = permute_rows(inv1, [(0, 1)], first)
    even_rows = sum(flat[1:], flat[0])
    back = permute_rows(even_rows, [(2 * t, 2 * t + 1) for t in range(1, levels)], first)
    inv1_own = jnp.where(row == 0, inv1, jnp.where(row == 1, hop, jnp.where(row % 2 == 1, back, even_rows)))
    inv1_sib = sibling(inv1_own)

    own = [mine] + got
    for j in range(near):
        send = lax.dynamic_index_in_dim(matrix, layer * owned + j, 3, keepdims=False)[0, 0, :, 0, :]
        pairs = [((0, c, l), (1, c, l)) for c in range(col_total) for l in range(layer_total)]
        users = {}
        for (l, t), step in plan.items():
            if j in step:
                users.setdefault(step[j][0], []).append((l, t))
                for c in range(col_total):
                    pairs += [((2 * t + y, c, l), (2 * t + 1 - y, c, l)) for y in range(2)]
        for slot, who in users.items():
            chosen = functools.reduce(
                jnp.logical_or, [(layer == l) & (level == t) for l, t in who]
            )
            send = jnp.where(chosen, own[slot], send)
        own.append(permute(send, pairs))
    sib = [other] + [sibling(x) for x in own[1:]]

    table = []
    for l in range(layer_total):
        for t in range(levels):
            slots = {h: (slot, 1 + len(rounds) + j) for j, (slot, h) in plan[l, t].items()}
            near_rows = range(l * near, (l + 1) * near)
            table += [slots.get(h, (0, 0))[0] for h in near_rows]
            if t:
                table += [slots.get(h, (0, 0))[1] for h in near_rows]
            else:
                table += [1 + len(rounds) + j for j in range(near)]
            table.append(1 + arrived[l, t, "cross"] if t else 0)
    dims = (len(own), owned, near, levels)
    p0, t1r, t1g, acc = call_early(
        dims, jnp.array(table, jnp.int32), matrix, own, sib, inv0_own, inv0_sib
    )
    return call_late(col_total, p0, t1r, t1g, acc, inv1_own, inv1_sib)


def solution(mesh):
    in_specs = (P(None, "row", None, None, "col", None),)
    out_specs = P(None, "row", None, "layer", "col", None)
    return jax.shard_map(
        on_device, mesh=mesh, in_specs=in_specs, out_specs=out_specs, check_vma=False
    )
```

time: 481 us -> 70.2 us (0.15)
  the two profiles are of different devices: /device:TPU:0 before, /device:TPU:7 now
where the time goes in v2:
time: 70.2 us; the launch traced here: 69.7 us
  starting transfers between devices  49.1 us (70%)
  Pallas kernels  10.8 us (15%)
  local copies, waits for them, and re-layouts  4.97 us (7%)
  other arithmetic  3.04 us (4%)
  waiting for transfers between devices  1.15 us (2%)
    ppermute x15, starting transfers between devices, permute(): return lax.ppermute(x, AXES, [(device(*s), device(*t)) for s, t in pairs])  26.3 us
    ppermute x8, starting transfers between devices, sibling(): return lax.ppermute(x, 'col', swap)  22.8 us
    pallas_call x1, Pallas kernels, call_early(): pl.pallas_call(functools.partial(early_kernel, dims), out_shape=(block, b...  6 us
    pallas_call x1, Pallas kernels, call_late(): pl.pallas_call(functools.partial(late_kernel, owned, col_total), out_shap...  4.8 us
    unnamed x43, local copies, waits for them, and re-layouts  4.43 us
    select_n x1, other arithmetic, on_device(): send = jnp.where(chosen, own[slot], send)  1.78 us
  transfers between devices with their start and end apart: 23, of which 1 were waited for; matrix products, arithmetic and copies ran while one was open for 5% of the time, Pallas kernels for 9%

profile of v2, /device:TPU:7, one launch (start us, length us, event | category | flops | bytes accessed | tf_op | source)
XLA Modules:
  0.0 69.7 jit_solution(11092578943973287883)
XLA Ops:
  0.0 0.8 %collective-permute-start.11 = (f32[256,256]{1,0:T(8,128)}, f32[256,256]{1,0:T(8,128)S(1)}, u32[]{:S(2)}, u32[]{:S(2)}) collective-permute-start(f32[256,256]{1,0:T(8,128)} %first.1.inv0), channel_id=1, source_target_pairs={{0,4},{1,5}} | collective-permute-start | bytes 786440 | tf_op jit(solution)/shard_map/ppermute | solution.py:469
  0.8 0.4 copy-done
  1.2 0.5 constant_dynamic-slice_fusion
  1.8 13.8 %collective-permute-start = (f32[256,256]{1,0:T(8,128)S(1)}, f32[256,256]{1,0:T(8,128)S(1)}, u32[]{:S(2)}, u32[]{:S(2)}) collective-permute-start(f32[256,256]{1,0:T(8,128)S(1)} %bitcast.15), channel_id=1, source_target_pairs={{6,0},{7,1},{8,16},{10,18},{12,20},{14,22},{17,25},{19,27},{21,29}... | collective-permute-start | bytes 786440 | tf_op jit(solution)/shard_map/ppermute | solution.py:469
  15.7 0.7 collective-permute-start.1
  16.4 0.7 collective-permute-start.2
  17.1 0.7 collective-permute-start.14
  17.8 1.1 %collective-permute-done.refs_1_.w11 = f32[256,256]{1,0:T(8,128)S(1)} collective-permute-done((f32[256,256]{1,0:T(8,128)S(1)}, f32[256,256]{1,0:T(8,128)S(1)}, u32[]{:S(2)}, u32[]{:S(2)}) %collective-permute-start) | collective-permute-done | bytes 262176 | tf_op jit(solution)/shard_map/ppermute | solution.py:469
  18.9 0.7 %copy-done.4 = f32[256,256]{1,0:T(8,128)} copy-done((f32[256,256]{1,0:T(8,128)}, f32[256,256]{1,0:T(8,128)S(1)}, u32[]{:S(2)}) %copy-start.4) | copy-done | bytes 262168
  19.6 0.7 %copy-done.8 = f32[256,256]{1,0:T(8,128)} copy-done((f32[256,256]{1,0:T(8,128)}, f32[256,256]{1,0:T(8,128)S(1)}, u32[]{:S(2)}) %copy-start.8) | copy-done | bytes 262168
  20.4 0.7 collective-permute-start.20
  21.1 0.7 collective-permute-start.18
  21.8 0.7 collective-permute-start.19
  22.5 0.7 collective-permute-start.12
  23.2 0.7 collective-permute-start.13
  23.8 1.8 %fusion = (f32[256,256]{1,0:T(8,128)}, f32[256,256]{1,0:T(8,128)S(1)}) fusion(f32[256,256]{1,0:T(8,128)} %copy-done.4, f32[256,256]{1,0:T(8,128)S(1)} %collective-permute-done.2.refs_3_, f32[1,1,256,1,1,256]{5,4,3,2,1,0:T(1,128)S(1)} %get-tuple-element.13, pred[]{:T(512)S(6)} %and.36, pred[]{:T(512)S(6)} %or.15, ...), kind=kLoop, calls=%fused_computation.2 | loop fusion | flops 327680 | bytes 2097157 | tf_op jit(solution)/shard_map/jit(_where)/select_n | solution.py:518
  25.6 1.4 %collective-permute-start.3 = (f32[256,256]{1,0:T(8,128)S(1)}, f32[256,256]{1,0:T(8,128)S(1)}, u32[]{:S(2)}, u32[]{:S(2)}) collective-permute-start(f32[256,256]{1,0:T(8,128)S(1)} %get-tuple-element.17), channel_id=1, source_target_pairs={{0,4},{1,5},{2,6},{3,7},{8,12},{12,8},{10,14},{14,10},{16,20},{20,... | collective-permute-start | bytes 786440 | tf_op jit(solution)/shard_map/ppermute | solution.py:469
  27.1 1.4 %collective-permute-start.15 = (f32[256,256]{1,0:T(8,128)S(1)}, f32[256,256]{1,0:T(8,128)}, u32[]{:S(2)}, u32[]{:S(2)}) collective-permute-start(f32[256,256]{1,0:T(8,128)S(1)} %add_add_fusion.1), channel_id=1, source_target_pairs={{12,8},{13,9},{20,16},{21,17},{28,24},{29,25}} | collective-permute-start | bytes 786440 | tf_op jit(solution)/shard_map/ppermute | solution.py:469
  28.5 0.7 collective-permute-start.17
  29.2 1.4 %collective-permute-start.4 = (f32[256,256]{1,0:T(8,128)}, f32[256,256]{1,0:T(8,128)S(1)}, u32[]{:S(2)}, u32[]{:S(2)}) collective-permute-start(f32[256,256]{1,0:T(8,128)} %get-tuple-element.16), channel_id=1, source_target_pairs={{0,4},{1,5},{2,6},{3,7},{9,13},{13,9},{11,15},{15,11},{17,21},{21,... | collective-permute-start | bytes 786440 | tf_op jit(solution)/shard_map/ppermute | solution.py:469
  30.7 8.5 %collective-permute-start.6 = (f32[256,256]{1,0:T(8,128)S(1)}, f32[256,256]{1,0:T(8,128)S(1)}, u32[]{:S(2)}, u32[]{:S(2)}) collective-permute-start(f32[256,256]{1,0:T(8,128)S(1)} %copy-done.5), channel_id=1, source_target_pairs={{0,2},{2,0},{1,3},{3,1},{4,6},{6,4},{5,7},{7,5},{8,10},{10,8},{9,1... | collective-permute-start | bytes 786440 | tf_op jit(solution)/shard_map/ppermute | solution.py:478
  39.3 1.4 %collective-permute-start.21 = (f32[256,256]{1,0:T(8,128)S(1)}, f32[256,256]{1,0:T(8,128)}, u32[]{:S(2)}, u32[]{:S(2)}) collective-permute-start(f32[256,256]{1,0:T(8,128)S(1)} %add_add_fusion), channel_id=1, source_target_pairs={{8,12},{9,13},{16,20},{17,21},{24,28},{25,29}} | collective-permute-start | bytes 786440 | tf_op jit(solution)/shard_map/ppermute | solution.py:469
  40.7 8.9 %collective-permute-start.7 = (f32[256,256]{1,0:T(8,128)S(1)}, f32[256,256]{1,0:T(8,128)S(1)}, u32[]{:S(2)}, u32[]{:S(2)}) collective-permute-start(f32[256,256]{1,0:T(8,128)S(1)} %collective-permute-done.1.refs_2_), channel_id=1, source_target_pairs={{0,2},{2,0},{1,3},{3,1},{4,6},{6,4},{5,7},{7,5},{8,10},{10,8},{9,1... | collective-permute-start | bytes 786440 | tf_op jit(solution)/shard_map/ppermute | solution.py:478
  49.7 4.1 %collective-permute-start.8 = (f32[256,256]{1,0:T(8,128)S(1)}, f32[256,256]{1,0:T(8,128)S(1)}, u32[]{:S(2)}, u32[]{:S(2)}) collective-permute-start(f32[256,256]{1,0:T(8,128)S(1)} %collective-permute-done.2.refs_3_), channel_id=1, source_target_pairs={{0,2},{2,0},{1,3},{3,1},{4,6},{6,4},{5,7},{7,5},{8,10},{10,8},{9,1... | collective-permute-start | bytes 786440 | tf_op jit(solution)/shard_map/ppermute | solution.py:478
  53.9 0.5 collective-permute-start.10
  54.6 0.5 collective-permute-start.16
  55.1 1.1 %select_select_fusion.inv_own = f32[256,256]{1,0:T(8,128)S(1)} fusion(f32[256,256]{1,0:T(8,128)S(1)} %copy-done.19, f32[256,256]{1,0:T(8,128)} %copy-done.20, f32[256,256]{1,0:T(8,128)} %collective-permute-done.21, f32[256,256]{1,0:T(8,128)S(1)} %add_add_fusion, pred[]{:T(512)S(6)} %eq.50, pred[]{:T(512)S(6)} %eq.25, pred[]{:T(512)S(6)} %eq.24), kind=kLoop, calls=%fused_computation.6 | loop fusion | flops 196608 | bytes 1310723 | tf_op jit(solution)/shard_map/jit(_where)/select_n | solution.py:501
  56.4 0.6 copy-done.12
  57.3 0.7 %copy-done.16 = f32[256,256]{1,0:T(8,128)} copy-done((f32[256,256]{1,0:T(8,128)}, f32[256,256]{1,0:T(8,128)S(1)}, u32[]{:S(2)}) %copy-start.16) | copy-done | bytes 262168
  58.0 6.0 %early.1 = (f32[256,256]{1,0:T(8,128)}, f32[256,256]{1,0:T(8,128)}, f32[2,256,256]{2,1,0:T(8,128)}, f32[2,256,256]{2,1,0:T(8,128)}) custom-call(s32[40]{0:T(128)} %constant.51.clone.table, f32[1,1,256,4,1,256]{5,4,3,2,1,0:T(1,128)} %matrix.3, f32[256,256]{1,0:T(8,128)} %bitcast.19, f32[256,256]{1,0:T(8,128)} %copy-done.4, f32[256,256]{1,0:T(8,128)} %copy-done.6, ...), custom_call_target="tpu_custom_call" | custom-call | flops 1006632960 | bytes 8388608 | tf_op jit(solution)/shard_map/early/pallas_call | solution.py:363
  64.1 0.7 copy-done.17
  64.7 4.8 %late.1 = f32[1,1,256,2,1,256]{5,4,3,2,1,0:T(1,128)} custom-call(f32[256,256]{1,0:T(8,128)} %get-tuple-element.9.p0, f32[256,256]{1,0:T(8,128)} %get-tuple-element.10.t1r, f32[2,256,256]{2,1,0:T(8,128)} %get-tuple-element.11.t1g, f32[2,256,256]{2,1,0:T(8,128)} %get-tuple-element.12.acc, f32[256,256]{1,0:T(8,128)} %copy-done.3, f32[256,256]{1,0:T(8,128)} %copy-done.17), custom_call_target="tpu_custom_call" | custom-call | flops 503316480 | bytes 4194304 | tf_op jit(solution)/shard_map/late/pallas_call | solution.py:385
  (67 shorter events, 1.2 us)
Async XLA Ops:
  0.0 17.0 %collective-permute-start.11 = (f32[256,256]{1,0:T(8,128)}, f32[256,256]{1,0:T(8,128)S(1)}, u32[]{:S(2)}, u32[]{:S(2)}) collective-permute-start(f32[256,256]{1,0:T(8,128)} %first.1.inv0), channel_id=1, source_target_pairs={{0,4},{1,5}} | collective-permute-start | bytes 786440 | tf_op jit(solution)/shard_map/ppermute | solution.py:469
  1.8 18.6 %copy-start.1 = (f32[1,1,256,1,1,256]{5,2,4,3,1,0:T(8,128)}, f32[1,1,256,1,1,256]{5,2,4,3,1,0:T(8,128)S(1)}, u32[]{:S(2)}) copy-start(f32[1,1,256,1,1,256]{5,2,4,3,1,0:T(8,128)S(1)} %copy.12) | copy-start | bytes 786436
  1.8 17.1 %collective-permute-start = (f32[256,256]{1,0:T(8,128)S(1)}, f32[256,256]{1,0:T(8,128)S(1)}, u32[]{:S(2)}, u32[]{:S(2)}) collective-permute-start(f32[256,256]{1,0:T(8,128)S(1)} %bitcast.15), channel_id=1, source_target_pairs={{6,0},{7,1},{8,16},{10,18},{12,20},{14,22},{17,25},{19,27},{21,29}... | collective-permute-start | bytes 786440 | tf_op jit(solution)/shard_map/ppermute | solution.py:469
  15.6 3.3 %collective-permute-start.5 = (f32[256,256]{1,0:T(8,128)S(1)}, f32[256,256]{1,0:T(8,128)S(1)}, u32[]{:S(2)}, u32[]{:S(2)}) collective-permute-start(f32[256,256]{1,0:T(8,128)S(1)} %bitcast.16), channel_id=1, source_target_pairs={{0,2},{2,0},{1,3},{3,1},{4,6},{6,4},{5,7},{7,5},{8,10},{10,8},{9,1... | collective-permute-start | bytes 786440 | tf_op jit(solution)/shard_map/ppermute | solution.py:478
  15.7 6.1 %collective-permute-start.1 = (f32[256,256]{1,0:T(8,128)S(1)}, f32[256,256]{1,0:T(8,128)S(1)}, u32[]{:S(2)}, u32[]{:S(2)}) collective-permute-start(f32[256,256]{1,0:T(8,128)S(1)} %bitcast.17), channel_id=1, source_target_pairs={{8,24},{10,26},{12,28},{14,30},{17,9},{19,11},{21,13},{23,15},{3,2... | collective-permute-start | bytes 786440 | tf_op jit(solution)/shard_map/ppermute | solution.py:469
  16.4 6.1 %collective-permute-start.2 = (f32[256,256]{1,0:T(8,128)S(1)}, f32[256,256]{1,0:T(8,128)S(1)}, u32[]{:S(2)}, u32[]{:S(2)}) collective-permute-start(f32[256,256]{1,0:T(8,128)S(1)} %bitcast.18), channel_id=1, source_target_pairs={{25,9},{27,11},{29,13},{31,15},{3,19},{5,21},{2,10},{4,12}} | collective-permute-start | bytes 786440 | tf_op jit(solution)/shard_map/ppermute | solution.py:469
  17.1 6.1 %collective-permute-start.14 = (f32[256,256]{1,0:T(8,128)S(1)}, f32[256,256]{1,0:T(8,128)S(1)}, u32[]{:S(2)}, u32[]{:S(2)}) collective-permute-start(f32[256,256]{1,0:T(8,128)S(1)} %collective-permute-done.11), channel_id=1, source_target_pairs={{4,12},{5,13}} | collective-permute-start | bytes 786440 | tf_op jit(solution)/shard_map/ppermute | solution.py:469
  20.4 8.2 %collective-permute-start.20 = (f32[256,256]{1,0:T(8,128)}, f32[256,256]{1,0:T(8,128)S(1)}, u32[]{:S(2)}, u32[]{:S(2)}) collective-permute-start(f32[256,256]{1,0:T(8,128)} %second.1), channel_id=1, source_target_pairs={{0,8},{1,9}} | collective-permute-start | bytes 786440 | tf_op jit(solution)/shard_map/ppermute | solution.py:469
  21.1 8.1 %collective-permute-start.18 = (f32[256,256]{1,0:T(8,128)}, f32[256,256]{1,0:T(8,128)S(1)}, u32[]{:S(2)}, u32[]{:S(2)}) collective-permute-start(f32[256,256]{1,0:T(8,128)} %second.1), channel_id=1, source_target_pairs={{0,24},{1,25}} | collective-permute-start | bytes 786440 | tf_op jit(solution)/shard_map/ppermute | solution.py:469
  21.7 18.9 %copy-start.6 = (f32[256,256]{1,0:T(8,128)}, f32[256,256]{1,0:T(8,128)S(1)}, u32[]{:S(2)}) copy-start(f32[256,256]{1,0:T(8,128)S(1)} %collective-permute-done.1.refs_2_) | copy-start | bytes 786436
  21.8 8.9 %collective-permute-start.19 = (f32[256,256]{1,0:T(8,128)}, f32[256,256]{1,0:T(8,128)S(1)}, u32[]{:S(2)}, u32[]{:S(2)}) collective-permute-start(f32[256,256]{1,0:T(8,128)} %second.1), channel_id=1, source_target_pairs={{0,16},{1,17}} | collective-permute-start | bytes 786440 | tf_op jit(solution)/shard_map/ppermute | solution.py:469
  22.5 27.2 %copy-start.7 = (f32[256,256]{1,0:T(8,128)}, f32[256,256]{1,0:T(8,128)S(1)}, u32[]{:S(2)}) copy-start(f32[256,256]{1,0:T(8,128)S(1)} %collective-permute-done.2.refs_3_) | copy-start | bytes 786436
  22.5 3.2 %collective-permute-start.12 = (f32[256,256]{1,0:T(8,128)S(1)}, f32[256,256]{1,0:T(8,128)S(1)}, u32[]{:S(2)}, u32[]{:S(2)}) collective-permute-start(f32[256,256]{1,0:T(8,128)S(1)} %collective-permute-done.11), channel_id=1, source_target_pairs={{4,28},{5,29}} | collective-permute-start | bytes 786440 | tf_op jit(solution)/shard_map/ppermute | solution.py:469
  23.2 3.9 %collective-permute-start.13 = (f32[256,256]{1,0:T(8,128)S(1)}, f32[256,256]{1,0:T(8,128)S(1)}, u32[]{:S(2)}, u32[]{:S(2)}) collective-permute-start(f32[256,256]{1,0:T(8,128)S(1)} %collective-permute-done.11), channel_id=1, source_target_pairs={{4,20},{5,21}} | collective-permute-start | bytes 786440 | tf_op jit(solution)/shard_map/ppermute | solution.py:469
  25.6 5.0 %copy-start.5 = (f32[256,256]{1,0:T(8,128)S(1)}, f32[256,256]{1,0:T(8,128)}, u32[]{:S(2)}) copy-start(f32[256,256]{1,0:T(8,128)} %copy-done.4) | copy-start | bytes 786436
  25.6 13.6 %collective-permute-start.3 = (f32[256,256]{1,0:T(8,128)S(1)}, f32[256,256]{1,0:T(8,128)S(1)}, u32[]{:S(2)}, u32[]{:S(2)}) collective-permute-start(f32[256,256]{1,0:T(8,128)S(1)} %get-tuple-element.17), channel_id=1, source_target_pairs={{0,4},{1,5},{2,6},{3,7},{8,12},{12,8},{10,14},{14,10},{16,20},{20,... | collective-permute-start | bytes 786440 | tf_op jit(solution)/shard_map/ppermute | solution.py:469
  27.1 13.5 %collective-permute-start.15 = (f32[256,256]{1,0:T(8,128)S(1)}, f32[256,256]{1,0:T(8,128)}, u32[]{:S(2)}, u32[]{:S(2)}) collective-permute-start(f32[256,256]{1,0:T(8,128)S(1)} %add_add_fusion.1), channel_id=1, source_target_pairs={{12,8},{13,9},{20,16},{21,17},{28,24},{29,25}} | collective-permute-start | bytes 786440 | tf_op jit(solution)/shard_map/ppermute | solution.py:469
  28.5 25.4 %collective-permute-start.17 = (f32[256,256]{1,0:T(8,128)S(1)}, f32[256,256]{1,0:T(8,128)S(1)}, u32[]{:S(2)}, u32[]{:S(2)}) collective-permute-start(f32[256,256]{1,0:T(8,128)S(1)} %copy-done.19), channel_id=1, source_target_pairs={{0,4},{1,5}} | collective-permute-start | bytes 786440 | tf_op jit(solution)/shard_map/ppermute | solution.py:469
  29.2 20.4 %copy-start.18 = (f32[256,256]{1,0:T(8,128)S(1)}, f32[256,256]{1,0:T(8,128)}, u32[]{:S(2)}) copy-start(f32[256,256]{1,0:T(8,128)} %first.1.inv0) | copy-start | bytes 786436
  29.2 20.4 %collective-permute-start.4 = (f32[256,256]{1,0:T(8,128)}, f32[256,256]{1,0:T(8,128)S(1)}, u32[]{:S(2)}, u32[]{:S(2)}) collective-permute-start(f32[256,256]{1,0:T(8,128)} %get-tuple-element.16), channel_id=1, source_target_pairs={{0,4},{1,5},{2,6},{3,7},{9,13},{13,9},{11,15},{15,11},{17,21},{21,... | collective-permute-start | bytes 786440 | tf_op jit(solution)/shard_map/ppermute | solution.py:469
  30.7 23.1 %collective-permute-start.6 = (f32[256,256]{1,0:T(8,128)S(1)}, f32[256,256]{1,0:T(8,128)S(1)}, u32[]{:S(2)}, u32[]{:S(2)}) collective-permute-start(f32[256,256]{1,0:T(8,128)S(1)} %copy-done.5), channel_id=1, source_target_pairs={{0,2},{2,0},{1,3},{3,1},{4,6},{6,4},{5,7},{7,5},{8,10},{10,8},{9,1... | collective-permute-start | bytes 786440 | tf_op jit(solution)/shard_map/ppermute | solution.py:478
  39.2 14.6 %copy-start.9 = (f32[256,256]{1,0:T(8,128)}, f32[256,256]{1,0:T(8,128)S(1)}, u32[]{:S(2)}) copy-start(f32[256,256]{1,0:T(8,128)S(1)} %collective-permute-done.3.refs_4_) | copy-start | bytes 786436
  39.3 15.4 %collective-permute-start.21 = (f32[256,256]{1,0:T(8,128)S(1)}, f32[256,256]{1,0:T(8,128)}, u32[]{:S(2)}, u32[]{:S(2)}) collective-permute-start(f32[256,256]{1,0:T(8,128)S(1)} %add_add_fusion), channel_id=1, source_target_pairs={{8,12},{9,13},{16,20},{17,21},{24,28},{25,29}} | collective-permute-start | bytes 786440 | tf_op jit(solution)/shard_map/ppermute | solution.py:469
  40.7 15.6 %collective-permute-start.7 = (f32[256,256]{1,0:T(8,128)S(1)}, f32[256,256]{1,0:T(8,128)S(1)}, u32[]{:S(2)}, u32[]{:S(2)}) collective-permute-start(f32[256,256]{1,0:T(8,128)S(1)} %collective-permute-done.1.refs_2_), channel_id=1, source_target_pairs={{0,2},{2,0},{1,3},{3,1},{4,6},{6,4},{5,7},{7,5},{8,10},{10,8},{9,1... | collective-permute-start | bytes 786440 | tf_op jit(solution)/shard_map/ppermute | solution.py:478
  49.6 6.6 %copy-start.2 = (f32[256,256]{1,0:T(8,128)}, f32[256,256]{1,0:T(8,128)S(1)}, u32[]{:S(2)}) copy-start(f32[256,256]{1,0:T(8,128)S(1)} %select_select_fusion.1.refs_12_) | copy-start | bytes 786436
  49.7 6.5 %copy-start.10 = (f32[256,256]{1,0:T(8,128)}, f32[256,256]{1,0:T(8,128)S(1)}, u32[]{:S(2)}) copy-start(f32[256,256]{1,0:T(8,128)S(1)} %collective-permute-done.4.refs_5_) | copy-start | bytes 786436
  49.7 6.7 %collective-permute-start.8 = (f32[256,256]{1,0:T(8,128)S(1)}, f32[256,256]{1,0:T(8,128)S(1)}, u32[]{:S(2)}, u32[]{:S(2)}) collective-permute-start(f32[256,256]{1,0:T(8,128)S(1)} %collective-permute-done.2.refs_3_), channel_id=1, source_target_pairs={{0,2},{2,0},{1,3},{3,1},{4,6},{6,4},{5,7},{7,5},{8,10},{10,8},{9,1... | collective-permute-start | bytes 786440 | tf_op jit(solution)/shard_map/ppermute | solution.py:478
  53.8 2.6 %collective-permute-start.9 = (f32[256,256]{1,0:T(8,128)S(1)}, f32[256,256]{1,0:T(8,128)S(1)}, u32[]{:S(2)}, u32[]{:S(2)}) collective-permute-start(f32[256,256]{1,0:T(8,128)S(1)} %collective-permute-done.3.refs_4_), channel_id=1, source_target_pairs={{0,2},{2,0},{1,3},{3,1},{4,6},{6,4},{5,7},{7,5},{8,10},{10,8},{9,1... | collective-permute-start | bytes 786440 | tf_op jit(solution)/shard_map/ppermute | solution.py:478
  53.9 2.5 %collective-permute-start.10 = (f32[256,256]{1,0:T(8,128)S(1)}, f32[256,256]{1,0:T(8,128)S(1)}, u32[]{:S(2)}, u32[]{:S(2)}) collective-permute-start(f32[256,256]{1,0:T(8,128)S(1)} %collective-permute-done.4.refs_5_), channel_id=1, source_target_pairs={{0,2},{2,0},{1,3},{3,1},{4,6},{6,4},{5,7},{7,5},{8,10},{10,8},{9,1... | collective-permute-start | bytes 786440 | tf_op jit(solution)/shard_map/ppermute | solution.py:478
  54.6 1.8 %collective-permute-start.16 = (f32[256,256]{1,0:T(8,128)S(1)}, f32[256,256]{1,0:T(8,128)S(1)}, u32[]{:S(2)}, u32[]{:S(2)}) collective-permute-start(f32[256,256]{1,0:T(8,128)S(1)} %select_select_fusion.1.refs_12_), channel_id=1, source_target_pairs={{0,2},{2,0},{1,3},{3,1},{4,6},{6,4},{5,7},{7,5},{8,10},{10,8},{9,1... | collective-permute-start | bytes 786440 | tf_op jit(solution)/shard_map/ppermute | solution.py:478
  56.2 7.8 %copy-start.3 = (f32[256,256]{1,0:T(8,128)}, f32[256,256]{1,0:T(8,128)S(1)}, u32[]{:S(2)}) copy-start(f32[256,256]{1,0:T(8,128)S(1)} %select_select_fusion.inv_own) | copy-start | bytes 786436
  56.3 7.8 %collective-permute-start.22 = (f32[256,256]{1,0:T(8,128)S(1)}, f32[256,256]{1,0:T(8,128)S(1)}, u32[]{:S(2)}, u32[]{:S(2)}) collective-permute-start(f32[256,256]{1,0:T(8,128)S(1)} %select_select_fusion.inv_own), channel_id=1, source_target_pairs={{0,2},{2,0},{1,3},{3,1},{4,6},{6,4},{5,7},{7,5},{8,10},{10,8},{9,1... | collective-permute-start | bytes 786440 | tf_op jit(solution)/shard_map/ppermute | solution.py:478
  (12 other events, 13.5 us)

commit v3 on v2

v3 whole, which is shorter than its diff:
```python
import functools

import jax
import jax.numpy as jnp
from jax import lax
from jax.experimental import pallas as pl
from jax.experimental.pallas import tpu as pltpu
from jax.sharding import PartitionSpec as P


HIGH = lax.Precision.HIGHEST
F32 = jnp.float32
AXES = ("row", "col", "layer")
VMEM = pl.BlockSpec(memory_space=pltpu.VMEM)
SMEM = pl.BlockSpec(memory_space=pltpu.SMEM)
ANY = pl.BlockSpec(memory_space=pl.ANY)
HBM = pl.BlockSpec(memory_space=pltpu.HBM)
LANES = 128
SUB = 8


def contract(left, right, ldim, rdim):
    return lax.dot_general(
        left,
        right,
        (((ldim,), (rdim,)), ((), ())),
        precision=HIGH,
        preferred_element_type=F32,
    )


def nn(a, b):
    return contract(a, b, 1, 0)


def tn(a, b):
    return contract(a, b, 0, 0)


def row_of(tile, k):
    return jnp.broadcast_to(tile[k : k + 1, :], tile.shape)


def small_inverse(block):
    size = block.shape[0]
    tiles = size // SUB
    width = 2 * size
    rows = lax.broadcasted_iota(jnp.int32, (size, size), 0)
    cols = lax.broadcasted_iota(jnp.int32, (size, size), 1)
    eye = jnp.where(rows == cols, 1.0, 0.0).astype(F32)
    full = jnp.concatenate([block, eye], axis=1)
    v = [full[SUB * t : SUB * (t + 1)] for t in range(tiles)]
    sub = lax.broadcasted_iota(jnp.int32, (SUB, width), 0)
    for s in range(tiles):
        c = {
            (j, t): jnp.broadcast_to(v[t][:, SUB * s + j : SUB * s + j + 1], (SUB, width))
            for j in range(SUB)
            for t in range(s, tiles)
        }
        pivots = jnp.ones((SUB, width), F32)
        for k in range(0, SUB, 2):
            p = row_of(c[k, s], k)
            q = row_of(c[k, s], k + 1)
            w = row_of(c[k + 1, s], k + 1)
            det = p * w - q * q
            over_det = 1.0 / det
            over_p = 1.0 / p
            v0, v1 = row_of(v[s], k), row_of(v[s], k + 1)
            c0 = {j: row_of(c[j, s], k) for j in range(k + 2, SUB)}
            c1 = {j: row_of(c[j, s], k + 1) for j in range(k + 2, SUB)}
            pivots = jnp.where(sub == k, p, jnp.where(sub == k + 1, det * over_p, pivots))
            for t in range(s, tiles):
                m0 = (w * c[k, t] - q * c[k + 1, t]) * over_det
                m1 = (p * c[k + 1, t] - q * c[k, t]) * over_det
                if t == s:
                    m0 = jnp.where(sub > k + 1, m0, jnp.where(sub == k + 1, q * over_p, 0.0))
                    m1 = jnp.where(sub > k + 1, m1, 0.0)
                v[t] = v[t] - m0 * v0 - m1 * v1
                for j in range(k + 2, SUB):
                    c[j, t] = c[j, t] - m0 * c0[j] - m1 * c1[j]
        v[s] = v[s] * lax.rsqrt(pivots)
    return jnp.concatenate(v, axis=0)[:, size:]


def inverse_factor(a, x):
    n = a.shape[0]
    base = min(n, LANES // 2)
    x[...] = jnp.zeros((n, n), F32)
    for lo in range(0, n, base):
        hi = lo + base
        inv = small_inverse(a[lo:hi, lo:hi])
        if lo:
            x[lo:hi, :lo] = nn(inv, x[lo:hi, :lo])
        x[lo:hi, lo:hi] = inv
        if hi < n:
            upper = nn(inv, a[lo:hi, hi:])
            a[hi:, hi:] = a[hi:, hi:] - tn(upper, upper)
            x[hi:, :hi] = x[hi:, :hi] - tn(upper, x[lo:hi, :hi])


def split(x):
    high = x.astype(jnp.bfloat16)
    return high, (x - high.astype(F32)).astype(jnp.bfloat16)


def three(left, right, ldim, rdim):
    def part(a, b):
        return lax.dot_general(
            a, b, (((ldim,), (rdim,)), ((), ())), preferred_element_type=F32
        )

    return part(left[0], right[0]) + (part(left[0], right[1]) + part(left[1], right[0]))


def lower_part(x):
    rows = lax.broadcasted_iota(jnp.int32, x.shape, 0)
    cols = lax.broadcasted_iota(jnp.int32, x.shape, 1)
    return jnp.where(rows >= cols, x, 0.0)


def place():
    return lax.axis_index("row"), lax.axis_index("col"), lax.axis_index("layer")


def is_owner():
    row, col, _ = place()
    return (row == 0) & (col == 0)


def first_kernel(w00, inv, a):
    @pl.when(is_owner())
    def _():
        a[...] = w00[...]
        inverse_factor(a, inv)

    @pl.when(jnp.logical_not(is_owner()))
    def _():
        inv[...] = jnp.zeros_like(inv)


def second_kernel(inv0, w01, w11, matrix, inv1, tiles, a, sems):
    row, _, layer = place()
    owned = tiles.shape[0]

    def tile_copy(k):
        return pltpu.make_async_copy(
            matrix.at[0, 0, :, layer * owned + k, 0, :], tiles.at[k], sems.at[k]
        )

    @pl.when(row == 0)
    def _():
        for k in range(owned):
            tile_copy(k).start()

    @pl.when(is_owner())
    def _():
        q = nn(inv0[...], w01[...])
        a[...] = w11[...] - tn(q, q)
        inverse_factor(a, inv1)

    @pl.when(jnp.logical_not(is_owner()))
    def _():
        inv1[...] = jnp.zeros_like(inv1)

    @pl.when(row == 0)
    def _():
        for k in range(owned):
            tile_copy(k).wait()


def lookup(slots):
    row, _, layer = place()
    value = jnp.int32(0)
    for (l, t), slot in slots.items():
        value = jnp.where((layer == l) & (row // 2 == t), slot, value)
    return value


def pick_kernel(slots, *refs):
    *sources, out = refs
    slot = lookup(slots)
    for i, source in enumerate(sources):

        @pl.when(slot == i)
        def _():
            out[...] = source[...]


def grant(n, blocks):
    return pltpu.CompilerParams(vmem_limit_bytes=(blocks + 12) * n * n * 4)


def factor_cost(n):
    return pl.CostEstimate(flops=40 * n**3, transcendentals=0, bytes_accessed=64 * n * n * 4)


def call_first(w00):
    n = w00.shape[0]
    return pl.pallas_call(
        first_kernel,
        out_shape=jax.ShapeDtypeStruct((n, n), F32),
        in_specs=[VMEM],
        out_specs=VMEM,
        scratch_shapes=[pltpu.VMEM((n, n), F32)],
        cost_estimate=factor_cost(n),
        compiler_params=grant(n, 3),
        name="first",
    )(w00)


def call_second(inv0, w01, w11, matrix, owned):
    n = w11.shape[0]
    return pl.pallas_call(
        second_kernel,
        out_shape=(
            jax.ShapeDtypeStruct((n, n), F32),
            jax.ShapeDtypeStruct((owned, n, n), F32),
        ),
        in_specs=[VMEM] * 3 + [HBM],
        out_specs=(VMEM, VMEM),
        scratch_shapes=[pltpu.VMEM((n, n), F32), pltpu.SemaphoreType.DMA((owned,))],
        cost_estimate=factor_cost(n),
        compiler_params=grant(n, 5 + owned),
        name="second",
    )(inv0, w01, w11, matrix)


def call_pick(slots, sources):
    n = sources[0].shape[0]
    return pl.pallas_call(
        functools.partial(pick_kernel, slots),
        out_shape=jax.ShapeDtypeStruct((n, n), F32),
        in_specs=[VMEM] * len(sources),
        out_specs=VMEM,
        compiler_params=grant(n, 1 + len(sources)),
        name="pick",
    )(*sources)


def early_kernel(dims, table, matrix, above, *refs):
    count, owned, near, levels = dims
    own, sib = refs[:count], refs[count : 2 * count]
    inv_own, inv_sib = refs[2 * count : 2 * count + 2]
    p0, t1r, t1g, acc = refs[2 * count + 2 : 2 * count + 6]
    inv, w01, wr, wg, sems = refs[2 * count + 6 :]
    row, col, layer = place()
    level, odd = row // 2, row % 2

    def tile_copy(k):
        return pltpu.make_async_copy(
            matrix.at[0, 0, :, layer * owned + k, 0, :], acc.at[k], sems.at[k]
        )

    for k in range(owned):
        tile_copy(k).start()

    @pl.when(col == 1)
    def _():
        inv[...] = inv_own[...]

    @pl.when(col != 1)
    def _():
        inv[...] = inv_sib[...]

    line = (layer * levels + level) * (2 * near + 1)
    slot = table[line + 2 * near]
    for i in range(count):

        @pl.when((slot == i) & (col != odd))
        def _():
            w01[...] = own[i][...]

        @pl.when((slot == i) & (col == odd))
        def _():
            w01[...] = sib[i][...]

    wr[col] = own[0][...]
    wr[1 - col] = sib[0][...]

    def gather(k, _):
        slot = jnp.where(odd == col, table[line + k], table[line + near + k])
        for i in range(count):

            @pl.when((slot == i) & (row > 1))
            def _():
                wg[k, col] = own[i][...]
                wg[k, 1 - col] = sib[i][...]

        return 0

    lax.fori_loop(0, owned, gather, 0)
    inverse = split(inv[...])
    cross = split(w01[...])

    @pl.when(odd == 0)
    def _():
        w01[...] = three(inverse, cross, 1, 0).T

    @pl.when(odd != 0)
    def _():
        w01[...] = three(cross, inverse, 1, 1)

    p01 = split(w01[...])
    solved = three(split(wr[0]), inverse, 1, 1)
    p0[...] = jnp.where(row == 0, lower_part(solved), solved)
    mine = split(p0[...])
    t1r[...] = wr[1] - three(mine, p01, 1, 1)
    for k in range(owned):
        tile_copy(k).wait()

    def body(k, _):
        @pl.when(row > 1)
        def _():
            g = three(split(wg[k, 0]), inverse, 1, 1)
            parts = split(g)
            t1g[k] = wg[k, 1] - three(parts, p01, 1, 1)
            acc[k] = acc[k] - three(mine, parts, 1, 1)

        @pl.when(row == 1)
        def _():
            g = split(three(inverse, split(above[k]), 1, 0))
            t1g[k] = (acc[k] - three(p01, g, 1, 0)).T
            acc[k] = acc[k] - three(mine, g, 1, 0)

        @pl.when(row == 0)
        def _():
            g = split(three(inverse, split(acc[k]), 1, 0))
            t1g[k] = jnp.zeros_like(acc[k])
            acc[k] = acc[k] - three(mine, g, 1, 0)

        return 0

    lax.fori_loop(0, owned, body, 0, unroll=2)


def late_kernel(owned, col_total, p0, t1r, t1g, acc, inv_own, inv_sib, out, inv, p1, res, sems):
    row, col, layer = place()

    @pl.when(col == 0)
    def _():
        inv[...] = inv_own[...]

    @pl.when(col != 0)
    def _():
        inv[...] = inv_sib[...]

    inverse = split(inv[...])
    solved = three(split(t1r[...]), inverse, 1, 1)
    solved = jnp.where(row == 1, lower_part(solved), solved)
    p1[...] = jnp.where(row == 0, 0.0, solved)
    mine = split(p1[...])

    def out_copy(k):
        return pltpu.make_async_copy(
            res.at[k], out.at[0, 0, :, k, 0, :], sems.at[k]
        )

    def body(k, _):
        block = (layer * owned + k) * col_total + col

        @pl.when(block == 0)
        def _():
            res[k] = p0[...]

        @pl.when(block == 1)
        def _():
            res[k] = p1[...]

        @pl.when(block > 1)
        def _():
            g = three(split(t1g[k]), inverse, 1, 1)
            res[k] = acc[k] - three(mine, split(g), 1, 1)

        out_copy(k).start()
        return 0

    lax.fori_loop(0, owned, body, 0, unroll=2)

    def end(k, _):
        out_copy(k).wait()
        return 0

    lax.fori_loop(0, owned, end, 0)


def call_early(dims, table, matrix, above, own, sib, inv_own, inv_sib):
    owned = dims[1]
    n = matrix.shape[2]
    block = jax.ShapeDtypeStruct((n, n), F32)
    stack = jax.ShapeDtypeStruct((owned, n, n), F32)
    return pl.pallas_call(
        functools.partial(early_kernel, dims),
        out_shape=(block, block, stack, stack),
        in_specs=[SMEM, HBM] + [VMEM] * (2 * len(own) + 3),
        out_specs=(VMEM,) * 4,
        scratch_shapes=[
            pltpu.VMEM((n, n), F32),
            pltpu.VMEM((n, n), F32),
            pltpu.VMEM((2, n, n), F32),
            pltpu.VMEM((owned, 2, n, n), F32),
            pltpu.SemaphoreType.DMA((owned,)),
        ],
        cost_estimate=pl.CostEstimate(flops=60 * n**3, transcendentals=0, bytes_accessed=32 * n * n * 4),
        compiler_params=grant(n, 2 * len(own) + 8 + 6 * owned),
        name="early",
    )(table, matrix, above, *own, *sib, inv_own, inv_sib)


def call_late(col_total, p0, t1r, t1g, acc, inv_own, inv_sib):
    owned, n, _ = acc.shape
    return pl.pallas_call(
        functools.partial(late_kernel, owned, col_total),
        out_shape=jax.ShapeDtypeStruct((1, 1, n, owned, 1, n), F32),
        in_specs=[VMEM] * 6,
        out_specs=ANY,
        scratch_shapes=[
            pltpu.VMEM((n, n), F32),
            pltpu.VMEM((n, n), F32),
            pltpu.VMEM((owned, n, n), F32),
            pltpu.SemaphoreType.DMA((owned,)),
        ],
        cost_estimate=pl.CostEstimate(flops=30 * n**3, transcendentals=0, bytes_accessed=16 * n * n * 4),
        compiler_params=grant(n, 6 + 3 * owned),
        name="late",
    )(p0, t1r, t1g, acc, inv_own, inv_sib)


def put(rounds, pairs, start):
    for i, taken in enumerate(rounds):
        if i >= start and all(s != a and t != b for s, t in pairs for a, b in taken):
            taken.extend(pairs)
            return i
    rounds.append(list(pairs))
    return len(rounds) - 1


def gather_plan(levels, near, layer_total, col_total):
    cores = range(col_total)
    rounds = [[((1, 1, l), (0, 0, l)) for l in range(layer_total)]]
    arrived = {}
    for l in range(layer_total):
        rounds[0] += [((y, 1 - y, l), (2 + y, 1 - y, l)) for y in range(2)]
        arrived[l, 1, "cross"] = 0
    for l in range(layer_total):
        for gap in range(1, levels):
            for h in range(max(1, l * near), (l + 1) * near):
                for t in (h - gap, h + gap):
                    if 1 <= t < levels:
                        pairs = [
                            ((2 * h + y, c, l), (2 * t + y, c, l)) for y in range(2) for c in cores
                        ]
                        arrived[l, t, h] = put(rounds, pairs, 1)
    for t in range(levels - 1, 1, -1):
        for l in range(layer_total):
            pairs = [((y, 1 - y, l), (2 * t + y, 1 - y, l)) for y in range(2)]
            arrived[l, t, "cross"] = put(rounds, pairs, 1)
    return rounds, arrived


def pair_plan(levels, near, layer_total, count, arrived):
    plan = {}
    for l in range(layer_total):
        for t in range(levels):
            line = []
            for h in range(l * near, (l + 1) * near):
                if t == h and h > 0:
                    line.append((0, 0, h))
                elif (l, t, h) in arrived:
                    line.append((1, 1 + arrived[l, t, h], h))
            line.sort()
            step = {}
            for order, slot, h in line:
                j = max(0, slot - 2 - (count - 1 - near)) if order else 0
                while j in step:
                    j += 1
                step[j % near if j >= near else j] = (slot, h)
            plan[l, t] = step
    return plan


def on_device(matrix):
    row_total = lax.axis_size("row")
    col_total = lax.axis_size("col")
    layer_total = lax.axis_size("layer")
    col_blocks = matrix.shape[3]
    owned = col_blocks // layer_total
    levels = row_total // 2
    near = levels // layer_total
    swap = [(0, 1), (1, 0)]

    def device(r, c, l):
        return (r * col_total + c) * layer_total + l

    def permute(x, pairs):
        return lax.ppermute(x, AXES, [(device(*s), device(*t)) for s, t in pairs])

    def permute_rows(x, pairs, cores):
        return permute(
            x,
            [((a, c, l), (b, c, l)) for a, b in pairs for c in cores for l in range(layer_total)],
        )

    def sibling(x):
        return lax.ppermute(x, "col", swap)

    rounds, arrived = gather_plan(levels, near, layer_total, col_total)
    plan = pair_plan(levels, near, layer_total, len(rounds), arrived)
    first = [0]

    mine = matrix[0, 0, :, 0, 0, :]
    own = [mine]
    for pairs in rounds:
        own.append(permute(mine, pairs))
    other = sibling(mine)
    inv0 = call_first(mine)
    inv0_sib = permute(inv0, [((0, 0, l), (0, 1, l)) for l in range(layer_total)])
    inv1, tiles = call_second(inv0, other, own[1], matrix, owned)
    above = permute(
        tiles,
        [((0, c, l), (1, c, l)) for c in range(col_total) for l in range(layer_total)],
    )

    sent = []
    for t in range(levels - 1, 0, -1):
        sent.append(permute_rows(inv1, [(0, 2 * t)], first))
    hop = permute_rows(inv1, [(0, 1)], first)

    for j in range(near):
        slots = {key: step[j][0] for key, step in plan.items() if j in step}
        used = sorted(set(slots.values()))
        pairs = []
        for l, t in slots:
            for c in range(col_total):
                pairs += [((2 * t + y, c, l), (2 * t + 1 - y, c, l)) for y in range(2)]
        send = call_pick(
            {key: used.index(slot) for key, slot in slots.items()},
            [own[slot] for slot in used],
        )
        own.append(permute(send, pairs))

    even = inv0_sib
    gap = levels // 2
    while gap:
        pairs = [
            ((2 * t, 1, l), (2 * t + 2 * gap, 1, l))
            for t in range(0, levels, 2 * gap)
            for l in range(layer_total)
        ]
        even = even + permute(even, pairs)
        gap //= 2
    back = permute_rows(even, [(2 * t, 2 * t + 1) for t in range(levels)], [1])
    inv0_own = even + back
    inv0_sib = sibling(inv0_own)
    sib = [other]
    for x in own[1:]:
        sib.append(sibling(x))

    even = sum(sent, inv1)
    back = permute_rows(even, [(2 * t, 2 * t + 1) for t in range(1, levels)], first)
    table = []
    for l in range(layer_total):
        for t in range(levels):
            slots = {h: (slot, 1 + len(rounds) + j) for j, (slot, h) in plan[l, t].items()}
            near_rows = range(l * near, (l + 1) * near)
            table += [slots.get(h, (0, 0))[0] for h in near_rows]
            table += [slots.get(h, (0, 0))[1] for h in near_rows]
            table.append(1 + arrived[l, t, "cross"] if t else 0)
    dims = (len(own), owned, near, levels)
    p0, t1r, t1g, acc = call_early(
        dims, jnp.array(table, jnp.int32), matrix, above, own, sib, inv0_own, inv0_sib
    )
    even, hop, p0 = lax.optimization_barrier((even, hop, p0))
    inv1_own = even + hop + back
    inv1_sib = sibling(inv1_own)
    return call_late(col_total, p0, t1r, t1g, acc, inv1_own, inv1_sib)


def solution(mesh):
    in_specs = (P(None, "row", None, None, "col", None),)
    out_specs = P(None, "row", None, "layer", "col", None)
    levels = mesh.shape["row"] // 2
    _, _ = gather_plan(levels, levels // mesh.shape["layer"], mesh.shape["layer"], mesh.shape["col"])

    return jax.shard_map(
        on_device, mesh=mesh, in_specs=in_specs, out_specs=out_specs, check_vma=False
    )
```

time: 70.2 us -> 64.7 us (0.922)
  the two profiles are of different devices: /device:TPU:7 before, /device:TPU:15 now
where the time goes in v3:
time: 64.7 us; the launch traced here: 64.3 us
  starting transfers between devices  40 us (62%)
  waiting for transfers between devices  16.2 us (25%)
  Pallas kernels  6.39 us (10%)
  local copies, waits for them, and re-layouts  0.98 us (2%)
    ppermute x8, starting transfers between devices, sibling(): return lax.ppermute(x, 'col', swap)  23.9 us
    ppermute x15, starting transfers between devices, permute(): return lax.ppermute(x, AXES, [(device(*s), device(*t)) for s, t in pairs])  16.1 us
    ppermute x15, waiting for transfers between devices, permute(): return lax.ppermute(x, AXES, [(device(*s), device(*t)) for s, t in pairs])  14.1 us
    pallas_call x1, Pallas kernels, call_early(): pl.pallas_call(functools.partial(early_kernel, dims), out_shape=(block, b...  3.54 us
    pallas_call x1, Pallas kernels, call_late(): pl.pallas_call(functools.partial(late_kernel, owned, col_total), out_shap...  2.51 us
    ppermute x8, waiting for transfers between devices, sibling(): return lax.ppermute(x, 'col', swap)  2.09 us
  transfers between devices with their start and end apart: 23, of which 7 were waited for; matrix products, arithmetic and copies ran while one was open for 0% of the time, Pallas kernels for 6%

profile of v3, /device:TPU:15, one launch (start us, length us, event | category | flops | bytes accessed | tf_op | source)
XLA Modules:
  0.0 64.3 jit_solution(8083582188000799427)
XLA Ops:
  0.0 0.9 %slice-done = f32[1,1,256,1,1,256]{5,4,3,2,1,0:T(1,128)S(1)} async-done(((f32[1,1,256,4,1,256]{5,4,3,2,1,0:T(1,128)}), f32[1,1,256,1,1,256]{5,4,3,2,1,0:T(1,128)S(1)}, s32[]{:S(2)}) %slice-start) | async-done | bytes 262168 | tf_op jit(solution)/shard_map/slice | solution.py:510
  1.0 0.7 %collective-permute-start.16 = (f32[256,256]{1,0:T(8,128)S(1)}, f32[256,256]{1,0:T(8,128)S(1)}, u32[]{:S(2)}, u32[]{:S(2)}) collective-permute-start(f32[256,256]{1,0:T(8,128)S(1)} %first.1.inv0), channel_id=1, source_target_pairs={{0,2},{1,3}} | collective-permute-start | bytes 786440 | tf_op jit(solution)/shard_map/ppermute | solution.py:495
  1.7 0.7 %collective-permute-start.17 = (f32[256,256]{1,0:T(8,128)S(1)}, f32[256,256]{1,0:T(8,128)S(1)}, u32[]{:S(2)}, u32[]{:S(2)}) collective-permute-start(f32[256,256]{1,0:T(8,128)S(1)} %collective-permute-done.16), channel_id=1, source_target_pairs={{2,18},{3,19}} | collective-permute-start | bytes 786440 | tf_op jit(solution)/shard_map/ppermute | solution.py:495
  2.4 1.3 %collective-permute-start.7 = (f32[256,256]{1,0:T(8,128)S(1)}, f32[256,256]{1,0:T(8,128)S(1)}, u32[]{:S(2)}, u32[]{:S(2)}) collective-permute-start(f32[256,256]{1,0:T(8,128)S(1)} %bitcast.4), channel_id=1, source_target_pairs={{8,16},{10,18},{12,20},{14,22},{17,9},{19,11},{21,13},{23,15},{25,... | collective-permute-start | bytes 786440 | tf_op jit(solution)/shard_map/ppermute | solution.py:495
  3.7 1.3 %collective-permute-start.8 = (f32[256,256]{1,0:T(8,128)S(1)}, f32[256,256]{1,0:T(8,128)S(1)}, u32[]{:S(2)}, u32[]{:S(2)}) collective-permute-start(f32[256,256]{1,0:T(8,128)S(1)} %bitcast.5), channel_id=1, source_target_pairs={{8,24},{10,26},{12,28},{14,30},{17,25},{19,27},{21,29},{23,31},{25... | collective-permute-start | bytes 786440 | tf_op jit(solution)/shard_map/ppermute | solution.py:495
  5.0 0.7 %collective-permute-start.1 = (f32[256,256]{1,0:T(8,128)S(1)}, f32[256,256]{1,0:T(8,128)S(1)}, u32[]{:S(2)}, u32[]{:S(2)}) collective-permute-start(f32[256,256]{1,0:T(8,128)S(1)} %bitcast.6), channel_id=1, source_target_pairs={{6,0},{7,1},{2,10},{4,12},{3,11},{5,13}} | collective-permute-start | bytes 786440 | tf_op jit(solution)/shard_map/ppermute | solution.py:495
  5.7 0.8 %collective-permute-start.18 = (f32[256,256]{1,0:T(8,128)S(1)}, f32[256,256]{1,0:T(8,128)S(1)}, u32[]{:S(2)}, u32[]{:S(2)}) collective-permute-start(f32[256,256]{1,0:T(8,128)S(1)} %add.27), channel_id=1, source_target_pairs={{2,10},{3,11},{18,26},{19,27}} | collective-permute-start | bytes 786440 | tf_op jit(solution)/shard_map/ppermute | solution.py:495
  6.6 1.4 %collective-permute-start = (f32[256,256]{1,0:T(8,128)S(1)}, f32[256,256]{1,0:T(8,128)S(1)}, u32[]{:S(2)}, u32[]{:S(2)}) collective-permute-start(f32[256,256]{1,0:T(8,128)S(1)} %bitcast.7), channel_id=1, source_target_pairs={{0,2},{2,0},{1,3},{3,1},{4,6},{6,4},{5,7},{7,5},{8,10},{10,8},{9,1... | collective-permute-start | bytes 786440 | tf_op jit(solution)/shard_map/ppermute | solution.py:504
  7.9 3.6 %collective-permute-done.7.refs_1_.refs_0_.refs_2_ = f32[256,256]{1,0:T(8,128)S(1)} collective-permute-done((f32[256,256]{1,0:T(8,128)S(1)}, f32[256,256]{1,0:T(8,128)S(1)}, u32[]{:S(2)}, u32[]{:S(2)}) %collective-permute-start.7) | collective-permute-done | bytes 262176 | tf_op jit(solution)/shard_map/ppermute | solution.py:495
  11.5 6.6 %collective-permute-done.8.refs_1_.refs_3_ = f32[256,256]{1,0:T(8,128)S(1)} collective-permute-done((f32[256,256]{1,0:T(8,128)S(1)}, f32[256,256]{1,0:T(8,128)S(1)}, u32[]{:S(2)}, u32[]{:S(2)}) %collective-permute-start.8) | collective-permute-done | bytes 262176 | tf_op jit(solution)/shard_map/ppermute | solution.py:495
  18.1 3.4 %collective-permute-start.10 = (f32[256,256]{1,0:T(8,128)S(1)}, f32[256,256]{1,0:T(8,128)S(1)}, u32[]{:S(2)}, u32[]{:S(2)}) collective-permute-start(f32[256,256]{1,0:T(8,128)S(1)} %pick.3), channel_id=1, source_target_pairs={{24,28},{28,24},{26,30},{30,26},{9,13},{13,9},{11,15},{15,11},{17,... | collective-permute-start | bytes 786440 | tf_op jit(solution)/shard_map/ppermute | solution.py:495
  21.6 1.9 %collective-permute-start.9 = (f32[256,256]{1,0:T(8,128)S(1)}, f32[256,256]{1,0:T(8,128)S(1)}, u32[]{:S(2)}, u32[]{:S(2)}) collective-permute-start(f32[256,256]{1,0:T(8,128)S(1)} %pick.2), channel_id=1, source_target_pairs={{8,12},{12,8},{10,14},{14,10},{16,20},{20,16},{18,22},{22,18},{9,1... | collective-permute-start | bytes 786440 | tf_op jit(solution)/shard_map/ppermute | solution.py:495
  23.5 2.2 %collective-permute-start.12 = (f32[256,256]{1,0:T(8,128)S(1)}, f32[256,256]{1,0:T(8,128)S(1)}, u32[]{:S(2)}, u32[]{:S(2)}) collective-permute-start(f32[256,256]{1,0:T(8,128)S(1)} %collective-permute-done.7.refs_1_.refs_0_.refs_2_), channel_id=1, source_target_pairs={{0,2},{2,0},{1,3},{3,1},{4,6},{6,4},{5,7},{7,5},{8,10},{10,8},{9,1... | collective-permute-start | bytes 786440 | tf_op jit(solution)/shard_map/ppermute | solution.py:504
  25.8 1.3 %collective-permute-start.19 = (f32[256,256]{1,0:T(8,128)S(1)}, f32[256,256]{1,0:T(8,128)S(1)}, u32[]{:S(2)}, u32[]{:S(2)}) collective-permute-start(f32[256,256]{1,0:T(8,128)S(1)} %add.28), channel_id=1, source_target_pairs={{2,6},{3,7},{10,14},{11,15},{18,22},{19,23},{26,30},{27,31}} | collective-permute-start | bytes 786440 | tf_op jit(solution)/shard_map/ppermute | solution.py:495
  27.1 0.2 second.1
  27.4 0.7 %collective-permute-start.6 = (f32[2,256,256]{2,1,0:T(8,128)S(1)}, f32[2,256,256]{2,1,0:T(8,128)S(1)}, u32[]{:S(2)}, u32[]{:S(2)}) collective-permute-start(f32[2,256,256]{2,1,0:T(8,128)S(1)} %get-tuple-element.15), channel_id=1, source_target_pairs={{0,4},{1,5},{2,6},{3,7}} | collective-permute-start | bytes 1572872 | tf_op jit(solution)/shard_map/ppermute | solution.py:495
  28.1 3.9 %collective-permute-done.9.refs_4_ = f32[256,256]{1,0:T(8,128)S(1)} collective-permute-done((f32[256,256]{1,0:T(8,128)S(1)}, f32[256,256]{1,0:T(8,128)S(1)}, u32[]{:S(2)}, u32[]{:S(2)}) %collective-permute-start.9) | collective-permute-done | bytes 262176 | tf_op jit(solution)/shard_map/ppermute | solution.py:495
  32.0 3.7 %collective-permute-start.13 = (f32[256,256]{1,0:T(8,128)S(1)}, f32[256,256]{1,0:T(8,128)S(1)}, u32[]{:S(2)}, u32[]{:S(2)}) collective-permute-start(f32[256,256]{1,0:T(8,128)S(1)} %collective-permute-done.8.refs_1_.refs_3_), channel_id=1, source_target_pairs={{0,2},{2,0},{1,3},{3,1},{4,6},{6,4},{5,7},{7,5},{8,10},{10,8},{9,1... | collective-permute-start | bytes 786440 | tf_op jit(solution)/shard_map/ppermute | solution.py:504
  35.7 0.7 %collective-permute-start.2 = (f32[256,256]{1,0:T(8,128)S(1)}, f32[256,256]{1,0:T(8,128)S(1)}, u32[]{:S(2)}, u32[]{:S(2)}) collective-permute-start(f32[256,256]{1,0:T(8,128)S(1)} %get-tuple-element.14), channel_id=1, source_target_pairs={{0,24},{1,25}} | collective-permute-start | bytes 786440 | tf_op jit(solution)/shard_map/ppermute | solution.py:495
  36.3 0.7 %collective-permute-start.3 = (f32[256,256]{1,0:T(8,128)S(1)}, f32[256,256]{1,0:T(8,128)S(1)}, u32[]{:S(2)}, u32[]{:S(2)}) collective-permute-start(f32[256,256]{1,0:T(8,128)S(1)} %get-tuple-element.14), channel_id=1, source_target_pairs={{0,16},{1,17}} | collective-permute-start | bytes 786440 | tf_op jit(solution)/shard_map/ppermute | solution.py:495
  37.0 0.7 %collective-permute-start.4 = (f32[256,256]{1,0:T(8,128)S(1)}, f32[256,256]{1,0:T(8,128)S(1)}, u32[]{:S(2)}, u32[]{:S(2)}) collective-permute-start(f32[256,256]{1,0:T(8,128)S(1)} %get-tuple-element.14), channel_id=1, source_target_pairs={{0,8},{1,9}} | collective-permute-start | bytes 786440 | tf_op jit(solution)/shard_map/ppermute | solution.py:495
  37.8 0.7 %collective-permute-start.5 = (f32[256,256]{1,0:T(8,128)S(1)}, f32[256,256]{1,0:T(8,128)S(1)}, u32[]{:S(2)}, u32[]{:S(2)}) collective-permute-start(f32[256,256]{1,0:T(8,128)S(1)} %get-tuple-element.14), channel_id=1, source_target_pairs={{0,4},{1,5}} | collective-permute-start | bytes 786440 | tf_op jit(solution)/shard_map/ppermute | solution.py:495
  38.6 0.5 collective-permute-start.14
  39.1 0.1 collective-permute-start.20
  39.2 0.7 %collective-permute-start.21 = (f32[256,256]{1,0:T(8,128)S(1)}, f32[256,256]{1,0:T(8,128)S(1)}, u32[]{:S(2)}, u32[]{:S(2)}) collective-permute-start(f32[256,256]{1,0:T(8,128)S(1)} %add_add_fusion.1), channel_id=1, source_target_pairs={{8,12},{9,13},{16,20},{17,21},{24,28},{25,29}} | collective-permute-start | bytes 786440 | tf_op jit(solution)/shard_map/ppermute | solution.py:495
  39.9 0.2 collective-permute-done.15.refs_11_
  40.1 0.4 collective-permute-done.14.refs_10_
  40.5 0.4 collective-permute-done.20.refs_13_
  40.8 3.5 %early.1 = (f32[256,256]{1,0:T(8,128)S(1)}, f32[256,256]{1,0:T(8,128)S(1)}, f32[2,256,256]{2,1,0:T(8,128)S(1)}, f32[2,256,256]{2,1,0:T(8,128)S(1)}) custom-call(s32[40]{0:T(128)S(1)} %copy-done.1, f32[1,1,256,4,1,256]{5,4,3,2,1,0:T(1,128)S(1)} %copy-done, f32[2,256,256]{2,1,0:T(8,128)S(1)} %collective-permute-done.6.above, f32[256,256]{1,0:T(8,128)S(1)} %bitcast.9, ...), custom_call_target="tpu_custom_call" | custom-call | flops 1006632960 | bytes 8388608 | tf_op jit(solution)/shard_map/early/pallas_call | solution.py:391
  44.5 16.0 %collective-permute-start.22 = (f32[256,256]{1,0:T(8,128)S(1)}, f32[256,256]{1,0:T(8,128)S(1)}, u32[]{:S(2)}, u32[]{:S(2)}) collective-permute-start(f32[256,256]{1,0:T(8,128)S(1)} %add_add_fusion.inv_own), channel_id=1, source_target_pairs={{0,2},{2,0},{1,3},{3,1},{4,6},{6,4},{5,7},{7,5},{8,10},{10,8},{9,1... | collective-permute-start | bytes 786440 | tf_op jit(solution)/shard_map/ppermute | solution.py:504
  60.5 1.2 %collective-permute-done.22.inv_sib = f32[256,256]{1,0:T(8,128)S(1)} collective-permute-done((f32[256,256]{1,0:T(8,128)S(1)}, f32[256,256]{1,0:T(8,128)S(1)}, u32[]{:S(2)}, u32[]{:S(2)}) %collective-permute-start.22) | collective-permute-done | bytes 262176 | tf_op jit(solution)/shard_map/ppermute | solution.py:504
  61.6 2.5 %late.1 = f32[1,1,256,2,1,256]{5,4,3,2,1,0:T(1,128)} custom-call(f32[256,256]{1,0:T(8,128)S(1)} %get-tuple-element.17.p0, f32[256,256]{1,0:T(8,128)S(1)} %get-tuple-element.18.t1r, f32[2,256,256]{2,1,0:T(8,128)S(1)} %get-tuple-element.19.t1g, f32[2,256,256]{2,1,0:T(8,128)S(1)} %get-tuple-element.20.acc, f32[256,256]{1,0:T(8,128)S(1)} %add_add_fusion.inv_own, ...), custom_call_target="tpu_custom_call" | custom-call | flops 503316480 | bytes 4194304 | tf_op jit(solution)/shard_map/late/pallas_call | solution.py:411
  (32 shorter events, 0.6 us)
Async XLA Ops:
  0.0 0.9 %slice-start = ((f32[1,1,256,4,1,256]{5,4,3,2,1,0:T(1,128)}), f32[1,1,256,1,1,256]{5,4,3,2,1,0:T(1,128)S(1)}, s32[]{:S(2)}) async-start(f32[1,1,256,4,1,256]{5,4,3,2,1,0:T(1,128)} %matrix.3), calls=%async_computation | async-start | bytes 524288 | tf_op jit(solution)/shard_map/slice | solution.py:510
  1.0 0.7 %collective-permute-start.16 = (f32[256,256]{1,0:T(8,128)S(1)}, f32[256,256]{1,0:T(8,128)S(1)}, u32[]{:S(2)}, u32[]{:S(2)}) collective-permute-start(f32[256,256]{1,0:T(8,128)S(1)} %first.1.inv0), channel_id=1, source_target_pairs={{0,2},{1,3}} | collective-permute-start | bytes 786440 | tf_op jit(solution)/shard_map/ppermute | solution.py:495
  1.7 4.0 %collective-permute-start.17 = (f32[256,256]{1,0:T(8,128)S(1)}, f32[256,256]{1,0:T(8,128)S(1)}, u32[]{:S(2)}, u32[]{:S(2)}) collective-permute-start(f32[256,256]{1,0:T(8,128)S(1)} %collective-permute-done.16), channel_id=1, source_target_pairs={{2,18},{3,19}} | collective-permute-start | bytes 786440 | tf_op jit(solution)/shard_map/ppermute | solution.py:495
  2.4 9.1 %collective-permute-start.7 = (f32[256,256]{1,0:T(8,128)S(1)}, f32[256,256]{1,0:T(8,128)S(1)}, u32[]{:S(2)}, u32[]{:S(2)}) collective-permute-start(f32[256,256]{1,0:T(8,128)S(1)} %bitcast.4), channel_id=1, source_target_pairs={{8,16},{10,18},{12,20},{14,22},{17,9},{19,11},{21,13},{23,15},{25,... | collective-permute-start | bytes 786440 | tf_op jit(solution)/shard_map/ppermute | solution.py:495
  3.7 14.4 %collective-permute-start.8 = (f32[256,256]{1,0:T(8,128)S(1)}, f32[256,256]{1,0:T(8,128)S(1)}, u32[]{:S(2)}, u32[]{:S(2)}) collective-permute-start(f32[256,256]{1,0:T(8,128)S(1)} %bitcast.5), channel_id=1, source_target_pairs={{8,24},{10,26},{12,28},{14,30},{17,25},{19,27},{21,29},{23,31},{25... | collective-permute-start | bytes 786440 | tf_op jit(solution)/shard_map/ppermute | solution.py:495
  5.0 18.5 %collective-permute-start.1 = (f32[256,256]{1,0:T(8,128)S(1)}, f32[256,256]{1,0:T(8,128)S(1)}, u32[]{:S(2)}, u32[]{:S(2)}) collective-permute-start(f32[256,256]{1,0:T(8,128)S(1)} %bitcast.6), channel_id=1, source_target_pairs={{6,0},{7,1},{2,10},{4,12},{3,11},{5,13}} | collective-permute-start | bytes 786440 | tf_op jit(solution)/shard_map/ppermute | solution.py:495
  5.7 21.4 %copy-start = (f32[1,1,256,4,1,256]{5,4,3,2,1,0:T(1,128)S(1)}, f32[1,1,256,4,1,256]{5,4,3,2,1,0:T(1,128)}, u32[]{:S(2)}) copy-start(f32[1,1,256,4,1,256]{5,4,3,2,1,0:T(1,128)} %matrix.3) | copy-start | bytes 3145732
  5.7 19.9 %collective-permute-start.18 = (f32[256,256]{1,0:T(8,128)S(1)}, f32[256,256]{1,0:T(8,128)S(1)}, u32[]{:S(2)}, u32[]{:S(2)}) collective-permute-start(f32[256,256]{1,0:T(8,128)S(1)} %add.27), channel_id=1, source_target_pairs={{2,10},{3,11},{18,26},{19,27}} | collective-permute-start | bytes 786440 | tf_op jit(solution)/shard_map/ppermute | solution.py:495
  6.6 19.2 %collective-permute-start = (f32[256,256]{1,0:T(8,128)S(1)}, f32[256,256]{1,0:T(8,128)S(1)}, u32[]{:S(2)}, u32[]{:S(2)}) collective-permute-start(f32[256,256]{1,0:T(8,128)S(1)} %bitcast.7), channel_id=1, source_target_pairs={{0,2},{2,0},{1,3},{3,1},{4,6},{6,4},{5,7},{7,5},{8,10},{10,8},{9,1... | collective-permute-start | bytes 786440 | tf_op jit(solution)/shard_map/ppermute | solution.py:504
  18.1 9.2 %collective-permute-start.10 = (f32[256,256]{1,0:T(8,128)S(1)}, f32[256,256]{1,0:T(8,128)S(1)}, u32[]{:S(2)}, u32[]{:S(2)}) collective-permute-start(f32[256,256]{1,0:T(8,128)S(1)} %pick.3), channel_id=1, source_target_pairs={{24,28},{28,24},{26,30},{30,26},{9,13},{13,9},{11,15},{15,11},{17,... | collective-permute-start | bytes 786440 | tf_op jit(solution)/shard_map/ppermute | solution.py:495
  21.6 10.4 %collective-permute-start.9 = (f32[256,256]{1,0:T(8,128)S(1)}, f32[256,256]{1,0:T(8,128)S(1)}, u32[]{:S(2)}, u32[]{:S(2)}) collective-permute-start(f32[256,256]{1,0:T(8,128)S(1)} %pick.2), channel_id=1, source_target_pairs={{8,12},{12,8},{10,14},{14,10},{16,20},{20,16},{18,22},{22,18},{9,1... | collective-permute-start | bytes 786440 | tf_op jit(solution)/shard_map/ppermute | solution.py:495
  23.5 12.2 %collective-permute-start.12 = (f32[256,256]{1,0:T(8,128)S(1)}, f32[256,256]{1,0:T(8,128)S(1)}, u32[]{:S(2)}, u32[]{:S(2)}) collective-permute-start(f32[256,256]{1,0:T(8,128)S(1)} %collective-permute-done.7.refs_1_.refs_0_.refs_2_), channel_id=1, source_target_pairs={{0,2},{2,0},{1,3},{3,1},{4,6},{6,4},{5,7},{7,5},{8,10},{10,8},{9,1... | collective-permute-start | bytes 786440 | tf_op jit(solution)/shard_map/ppermute | solution.py:504
  25.7 10.7 %collective-permute-start.11 = (f32[256,256]{1,0:T(8,128)S(1)}, f32[256,256]{1,0:T(8,128)S(1)}, u32[]{:S(2)}, u32[]{:S(2)}) collective-permute-start(f32[256,256]{1,0:T(8,128)S(1)} %collective-permute-done.1.w11.refs_1_), channel_id=1, source_target_pairs={{0,2},{2,0},{1,3},{3,1},{4,6},{6,4},{5,7},{7,5},{8,10},{10,8},{9,1... | collective-permute-start | bytes 786440 | tf_op jit(solution)/shard_map/ppermute | solution.py:504
  25.8 11.2 %collective-permute-start.19 = (f32[256,256]{1,0:T(8,128)S(1)}, f32[256,256]{1,0:T(8,128)S(1)}, u32[]{:S(2)}, u32[]{:S(2)}) collective-permute-start(f32[256,256]{1,0:T(8,128)S(1)} %add.28), channel_id=1, source_target_pairs={{2,6},{3,7},{10,14},{11,15},{18,22},{19,23},{26,30},{27,31}} | collective-permute-start | bytes 786440 | tf_op jit(solution)/shard_map/ppermute | solution.py:495
  27.4 11.9 %collective-permute-start.6 = (f32[2,256,256]{2,1,0:T(8,128)S(1)}, f32[2,256,256]{2,1,0:T(8,128)S(1)}, u32[]{:S(2)}, u32[]{:S(2)}) collective-permute-start(f32[2,256,256]{2,1,0:T(8,128)S(1)} %get-tuple-element.15), channel_id=1, source_target_pairs={{0,4},{1,5},{2,6},{3,7}} | collective-permute-start | bytes 1572872 | tf_op jit(solution)/shard_map/ppermute | solution.py:495
  32.0 5.8 %collective-permute-start.13 = (f32[256,256]{1,0:T(8,128)S(1)}, f32[256,256]{1,0:T(8,128)S(1)}, u32[]{:S(2)}, u32[]{:S(2)}) collective-permute-start(f32[256,256]{1,0:T(8,128)S(1)} %collective-permute-done.8.refs_1_.refs_3_), channel_id=1, source_target_pairs={{0,2},{2,0},{1,3},{3,1},{4,6},{6,4},{5,7},{7,5},{8,10},{10,8},{9,1... | collective-permute-start | bytes 786440 | tf_op jit(solution)/shard_map/ppermute | solution.py:504
  35.7 2.8 %collective-permute-start.2 = (f32[256,256]{1,0:T(8,128)S(1)}, f32[256,256]{1,0:T(8,128)S(1)}, u32[]{:S(2)}, u32[]{:S(2)}) collective-permute-start(f32[256,256]{1,0:T(8,128)S(1)} %get-tuple-element.14), channel_id=1, source_target_pairs={{0,24},{1,25}} | collective-permute-start | bytes 786440 | tf_op jit(solution)/shard_map/ppermute | solution.py:495
  36.3 2.2 %collective-permute-start.3 = (f32[256,256]{1,0:T(8,128)S(1)}, f32[256,256]{1,0:T(8,128)S(1)}, u32[]{:S(2)}, u32[]{:S(2)}) collective-permute-start(f32[256,256]{1,0:T(8,128)S(1)} %get-tuple-element.14), channel_id=1, source_target_pairs={{0,16},{1,17}} | collective-permute-start | bytes 786440 | tf_op jit(solution)/shard_map/ppermute | solution.py:495
  37.0 2.0 %collective-permute-start.4 = (f32[256,256]{1,0:T(8,128)S(1)}, f32[256,256]{1,0:T(8,128)S(1)}, u32[]{:S(2)}, u32[]{:S(2)}) collective-permute-start(f32[256,256]{1,0:T(8,128)S(1)} %get-tuple-element.14), channel_id=1, source_target_pairs={{0,8},{1,9}} | collective-permute-start | bytes 786440 | tf_op jit(solution)/shard_map/ppermute | solution.py:495
  37.8 3.1 %copy-start.1 = (s32[40]{0:T(128)S(1)}, s32[40]{0:T(128)}, u32[]{:S(2)}) copy-start(s32[40]{0:T(128)} %constant.2.clone.table) | copy-start | bytes 484
  37.8 6.6 %collective-permute-start.5 = (f32[256,256]{1,0:T(8,128)S(1)}, f32[256,256]{1,0:T(8,128)S(1)}, u32[]{:S(2)}, u32[]{:S(2)}) collective-permute-start(f32[256,256]{1,0:T(8,128)S(1)} %get-tuple-element.14), channel_id=1, source_target_pairs={{0,4},{1,5}} | collective-permute-start | bytes 786440 | tf_op jit(solution)/shard_map/ppermute | solution.py:495
  38.5 1.6 %collective-permute-start.15 = (f32[256,256]{1,0:T(8,128)S(1)}, f32[256,256]{1,0:T(8,128)S(1)}, u32[]{:S(2)}, u32[]{:S(2)}) collective-permute-start(f32[256,256]{1,0:T(8,128)S(1)} %collective-permute-done.10.refs_5_), channel_id=1, source_target_pairs={{0,2},{2,0},{1,3},{3,1},{4,6},{6,4},{5,7},{7,5},{8,10},{10,8},{9,1... | collective-permute-start | bytes 786440 | tf_op jit(solution)/shard_map/ppermute | solution.py:504
  38.6 1.9 %collective-permute-start.14 = (f32[256,256]{1,0:T(8,128)S(1)}, f32[256,256]{1,0:T(8,128)S(1)}, u32[]{:S(2)}, u32[]{:S(2)}) collective-permute-start(f32[256,256]{1,0:T(8,128)S(1)} %collective-permute-done.9.refs_4_), channel_id=1, source_target_pairs={{0,2},{2,0},{1,3},{3,1},{4,6},{6,4},{5,7},{7,5},{8,10},{10,8},{9,1... | collective-permute-start | bytes 786440 | tf_op jit(solution)/shard_map/ppermute | solution.py:504
  39.1 1.8 %collective-permute-start.20 = (f32[256,256]{1,0:T(8,128)S(1)}, f32[256,256]{1,0:T(8,128)S(1)}, u32[]{:S(2)}, u32[]{:S(2)}) collective-permute-start(f32[256,256]{1,0:T(8,128)S(1)} %add.29.refs_12_), channel_id=1, source_target_pairs={{0,2},{2,0},{1,3},{3,1},{4,6},{6,4},{5,7},{7,5},{8,10},{10,8},{9,1... | collective-permute-start | bytes 786440 | tf_op jit(solution)/shard_map/ppermute | solution.py:504
  39.2 5.2 %collective-permute-start.21 = (f32[256,256]{1,0:T(8,128)S(1)}, f32[256,256]{1,0:T(8,128)S(1)}, u32[]{:S(2)}, u32[]{:S(2)}) collective-permute-start(f32[256,256]{1,0:T(8,128)S(1)} %add_add_fusion.1), channel_id=1, source_target_pairs={{8,12},{9,13},{16,20},{17,21},{24,28},{25,29}} | collective-permute-start | bytes 786440 | tf_op jit(solution)/shard_map/ppermute | solution.py:495
  44.5 17.2 %collective-permute-start.22 = (f32[256,256]{1,0:T(8,128)S(1)}, f32[256,256]{1,0:T(8,128)S(1)}, u32[]{:S(2)}, u32[]{:S(2)}) collective-permute-start(f32[256,256]{1,0:T(8,128)S(1)} %add_add_fusion.inv_own), channel_id=1, source_target_pairs={{0,2},{2,0},{1,3},{3,1},{4,6},{6,4},{5,7},{7,5},{8,10},{10,8},{9,1... | collective-permute-start | bytes 786440 | tf_op jit(solution)/shard_map/ppermute | solution.py:504

commit v4 on v3

--- a/solution.py
+++ b/solution.py
@@ -39,6 +39,11 @@
 
 def row_of(tile, k):
     return jnp.broadcast_to(tile[k : k + 1, :], tile.shape)
+
+
+def lane_of(tile, lane):
+    index = jnp.full(tile.shape, lane, jnp.int32)
+    return jnp.take_along_axis(tile, index, axis=1)
 
 
 def small_inverse(block):
@@ -52,11 +57,7 @@
     v = [full[SUB * t : SUB * (t + 1)] for t in range(tiles)]
     sub = lax.broadcasted_iota(jnp.int32, (SUB, width), 0)
     for s in range(tiles):
-        c = {
-            (j, t): jnp.broadcast_to(v[t][:, SUB * s + j : SUB * s + j + 1], (SUB, width))
-            for j in range(SUB)
-            for t in range(s, tiles)
-        }
+        c = {(j, t): lane_of(v[t], SUB * s + j) for j in range(SUB) for t in range(s, tiles)}
         pivots = jnp.ones((SUB, width), F32)
         for k in range(0, SUB, 2):
             p = row_of(c[k, s], k)
@@ -70,14 +71,18 @@
             c1 = {j: row_of(c[j, s], k + 1) for j in range(k + 2, SUB)}
             pivots = jnp.where(sub == k, p, jnp.where(sub == k + 1, det * over_p, pivots))
             for t in range(s, tiles):
-                m0 = (w * c[k, t] - q * c[k + 1, t]) * over_det
-                m1 = (p * c[k + 1, t] - q * c[k, t]) * over_det
+                m0 = w * c[k, t] - q * c[k + 1, t]
+                m1 = p * c[k + 1, t] - q * c[k, t]
+                for j in range(k + 2, SUB):
+                    c[j, t] = c[j, t] - (m0 * c0[j] + m1 * c1[j]) * over_det
                 if t == s:
-                    m0 = jnp.where(sub > k + 1, m0, jnp.where(sub == k + 1, q * over_p, 0.0))
-                    m1 = jnp.where(sub > k + 1, m1, 0.0)
-                v[t] = v[t] - m0 * v0 - m1 * v1
-                for j in range(k + 2, SUB):
-                    c[j, t] = c[j, t] - m0 * c0[j] - m1 * c1[j]
+                    m0 = jnp.where(
+                        sub > k + 1, m0 * over_det, jnp.where(sub == k + 1, q * over_p, 0.0)
+                    )
+                    m1 = jnp.where(sub > k + 1, m1 * over_det, 0.0)
+                    v[t] = v[t] - (m0 * v0 + m1 * v1)
+                else:
+                    v[t] = v[t] - (m0 * v0 + m1 * v1) * over_det
         v[s] = v[s] * lax.rsqrt(pivots)
     return jnp.concatenate(v, axis=0)[:, size:]
 
@@ -86,16 +91,23 @@
     n = a.shape[0]
     base = min(n, LANES // 2)
     x[...] = jnp.zeros((n, n), F32)
+    diagonal = a[:base, :base]
     for lo in range(0, n, base):
-        hi = lo + base
-        inv = small_inverse(a[lo:hi, lo:hi])
+        hi, end = lo + base, lo + 2 * base
+        inv = small_inverse(diagonal)
+        if hi < n:
+            upper = nn(inv, a[lo:hi, hi:end])
+            diagonal = a[hi:end, hi:end] - tn(upper, upper)
         if lo:
             x[lo:hi, :lo] = nn(inv, x[lo:hi, :lo])
         x[lo:hi, lo:hi] = inv
         if hi < n:
-            upper = nn(inv, a[lo:hi, hi:])
-            a[hi:, hi:] = a[hi:, hi:] - tn(upper, upper)
-            x[hi:, :hi] = x[hi:, :hi] - tn(upper, x[lo:hi, :hi])
+            x[hi:end, :hi] = x[hi:end, :hi] - tn(upper, x[lo:hi, :hi])
+        if end < n:
+            rest = nn(inv, a[lo:hi, end:])
+            a[hi:end, end:] = a[hi:end, end:] - tn(upper, rest)
+            a[end:, end:] = a[end:, end:] - tn(rest, rest)
+            x[end:, :hi] = x[end:, :hi] - tn(rest, x[lo:hi, :hi])
 
 
 def split(x):
@@ -425,12 +437,14 @@
     )(p0, t1r, t1g, acc, inv_own, inv_sib)
 
 
-def put(rounds, pairs, start):
+def put(rounds, choices):
     for i, taken in enumerate(rounds):
-        if i >= start and all(s != a and t != b for s, t in pairs for a, b in taken):
-            taken.extend(pairs)
-            return i
-    rounds.append(list(pairs))
+        for k in range(len(choices)):
+            pairs = choices[(i - 1 + k) % len(choices)]
+            if i and all(s != a and t != b for s, t in pairs for a, b in taken):
+                taken.extend(pairs)
+                return i
+    rounds.append(list(choices[(len(rounds) - 1) % len(choices)]))
     return len(rounds) - 1
 
 
@@ -441,19 +455,26 @@
     for l in range(layer_total):
         rounds[0] += [((y, 1 - y, l), (2 + y, 1 - y, l)) for y in range(2)]
         arrived[l, 1, "cross"] = 0
+    for t in range(levels - 1, 1, -1):
+        for l in range(layer_total):
+            pairs = [((y, 1 - y, l), (2 * t + y, 1 - y, l)) for y in range(2)]
+            arrived[l, t, "cross"] = put(rounds, [pairs])
     for l in range(layer_total):
         for gap in range(1, levels):
             for h in range(max(1, l * near), (l + 1) * near):
                 for t in (h - gap, h + gap):
                     if 1 <= t < levels:
-                        pairs = [
-                            ((2 * h + y, c, l), (2 * t + y, c, l)) for y in range(2) for c in cores
-                        ]
-                        arrived[l, t, h] = put(rounds, pairs, 1)
-    for t in range(levels - 1, 1, -1):
-        for l in range(layer_total):
-            pairs = [((y, 1 - y, l), (2 * t + y, 1 - y, l)) for y in range(2)]
-            arrived[l, t, "cross"] = put(rounds, pairs, 1)
+                        arrived[l, t, h] = put(
+                            rounds,
+                            [
+                                [
+                                    ((2 * h + y, c, (l + k) % layer_total), (2 * t + y, c, l))
+                                    for y in range(2)
+                                    for c in cores
+                                ]
+                                for k in range(layer_total)
+                            ],
+                        )
     return rounds, arrived
 
 
@@ -538,16 +559,10 @@
         )
         own.append(permute(send, pairs))
 
-    even = inv0_sib
-    gap = levels // 2
-    while gap:
-        pairs = [
-            ((2 * t, 1, l), (2 * t + 2 * gap, 1, l))
-            for t in range(0, levels, 2 * gap)
-            for l in range(layer_total)
-        ]
-        even = even + permute(even, pairs)
-        gap //= 2
+    spread = []
+    for t in range(levels - 1, 0, -1):
+        spread.append(permute(inv0_sib, [((0, 1, l), (2 * t, 1, l)) for l in range(layer_total)]))
+    even = sum(spread, inv0_sib)
     back = permute_rows(even, [(2 * t, 2 * t + 1) for t in range(levels)], [1])
     inv0_own = even + back
     inv0_sib = sibling(inv0_own)
@@ -579,7 +594,8 @@
     in_specs = (P(None, "row", None, None, "col", None),)
     out_specs = P(None, "row", None, "layer", "col", None)
     levels = mesh.shape["row"] // 2
-    _, _ = gather_plan(levels, levels // mesh.shape["layer"], mesh.shape["layer"], mesh.shape["col"])
+    near = levels // mesh.shape["layer"]
+    _, _ = gather_plan(levels, near, mesh.shape["layer"], mesh.shape["col"])
 
     return jax.shard_map(
         on_device, mesh=mesh, in_specs=in_specs, out_specs=out_specs, check_vma=False

time: 64.7 us -> 63.8 us (0.986)
  the two profiles are of different devices: /device:TPU:15 before, /device:TPU:0 now
where the time goes in v4:
time: 63.8 us; the launch traced here: 62.7 us
  starting transfers between devices  33.7 us (53%)
  Pallas kernels  19.7 us (31%)
  waiting for transfers between devices  7.54 us (12%)
  local copies, waits for them, and re-layouts  0.98 us (2%)
    ppermute x16, starting transfers between devices, permute(): return lax.ppermute(x, AXES, [(device(*s), device(*t)) for s, t in pairs])  22.8 us
    ppermute x8, starting transfers between devices, sibling(): return lax.ppermute(x, 'col', swap)  11 us
    pallas_call x1, Pallas kernels, call_second(): pl.pallas_call(second_kernel, out_shape=(jax.ShapeDtypeStruct((n, n), F32...  7.78 us
    pallas_call x1, Pallas kernels, call_first(): pl.pallas_call(first_kernel, out_shape=jax.ShapeDtypeStruct((n, n), F32),...  6.41 us
    ppermute x16, waiting for transfers between devices, permute(): return lax.ppermute(x, AXES, [(device(*s), device(*t)) for s, t in pairs])  5.39 us
    pallas_call x1, Pallas kernels, call_early(): pl.pallas_call(functools.partial(early_kernel, dims), out_shape=(block, b...  3.59 us
    ppermute x8, waiting for transfers between devices, sibling(): return lax.ppermute(x, 'col', swap)  2.15 us
    pallas_call x1, Pallas kernels, call_late(): pl.pallas_call(functools.partial(late_kernel, owned, col_total), out_shap...  1.82 us
  transfers between devices with their start and end apart: 24, of which 4 were waited for; matrix products, arithmetic and copies ran while one was open for 0% of the time, Pallas kernels for 18%

profile of v4, /device:TPU:0, one launch (start us, length us, event | category | flops | bytes accessed | tf_op | source)
XLA Modules:
  0.0 62.7 jit_solution(12481255238171343471)
XLA Ops:
  0.0 0.9 %slice-done = f32[1,1,256,1,1,256]{5,4,3,2,1,0:T(1,128)S(1)} async-done(((f32[1,1,256,4,1,256]{5,4,3,2,1,0:T(1,128)}), f32[1,1,256,1,1,256]{5,4,3,2,1,0:T(1,128)S(1)}, s32[]{:S(2)}) %slice-start) | async-done | bytes 262168 | tf_op jit(solution)/shard_map/slice | solution.py:531
  1.0 6.4 %first.1.inv0 = f32[256,256]{1,0:T(8,128)S(1)} custom-call(f32[256,256]{1,0:T(8,128)S(1)} %bitcast.3), custom_call_target="tpu_custom_call" | custom-call | flops 671088640 | bytes 16777216 | tf_op jit(solution)/shard_map/first/pallas_call | solution.py:211
  7.4 1.3 %collective-permute-start.16 = (f32[256,256]{1,0:T(8,128)S(1)}, f32[256,256]{1,0:T(8,128)S(1)}, u32[]{:S(2)}, u32[]{:S(2)}) collective-permute-start(f32[256,256]{1,0:T(8,128)S(1)} %first.1.inv0), channel_id=1, source_target_pairs={{0,2},{1,3}} | collective-permute-start | bytes 786440 | tf_op jit(solution)/shard_map/ppermute | solution.py:516
  8.7 0.7 %collective-permute-start.7 = (f32[256,256]{1,0:T(8,128)S(1)}, f32[256,256]{1,0:T(8,128)S(1)}, u32[]{:S(2)}, u32[]{:S(2)}) collective-permute-start(f32[256,256]{1,0:T(8,128)S(1)} %bitcast.4), channel_id=1, source_target_pairs={{2,26},{4,28},{3,27},{5,29},{8,16},{10,18},{12,20},{14,22},{17,9},... | collective-permute-start | bytes 786440 | tf_op jit(solution)/shard_map/ppermute | solution.py:516
  9.4 0.7 %collective-permute-start.8 = (f32[256,256]{1,0:T(8,128)S(1)}, f32[256,256]{1,0:T(8,128)S(1)}, u32[]{:S(2)}, u32[]{:S(2)}) collective-permute-start(f32[256,256]{1,0:T(8,128)S(1)} %bitcast.5), channel_id=1, source_target_pairs={{2,18},{4,20},{3,19},{5,21},{9,24},{11,26},{13,28},{15,30},{16,25}... | collective-permute-start | bytes 786440 | tf_op jit(solution)/shard_map/ppermute | solution.py:516
  10.1 1.3 %collective-permute-start.1 = (f32[256,256]{1,0:T(8,128)S(1)}, f32[256,256]{1,0:T(8,128)S(1)}, u32[]{:S(2)}, u32[]{:S(2)}) collective-permute-start(f32[256,256]{1,0:T(8,128)S(1)} %bitcast.6), channel_id=1, source_target_pairs={{6,0},{7,1},{2,10},{4,12},{3,11},{5,13}} | collective-permute-start | bytes 786440 | tf_op jit(solution)/shard_map/ppermute | solution.py:516
  11.4 0.7 %collective-permute-start.17 = (f32[256,256]{1,0:T(8,128)S(1)}, f32[256,256]{1,0:T(8,128)S(1)}, u32[]{:S(2)}, u32[]{:S(2)}) collective-permute-start(f32[256,256]{1,0:T(8,128)S(1)} %collective-permute-done.16), channel_id=1, source_target_pairs={{2,26},{3,27}} | collective-permute-start | bytes 786440 | tf_op jit(solution)/shard_map/ppermute | solution.py:516
  12.1 0.7 %collective-permute-start.18 = (f32[256,256]{1,0:T(8,128)S(1)}, f32[256,256]{1,0:T(8,128)S(1)}, u32[]{:S(2)}, u32[]{:S(2)}) collective-permute-start(f32[256,256]{1,0:T(8,128)S(1)} %collective-permute-done.16), channel_id=1, source_target_pairs={{2,18},{3,19}} | collective-permute-start | bytes 786440 | tf_op jit(solution)/shard_map/ppermute | solution.py:516
  12.8 0.7 %collective-permute-start.19 = (f32[256,256]{1,0:T(8,128)S(1)}, f32[256,256]{1,0:T(8,128)S(1)}, u32[]{:S(2)}, u32[]{:S(2)}) collective-permute-start(f32[256,256]{1,0:T(8,128)S(1)} %collective-permute-done.16), channel_id=1, source_target_pairs={{2,10},{3,11}} | collective-permute-start | bytes 786440 | tf_op jit(solution)/shard_map/ppermute | solution.py:516
  13.5 6.6 %collective-permute-start = (f32[256,256]{1,0:T(8,128)S(1)}, f32[256,256]{1,0:T(8,128)S(1)}, u32[]{:S(2)}, u32[]{:S(2)}) collective-permute-start(f32[256,256]{1,0:T(8,128)S(1)} %bitcast.7), channel_id=1, source_target_pairs={{0,2},{2,0},{1,3},{3,1},{4,6},{6,4},{5,7},{7,5},{8,10},{10,8},{9,1... | collective-permute-start | bytes 786440 | tf_op jit(solution)/shard_map/ppermute | solution.py:525
  20.2 0.8 %collective-permute-start.10 = (f32[256,256]{1,0:T(8,128)S(1)}, f32[256,256]{1,0:T(8,128)S(1)}, u32[]{:S(2)}, u32[]{:S(2)}) collective-permute-start(f32[256,256]{1,0:T(8,128)S(1)} %pick.3), channel_id=1, source_target_pairs={{24,28},{28,24},{26,30},{30,26},{9,13},{13,9},{11,15},{15,11},{17,... | collective-permute-start | bytes 786440 | tf_op jit(solution)/shard_map/ppermute | solution.py:516
  21.0 0.7 %collective-permute-start.9 = (f32[256,256]{1,0:T(8,128)S(1)}, f32[256,256]{1,0:T(8,128)S(1)}, u32[]{:S(2)}, u32[]{:S(2)}) collective-permute-start(f32[256,256]{1,0:T(8,128)S(1)} %pick.2), channel_id=1, source_target_pairs={{8,12},{12,8},{10,14},{14,10},{16,20},{20,16},{18,22},{22,18},{9,1... | collective-permute-start | bytes 786440 | tf_op jit(solution)/shard_map/ppermute | solution.py:516
  21.7 1.2 %collective-permute-start.12 = (f32[256,256]{1,0:T(8,128)S(1)}, f32[256,256]{1,0:T(8,128)S(1)}, u32[]{:S(2)}, u32[]{:S(2)}) collective-permute-start(f32[256,256]{1,0:T(8,128)S(1)} %collective-permute-done.7.refs_1_.refs_0_.refs_2_), channel_id=1, source_target_pairs={{0,2},{2,0},{1,3},{3,1},{4,6},{6,4},{5,7},{7,5},{8,10},{10,8},{9,1... | collective-permute-start | bytes 786440 | tf_op jit(solution)/shard_map/ppermute | solution.py:525
  22.9 2.8 %collective-permute-start.11 = (f32[256,256]{1,0:T(8,128)S(1)}, f32[256,256]{1,0:T(8,128)S(1)}, u32[]{:S(2)}, u32[]{:S(2)}) collective-permute-start(f32[256,256]{1,0:T(8,128)S(1)} %collective-permute-done.1.w11.refs_1_), channel_id=1, source_target_pairs={{0,2},{2,0},{1,3},{3,1},{4,6},{6,4},{5,7},{7,5},{8,10},{10,8},{9,1... | collective-permute-start | bytes 786440 | tf_op jit(solution)/shard_map/ppermute | solution.py:525
  25.7 0.1 add_add_fusion.1
  25.8 0.7 %collective-permute-start.20 = (f32[256,256]{1,0:T(8,128)S(1)}, f32[256,256]{1,0:T(8,128)S(1)}, u32[]{:S(2)}, u32[]{:S(2)}) collective-permute-start(f32[256,256]{1,0:T(8,128)S(1)} %add_add_fusion.1), channel_id=1, source_target_pairs={{2,6},{3,7},{10,14},{11,15},{18,22},{19,23},{26,30},{27,31}} | collective-permute-start | bytes 786440 | tf_op jit(solution)/shard_map/ppermute | solution.py:516
  26.5 7.8 %second.1 = (f32[256,256]{1,0:T(8,128)S(1)}, f32[2,256,256]{2,1,0:T(8,128)S(1)}) custom-call(f32[256,256]{1,0:T(8,128)S(1)} %first.1.inv0, f32[256,256]{1,0:T(8,128)S(1)} %collective-permute-done.w01.refs_6_, f32[256,256]{1,0:T(8,128)S(1)} %collective-permute-done.1.w11.refs_1_, f32[1,1,256,4,1,256]{5,4,3,2,1,0:T(1,128)S(1)} %copy-done), custom_call_target="tpu_custom_call" | custom-call | flops 671088640 | bytes 16777216 | tf_op jit(solution)/shard_map/second/pallas_call | solution.py:225
  34.3 1.5 %collective-permute-start.6 = (f32[2,256,256]{2,1,0:T(8,128)S(1)}, f32[2,256,256]{2,1,0:T(8,128)S(1)}, u32[]{:S(2)}, u32[]{:S(2)}) collective-permute-start(f32[2,256,256]{2,1,0:T(8,128)S(1)} %get-tuple-element.15), channel_id=1, source_target_pairs={{0,4},{1,5},{2,6},{3,7}} | collective-permute-start | bytes 1572872 | tf_op jit(solution)/shard_map/ppermute | solution.py:516
  35.8 0.1 collective-permute-start.13
  35.9 8.5 %collective-permute-start.2 = (f32[256,256]{1,0:T(8,128)S(1)}, f32[256,256]{1,0:T(8,128)S(1)}, u32[]{:S(2)}, u32[]{:S(2)}) collective-permute-start(f32[256,256]{1,0:T(8,128)S(1)} %get-tuple-element.14), channel_id=1, source_target_pairs={{0,24},{1,25}} | collective-permute-start | bytes 786440 | tf_op jit(solution)/shard_map/ppermute | solution.py:516
  44.4 1.3 %collective-permute-start.3 = (f32[256,256]{1,0:T(8,128)S(1)}, f32[256,256]{1,0:T(8,128)S(1)}, u32[]{:S(2)}, u32[]{:S(2)}) collective-permute-start(f32[256,256]{1,0:T(8,128)S(1)} %get-tuple-element.14), channel_id=1, source_target_pairs={{0,16},{1,17}} | collective-permute-start | bytes 786440 | tf_op jit(solution)/shard_map/ppermute | solution.py:516
  45.8 1.3 %collective-permute-start.4 = (f32[256,256]{1,0:T(8,128)S(1)}, f32[256,256]{1,0:T(8,128)S(1)}, u32[]{:S(2)}, u32[]{:S(2)}) collective-permute-start(f32[256,256]{1,0:T(8,128)S(1)} %get-tuple-element.14), channel_id=1, source_target_pairs={{0,8},{1,9}} | collective-permute-start | bytes 786440 | tf_op jit(solution)/shard_map/ppermute | solution.py:516
  47.1 1.3 %collective-permute-start.5 = (f32[256,256]{1,0:T(8,128)S(1)}, f32[256,256]{1,0:T(8,128)S(1)}, u32[]{:S(2)}, u32[]{:S(2)}) collective-permute-start(f32[256,256]{1,0:T(8,128)S(1)} %get-tuple-element.14), channel_id=1, source_target_pairs={{0,4},{1,5}} | collective-permute-start | bytes 786440 | tf_op jit(solution)/shard_map/ppermute | solution.py:516
  48.5 0.1 collective-permute-start.15
  48.5 2.5 %collective-permute-done.3 = f32[256,256]{1,0:T(8,128)S(1)} collective-permute-done((f32[256,256]{1,0:T(8,128)S(1)}, f32[256,256]{1,0:T(8,128)S(1)}, u32[]{:S(2)}, u32[]{:S(2)}) %collective-permute-start.3) | collective-permute-done | bytes 262176 | tf_op jit(solution)/shard_map/ppermute | solution.py:516
  51.1 2.8 %collective-permute-done.4 = f32[256,256]{1,0:T(8,128)S(1)} collective-permute-done((f32[256,256]{1,0:T(8,128)S(1)}, f32[256,256]{1,0:T(8,128)S(1)}, u32[]{:S(2)}, u32[]{:S(2)}) %collective-permute-start.4) | collective-permute-done | bytes 262176 | tf_op jit(solution)/shard_map/ppermute | solution.py:516
  54.0 0.7 %collective-permute-start.22 = (f32[256,256]{1,0:T(8,128)S(1)}, f32[256,256]{1,0:T(8,128)S(1)}, u32[]{:S(2)}, u32[]{:S(2)}) collective-permute-start(f32[256,256]{1,0:T(8,128)S(1)} %add_add_fusion.2), channel_id=1, source_target_pairs={{8,12},{9,13},{16,20},{17,21},{24,28},{25,29}} | collective-permute-start | bytes 786440 | tf_op jit(solution)/shard_map/ppermute | solution.py:516
  54.7 0.7 %collective-permute-done.21.refs_13_ = f32[256,256]{1,0:T(8,128)S(1)} collective-permute-done((f32[256,256]{1,0:T(8,128)S(1)}, f32[256,256]{1,0:T(8,128)S(1)}, u32[]{:S(2)}, u32[]{:S(2)}) %collective-permute-start.21) | collective-permute-done | bytes 262176 | tf_op jit(solution)/shard_map/ppermute | solution.py:525
  55.4 3.6 %early.1 = (f32[256,256]{1,0:T(8,128)S(1)}, f32[256,256]{1,0:T(8,128)S(1)}, f32[2,256,256]{2,1,0:T(8,128)S(1)}, f32[2,256,256]{2,1,0:T(8,128)S(1)}) custom-call(s32[40]{0:T(128)S(1)} %copy-done.1, f32[1,1,256,4,1,256]{5,4,3,2,1,0:T(1,128)S(1)} %copy-done, f32[2,256,256]{2,1,0:T(8,128)S(1)} %collective-permute-done.6.above, f32[256,256]{1,0:T(8,128)S(1)} %bitcast.9, ...), custom_call_target="tpu_custom_call" | custom-call | flops 1006632960 | bytes 8388608 | tf_op jit(solution)/shard_map/early/pallas_call | solution.py:403
  59.1 0.2 collective-permute-start.23
  59.3 1.4 %collective-permute-done.23.inv_sib = f32[256,256]{1,0:T(8,128)S(1)} collective-permute-done((f32[256,256]{1,0:T(8,128)S(1)}, f32[256,256]{1,0:T(8,128)S(1)}, u32[]{:S(2)}, u32[]{:S(2)}) %collective-permute-start.23) | collective-permute-done | bytes 262176 | tf_op jit(solution)/shard_map/ppermute | solution.py:525
  60.7 1.8 %late.1 = f32[1,1,256,2,1,256]{5,4,3,2,1,0:T(1,128)} custom-call(f32[256,256]{1,0:T(8,128)S(1)} %get-tuple-element.17.p0, f32[256,256]{1,0:T(8,128)S(1)} %get-tuple-element.18.t1r, f32[2,256,256]{2,1,0:T(8,128)S(1)} %get-tuple-element.19.t1g, f32[2,256,256]{2,1,0:T(8,128)S(1)} %get-tuple-element.20.acc, f32[256,256]{1,0:T(8,128)S(1)} %add_add_fusion.inv_own, ...), custom_call_target="tpu_custom_call" | custom-call | flops 503316480 | bytes 4194304 | tf_op jit(solution)/shard_map/late/pallas_call | solution.py:423
  (33 shorter events, 0.3 us)
Async XLA Ops:
  0.0 0.9 %slice-start = ((f32[1,1,256,4,1,256]{5,4,3,2,1,0:T(1,128)}), f32[1,1,256,1,1,256]{5,4,3,2,1,0:T(1,128)S(1)}, s32[]{:S(2)}) async-start(f32[1,1,256,4,1,256]{5,4,3,2,1,0:T(1,128)} %matrix.3), calls=%async_computation | async-start | bytes 524288 | tf_op jit(solution)/shard_map/slice | solution.py:531
  7.4 4.0 %collective-permute-start.16 = (f32[256,256]{1,0:T(8,128)S(1)}, f32[256,256]{1,0:T(8,128)S(1)}, u32[]{:S(2)}, u32[]{:S(2)}) collective-permute-start(f32[256,256]{1,0:T(8,128)S(1)} %first.1.inv0), channel_id=1, source_target_pairs={{0,2},{1,3}} | collective-permute-start | bytes 786440 | tf_op jit(solution)/shard_map/ppermute | solution.py:516
  8.7 4.1 %collective-permute-start.7 = (f32[256,256]{1,0:T(8,128)S(1)}, f32[256,256]{1,0:T(8,128)S(1)}, u32[]{:S(2)}, u32[]{:S(2)}) collective-permute-start(f32[256,256]{1,0:T(8,128)S(1)} %bitcast.4), channel_id=1, source_target_pairs={{2,26},{4,28},{3,27},{5,29},{8,16},{10,18},{12,20},{14,22},{17,9},... | collective-permute-start | bytes 786440 | tf_op jit(solution)/shard_map/ppermute | solution.py:516
  9.4 4.1 %collective-permute-start.8 = (f32[256,256]{1,0:T(8,128)S(1)}, f32[256,256]{1,0:T(8,128)S(1)}, u32[]{:S(2)}, u32[]{:S(2)}) collective-permute-start(f32[256,256]{1,0:T(8,128)S(1)} %bitcast.5), channel_id=1, source_target_pairs={{2,18},{4,20},{3,19},{5,21},{9,24},{11,26},{13,28},{15,30},{16,25}... | collective-permute-start | bytes 786440 | tf_op jit(solution)/shard_map/ppermute | solution.py:516
  10.1 10.1 %collective-permute-start.1 = (f32[256,256]{1,0:T(8,128)S(1)}, f32[256,256]{1,0:T(8,128)S(1)}, u32[]{:S(2)}, u32[]{:S(2)}) collective-permute-start(f32[256,256]{1,0:T(8,128)S(1)} %bitcast.6), channel_id=1, source_target_pairs={{6,0},{7,1},{2,10},{4,12},{3,11},{5,13}} | collective-permute-start | bytes 786440 | tf_op jit(solution)/shard_map/ppermute | solution.py:516
  11.4 9.6 %collective-permute-start.17 = (f32[256,256]{1,0:T(8,128)S(1)}, f32[256,256]{1,0:T(8,128)S(1)}, u32[]{:S(2)}, u32[]{:S(2)}) collective-permute-start(f32[256,256]{1,0:T(8,128)S(1)} %collective-permute-done.16), channel_id=1, source_target_pairs={{2,26},{3,27}} | collective-permute-start | bytes 786440 | tf_op jit(solution)/shard_map/ppermute | solution.py:516
  12.1 9.6 %collective-permute-start.18 = (f32[256,256]{1,0:T(8,128)S(1)}, f32[256,256]{1,0:T(8,128)S(1)}, u32[]{:S(2)}, u32[]{:S(2)}) collective-permute-start(f32[256,256]{1,0:T(8,128)S(1)} %collective-permute-done.16), channel_id=1, source_target_pairs={{2,18},{3,19}} | collective-permute-start | bytes 786440 | tf_op jit(solution)/shard_map/ppermute | solution.py:516
  12.8 10.1 %collective-permute-start.19 = (f32[256,256]{1,0:T(8,128)S(1)}, f32[256,256]{1,0:T(8,128)S(1)}, u32[]{:S(2)}, u32[]{:S(2)}) collective-permute-start(f32[256,256]{1,0:T(8,128)S(1)} %collective-permute-done.16), channel_id=1, source_target_pairs={{2,10},{3,11}} | collective-permute-start | bytes 786440 | tf_op jit(solution)/shard_map/ppermute | solution.py:516
  13.5 12.3 %collective-permute-start = (f32[256,256]{1,0:T(8,128)S(1)}, f32[256,256]{1,0:T(8,128)S(1)}, u32[]{:S(2)}, u32[]{:S(2)}) collective-permute-start(f32[256,256]{1,0:T(8,128)S(1)} %bitcast.7), channel_id=1, source_target_pairs={{0,2},{2,0},{1,3},{3,1},{4,6},{6,4},{5,7},{7,5},{8,10},{10,8},{9,1... | collective-permute-start | bytes 786440 | tf_op jit(solution)/shard_map/ppermute | solution.py:525
  20.1 6.3 %copy-start = (f32[1,1,256,4,1,256]{5,4,3,2,1,0:T(1,128)S(1)}, f32[1,1,256,4,1,256]{5,4,3,2,1,0:T(1,128)}, u32[]{:S(2)}) copy-start(f32[1,1,256,4,1,256]{5,4,3,2,1,0:T(1,128)} %matrix.3) | copy-start | bytes 3145732
  20.2 14.1 %collective-permute-start.10 = (f32[256,256]{1,0:T(8,128)S(1)}, f32[256,256]{1,0:T(8,128)S(1)}, u32[]{:S(2)}, u32[]{:S(2)}) collective-permute-start(f32[256,256]{1,0:T(8,128)S(1)} %pick.3), channel_id=1, source_target_pairs={{24,28},{28,24},{26,30},{30,26},{9,13},{13,9},{11,15},{15,11},{17,... | collective-permute-start | bytes 786440 | tf_op jit(solution)/shard_map/ppermute | solution.py:516
  21.0 14.8 %collective-permute-start.9 = (f32[256,256]{1,0:T(8,128)S(1)}, f32[256,256]{1,0:T(8,128)S(1)}, u32[]{:S(2)}, u32[]{:S(2)}) collective-permute-start(f32[256,256]{1,0:T(8,128)S(1)} %pick.2), channel_id=1, source_target_pairs={{8,12},{12,8},{10,14},{14,10},{16,20},{20,16},{18,22},{22,18},{9,1... | collective-permute-start | bytes 786440 | tf_op jit(solution)/shard_map/ppermute | solution.py:516
  21.7 14.2 %collective-permute-start.12 = (f32[256,256]{1,0:T(8,128)S(1)}, f32[256,256]{1,0:T(8,128)S(1)}, u32[]{:S(2)}, u32[]{:S(2)}) collective-permute-start(f32[256,256]{1,0:T(8,128)S(1)} %collective-permute-done.7.refs_1_.refs_0_.refs_2_), channel_id=1, source_target_pairs={{0,2},{2,0},{1,3},{3,1},{4,6},{6,4},{5,7},{7,5},{8,10},{10,8},{9,1... | collective-permute-start | bytes 786440 | tf_op jit(solution)/shard_map/ppermute | solution.py:525
  22.9 21.5 %collective-permute-start.11 = (f32[256,256]{1,0:T(8,128)S(1)}, f32[256,256]{1,0:T(8,128)S(1)}, u32[]{:S(2)}, u32[]{:S(2)}) collective-permute-start(f32[256,256]{1,0:T(8,128)S(1)} %collective-permute-done.1.w11.refs_1_), channel_id=1, source_target_pairs={{0,2},{2,0},{1,3},{3,1},{4,6},{6,4},{5,7},{7,5},{8,10},{10,8},{9,1... | collective-permute-start | bytes 786440 | tf_op jit(solution)/shard_map/ppermute | solution.py:525
  25.8 20.0 %collective-permute-start.20 = (f32[256,256]{1,0:T(8,128)S(1)}, f32[256,256]{1,0:T(8,128)S(1)}, u32[]{:S(2)}, u32[]{:S(2)}) collective-permute-start(f32[256,256]{1,0:T(8,128)S(1)} %add_add_fusion.1), channel_id=1, source_target_pairs={{2,6},{3,7},{10,14},{11,15},{18,22},{19,23},{26,30},{27,31}} | collective-permute-start | bytes 786440 | tf_op jit(solution)/shard_map/ppermute | solution.py:516
  34.3 19.7 %collective-permute-start.6 = (f32[2,256,256]{2,1,0:T(8,128)S(1)}, f32[2,256,256]{2,1,0:T(8,128)S(1)}, u32[]{:S(2)}, u32[]{:S(2)}) collective-permute-start(f32[2,256,256]{2,1,0:T(8,128)S(1)} %get-tuple-element.15), channel_id=1, source_target_pairs={{0,4},{1,5},{2,6},{3,7}} | collective-permute-start | bytes 1572872 | tf_op jit(solution)/shard_map/ppermute | solution.py:516
  35.8 11.3 %collective-permute-start.13 = (f32[256,256]{1,0:T(8,128)S(1)}, f32[256,256]{1,0:T(8,128)S(1)}, u32[]{:S(2)}, u32[]{:S(2)}) collective-permute-start(f32[256,256]{1,0:T(8,128)S(1)} %collective-permute-done.8.refs_1_.refs_3_), channel_id=1, source_target_pairs={{0,2},{2,0},{1,3},{3,1},{4,6},{6,4},{5,7},{7,5},{8,10},{10,8},{9,1... | collective-permute-start | bytes 786440 | tf_op jit(solution)/shard_map/ppermute | solution.py:525
  35.9 12.6 %collective-permute-start.2 = (f32[256,256]{1,0:T(8,128)S(1)}, f32[256,256]{1,0:T(8,128)S(1)}, u32[]{:S(2)}, u32[]{:S(2)}) collective-permute-start(f32[256,256]{1,0:T(8,128)S(1)} %get-tuple-element.14), channel_id=1, source_target_pairs={{0,24},{1,25}} | collective-permute-start | bytes 786440 | tf_op jit(solution)/shard_map/ppermute | solution.py:516
  44.4 6.7 %collective-permute-start.3 = (f32[256,256]{1,0:T(8,128)S(1)}, f32[256,256]{1,0:T(8,128)S(1)}, u32[]{:S(2)}, u32[]{:S(2)}) collective-permute-start(f32[256,256]{1,0:T(8,128)S(1)} %get-tuple-element.14), channel_id=1, source_target_pairs={{0,16},{1,17}} | collective-permute-start | bytes 786440 | tf_op jit(solution)/shard_map/ppermute | solution.py:516
  45.8 8.1 %collective-permute-start.4 = (f32[256,256]{1,0:T(8,128)S(1)}, f32[256,256]{1,0:T(8,128)S(1)}, u32[]{:S(2)}, u32[]{:S(2)}) collective-permute-start(f32[256,256]{1,0:T(8,128)S(1)} %get-tuple-element.14), channel_id=1, source_target_pairs={{0,8},{1,9}} | collective-permute-start | bytes 786440 | tf_op jit(solution)/shard_map/ppermute | solution.py:516
  47.1 8.3 %copy-start.1 = (s32[40]{0:T(128)S(1)}, s32[40]{0:T(128)}, u32[]{:S(2)}) copy-start(s32[40]{0:T(128)} %constant.2.clone.table) | copy-start | bytes 484
  47.1 11.9 %collective-permute-start.5 = (f32[256,256]{1,0:T(8,128)S(1)}, f32[256,256]{1,0:T(8,128)S(1)}, u32[]{:S(2)}, u32[]{:S(2)}) collective-permute-start(f32[256,256]{1,0:T(8,128)S(1)} %get-tuple-element.14), channel_id=1, source_target_pairs={{0,4},{1,5}} | collective-permute-start | bytes 786440 | tf_op jit(solution)/shard_map/ppermute | solution.py:516
  48.5 6.2 %collective-permute-start.15 = (f32[256,256]{1,0:T(8,128)S(1)}, f32[256,256]{1,0:T(8,128)S(1)}, u32[]{:S(2)}, u32[]{:S(2)}) collective-permute-start(f32[256,256]{1,0:T(8,128)S(1)} %collective-permute-done.10.refs_5_), channel_id=1, source_target_pairs={{0,2},{2,0},{1,3},{3,1},{4,6},{6,4},{5,7},{7,5},{8,10},{10,8},{9,1... | collective-permute-start | bytes 786440 | tf_op jit(solution)/shard_map/ppermute | solution.py:525
  51.1 3.6 %collective-permute-start.14 = (f32[256,256]{1,0:T(8,128)S(1)}, f32[256,256]{1,0:T(8,128)S(1)}, u32[]{:S(2)}, u32[]{:S(2)}) collective-permute-start(f32[256,256]{1,0:T(8,128)S(1)} %collective-permute-done.9.refs_4_), channel_id=1, source_target_pairs={{0,2},{2,0},{1,3},{3,1},{4,6},{6,4},{5,7},{7,5},{8,10},{10,8},{9,1... | collective-permute-start | bytes 786440 | tf_op jit(solution)/shard_map/ppermute | solution.py:525
  53.9 1.5 %collective-permute-start.21 = (f32[256,256]{1,0:T(8,128)S(1)}, f32[256,256]{1,0:T(8,128)S(1)}, u32[]{:S(2)}, u32[]{:S(2)}) collective-permute-start(f32[256,256]{1,0:T(8,128)S(1)} %add.33.refs_12_), channel_id=1, source_target_pairs={{0,2},{2,0},{1,3},{3,1},{4,6},{6,4},{5,7},{7,5},{8,10},{10,8},{9,1... | collective-permute-start | bytes 786440 | tf_op jit(solution)/shard_map/ppermute | solution.py:525
  54.0 5.1 %collective-permute-start.22 = (f32[256,256]{1,0:T(8,128)S(1)}, f32[256,256]{1,0:T(8,128)S(1)}, u32[]{:S(2)}, u32[]{:S(2)}) collective-permute-start(f32[256,256]{1,0:T(8,128)S(1)} %add_add_fusion.2), channel_id=1, source_target_pairs={{8,12},{9,13},{16,20},{17,21},{24,28},{25,29}} | collective-permute-start | bytes 786440 | tf_op jit(solution)/shard_map/ppermute | solution.py:516
  59.1 1.6 %collective-permute-start.23 = (f32[256,256]{1,0:T(8,128)S(1)}, f32[256,256]{1,0:T(8,128)S(1)}, u32[]{:S(2)}, u32[]{:S(2)}) collective-permute-start(f32[256,256]{1,0:T(8,128)S(1)} %add_add_fusion.inv_own), channel_id=1, source_target_pairs={{0,2},{2,0},{1,3},{3,1},{4,6},{6,4},{5,7},{7,5},{8,10},{10,8},{9,1... | collective-permute-start | bytes 786440 | tf_op jit(solution)/shard_map/ppermute | solution.py:525

commit v5 on v4

--- a/solution.py
+++ b/solution.py
@@ -139,18 +139,36 @@
     return (row == 0) & (col == 0)
 
 
-def first_kernel(w00, inv, a):
+def pack(x, out):
+    n = x.shape[0]
+    half, quarter = n // 2, n // 4
+    out[:half] = x[half:]
+    out[half:, :half] = x[:quarter, :half]
+    out[half:, half:] = x[quarter:half, :half]
+
+
+def unpack(source, x):
+    n = x.shape[0]
+    half, quarter = n // 2, n // 4
+    x[half:] = source[:half]
+    x[:quarter, :half] = source[half:, :half]
+    x[quarter:half, :half] = source[half:, half:]
+    x[:half, half:] = jnp.zeros((half, half), F32)
+
+
+def first_kernel(w00, inv, packed, a):
     @pl.when(is_owner())
     def _():
         a[...] = w00[...]
         inverse_factor(a, inv)
+        pack(inv, packed)
 
     @pl.when(jnp.logical_not(is_owner()))
     def _():
-        inv[...] = jnp.zeros_like(inv)
-
-
-def second_kernel(inv0, w01, w11, matrix, inv1, tiles, a, sems):
+        packed[...] = jnp.zeros_like(packed)
+
+
+def second_kernel(inv0, w01, w11, matrix, packed, tiles, a, x, sems):
     row, _, layer = place()
     owned = tiles.shape[0]
 
@@ -168,11 +186,12 @@
     def _():
         q = nn(inv0[...], w01[...])
         a[...] = w11[...] - tn(q, q)
-        inverse_factor(a, inv1)
+        inverse_factor(a, x)
+        pack(x, packed)
 
     @pl.when(jnp.logical_not(is_owner()))
     def _():
-        inv1[...] = jnp.zeros_like(inv1)
+        packed[...] = jnp.zeros_like(packed)
 
     @pl.when(row == 0)
     def _():
@@ -210,12 +229,15 @@
     n = w00.shape[0]
     return pl.pallas_call(
         first_kernel,
-        out_shape=jax.ShapeDtypeStruct((n, n), F32),
+        out_shape=(
+            jax.ShapeDtypeStruct((n, n), F32),
+            jax.ShapeDtypeStruct((n - n // 4, n), F32),
+        ),
         in_specs=[VMEM],
-        out_specs=VMEM,
+        out_specs=(VMEM, VMEM),
         scratch_shapes=[pltpu.VMEM((n, n), F32)],
         cost_estimate=factor_cost(n),
-        compiler_params=grant(n, 3),
+        compiler_params=grant(n, 4),
         name="first",
     )(w00)
 
@@ -225,14 +247,14 @@
     return pl.pallas_call(
         second_kernel,
         out_shape=(
-            jax.ShapeDtypeStruct((n, n), F32),
+            jax.ShapeDtypeStruct((n - n // 4, n), F32),
             jax.ShapeDtypeStruct((owned, n, n), F32),
         ),
         in_specs=[VMEM] * 3 + [HBM],
         out_specs=(VMEM, VMEM),
-        scratch_shapes=[pltpu.VMEM((n, n), F32), pltpu.SemaphoreType.DMA((owned,))],
+        scratch_shapes=[pltpu.VMEM((n, n), F32)] * 2 + [pltpu.SemaphoreType.DMA((owned,))],
         cost_estimate=factor_cost(n),
-        compiler_params=grant(n, 5 + owned),
+        compiler_params=grant(n, 6 + owned),
         name="second",
     )(inv0, w01, w11, matrix)
 
@@ -268,11 +290,11 @@
 
     @pl.when(col == 1)
     def _():
-        inv[...] = inv_own[...]
+        unpack(inv_own, inv)
 
     @pl.when(col != 1)
     def _():
-        inv[...] = inv_sib[...]
+        unpack(inv_sib, inv)
 
     line = (layer * levels + level) * (2 * near + 1)
     slot = table[line + 2 * near]
@@ -350,11 +372,11 @@
 
     @pl.when(col == 0)
     def _():
-        inv[...] = inv_own[...]
+        unpack(inv_own, inv)
 
     @pl.when(col != 0)
     def _():
-        inv[...] = inv_sib[...]
+        unpack(inv_sib, inv)
 
     inverse = split(inv[...])
     solved = three(split(t1r[...]), inverse, 1, 1)
@@ -533,8 +555,8 @@
     for pairs in rounds:
         own.append(permute(mine, pairs))
     other = sibling(mine)
-    inv0 = call_first(mine)
-    inv0_sib = permute(inv0, [((0, 0, l), (0, 1, l)) for l in range(layer_total)])
+    inv0, packed = call_first(mine)
+    inv0_sib = permute(packed, [((0, 0, l), (0, 1, l)) for l in range(layer_total)])
     inv1, tiles = call_second(inv0, other, own[1], matrix, owned)
     above = permute(
         tiles,

time: 63.8 us -> 55.8 us (0.87)
  the two profiles are of different devices: /device:TPU:0 before, /device:TPU:15 now
where the time goes in v5:
time: 55.8 us; the launch traced here: 55.4 us
  starting transfers between devices  31.7 us (57%)
  waiting for transfers between devices  15.8 us (28%)
  Pallas kernels  6.22 us (11%)
  local copies, waits for them, and re-layouts  0.98 us (2%)
    ppermute x16, starting transfers between devices, permute(): return lax.ppermute(x, AXES, [(device(*s), device(*t)) for s, t in pairs])  24.7 us
    ppermute x16, waiting for transfers between devices, permute(): return lax.ppermute(x, AXES, [(device(*s), device(*t)) for s, t in pairs])  13.9 us
    ppermute x8, starting transfers between devices, sibling(): return lax.ppermute(x, 'col', swap)  7.02 us
    pallas_call x1, Pallas kernels, call_early(): pl.pallas_call(functools.partial(early_kernel, dims), out_shape=(block, b...  3.54 us
    pallas_call x1, Pallas kernels, call_late(): pl.pallas_call(functools.partial(late_kernel, owned, col_total), out_shap...  2.52 us
    ppermute x8, waiting for transfers between devices, sibling(): return lax.ppermute(x, 'col', swap)  1.92 us
  transfers between devices with their start and end apart: 24, of which 8 were waited for; matrix products, arithmetic and copies ran while one was open for 0% of the time, Pallas kernels for 7%

profile of v5, /device:TPU:15, one launch (start us, length us, event | category | flops | bytes accessed | tf_op | source)
XLA Modules:
  0.0 55.4 jit_solution(11555806814871698699)
XLA Ops:
  0.0 0.9 %slice-done = f32[1,1,256,1,1,256]{5,4,3,2,1,0:T(1,128)S(1)} async-done(((f32[1,1,256,4,1,256]{5,4,3,2,1,0:T(1,128)}), f32[1,1,256,1,1,256]{5,4,3,2,1,0:T(1,128)S(1)}, s32[]{:S(2)}) %slice-start) | async-done | bytes 262168 | tf_op jit(solution)/shard_map/slice | solution.py:553
  1.0 0.8 %collective-permute-start.1 = (f32[256,256]{1,0:T(8,128)S(1)}, f32[256,256]{1,0:T(8,128)S(1)}, u32[]{:S(2)}, u32[]{:S(2)}) collective-permute-start(f32[256,256]{1,0:T(8,128)S(1)} %bitcast.3), channel_id=1, source_target_pairs={{6,0},{7,1},{2,10},{4,12},{3,11},{5,13}} | collective-permute-start | bytes 786440 | tf_op jit(solution)/shard_map/ppermute | solution.py:538
  1.8 1.4 %collective-permute-start = (f32[256,256]{1,0:T(8,128)S(1)}, f32[256,256]{1,0:T(8,128)S(1)}, u32[]{:S(2)}, u32[]{:S(2)}) collective-permute-start(f32[256,256]{1,0:T(8,128)S(1)} %bitcast.4), channel_id=1, source_target_pairs={{0,2},{2,0},{1,3},{3,1},{4,6},{6,4},{5,7},{7,5},{8,10},{10,8},{9,1... | collective-permute-start | bytes 786440 | tf_op jit(solution)/shard_map/ppermute | solution.py:547
  3.2 0.7 %collective-permute-start.16 = (f32[192,256]{1,0:T(8,128)S(1)}, f32[192,256]{1,0:T(8,128)S(1)}, u32[]{:S(2)}, u32[]{:S(2)}) collective-permute-start(f32[192,256]{1,0:T(8,128)S(1)} %get-tuple-element.19), channel_id=1, source_target_pairs={{0,2},{1,3}} | collective-permute-start | bytes 589832 | tf_op jit(solution)/shard_map/ppermute | solution.py:538
  3.9 1.3 %collective-permute-start.7 = (f32[256,256]{1,0:T(8,128)S(1)}, f32[256,256]{1,0:T(8,128)S(1)}, u32[]{:S(2)}, u32[]{:S(2)}) collective-permute-start(f32[256,256]{1,0:T(8,128)S(1)} %bitcast.6), channel_id=1, source_target_pairs={{2,26},{4,28},{3,27},{5,29},{8,16},{10,18},{12,20},{14,22},{17,9},... | collective-permute-start | bytes 786440 | tf_op jit(solution)/shard_map/ppermute | solution.py:538
  5.2 3.0 %collective-permute-start.8 = (f32[256,256]{1,0:T(8,128)S(1)}, f32[256,256]{1,0:T(8,128)S(1)}, u32[]{:S(2)}, u32[]{:S(2)}) collective-permute-start(f32[256,256]{1,0:T(8,128)S(1)} %bitcast.7), channel_id=1, source_target_pairs={{2,18},{4,20},{3,19},{5,21},{9,24},{11,26},{13,28},{15,30},{16,25}... | collective-permute-start | bytes 786440 | tf_op jit(solution)/shard_map/ppermute | solution.py:538
  8.1 0.7 %collective-permute-start.17 = (f32[192,256]{1,0:T(8,128)S(1)}, f32[192,256]{1,0:T(8,128)S(1)}, u32[]{:S(2)}, u32[]{:S(2)}) collective-permute-start(f32[192,256]{1,0:T(8,128)S(1)} %collective-permute-done.16), channel_id=1, source_target_pairs={{2,26},{3,27}} | collective-permute-start | bytes 589832 | tf_op jit(solution)/shard_map/ppermute | solution.py:538
  8.8 0.7 %collective-permute-start.18 = (f32[192,256]{1,0:T(8,128)S(1)}, f32[192,256]{1,0:T(8,128)S(1)}, u32[]{:S(2)}, u32[]{:S(2)}) collective-permute-start(f32[192,256]{1,0:T(8,128)S(1)} %collective-permute-done.16), channel_id=1, source_target_pairs={{2,18},{3,19}} | collective-permute-start | bytes 589832 | tf_op jit(solution)/shard_map/ppermute | solution.py:538
  9.5 0.7 %collective-permute-start.19 = (f32[192,256]{1,0:T(8,128)S(1)}, f32[192,256]{1,0:T(8,128)S(1)}, u32[]{:S(2)}, u32[]{:S(2)}) collective-permute-start(f32[192,256]{1,0:T(8,128)S(1)} %collective-permute-done.16), channel_id=1, source_target_pairs={{2,10},{3,11}} | collective-permute-start | bytes 589832 | tf_op jit(solution)/shard_map/ppermute | solution.py:538
  10.3 3.3 %collective-permute-done.7.refs_1_.refs_0_.refs_2_ = f32[256,256]{1,0:T(8,128)S(1)} collective-permute-done((f32[256,256]{1,0:T(8,128)S(1)}, f32[256,256]{1,0:T(8,128)S(1)}, u32[]{:S(2)}, u32[]{:S(2)}) %collective-permute-start.7) | collective-permute-done | bytes 262176 | tf_op jit(solution)/shard_map/ppermute | solution.py:538
  13.6 0.7 %collective-permute-start.2 = (f32[192,256]{1,0:T(8,128)S(1)}, f32[192,256]{1,0:T(8,128)S(1)}, u32[]{:S(2)}, u32[]{:S(2)}) collective-permute-start(f32[192,256]{1,0:T(8,128)S(1)} %get-tuple-element.17), channel_id=1, source_target_pairs={{0,24},{1,25}} | collective-permute-start | bytes 589832 | tf_op jit(solution)/shard_map/ppermute | solution.py:538
  14.2 4.8 %collective-permute-done.8.refs_1_.refs_3_ = f32[256,256]{1,0:T(8,128)S(1)} collective-permute-done((f32[256,256]{1,0:T(8,128)S(1)}, f32[256,256]{1,0:T(8,128)S(1)}, u32[]{:S(2)}, u32[]{:S(2)}) %collective-permute-start.8) | collective-permute-done | bytes 262176 | tf_op jit(solution)/shard_map/ppermute | solution.py:538
  19.0 0.7 %collective-permute-start.3 = (f32[192,256]{1,0:T(8,128)S(1)}, f32[192,256]{1,0:T(8,128)S(1)}, u32[]{:S(2)}, u32[]{:S(2)}) collective-permute-start(f32[192,256]{1,0:T(8,128)S(1)} %get-tuple-element.17), channel_id=1, source_target_pairs={{0,16},{1,17}} | collective-permute-start | bytes 589832 | tf_op jit(solution)/shard_map/ppermute | solution.py:538
  19.7 0.7 %collective-permute-start.4 = (f32[192,256]{1,0:T(8,128)S(1)}, f32[192,256]{1,0:T(8,128)S(1)}, u32[]{:S(2)}, u32[]{:S(2)}) collective-permute-start(f32[192,256]{1,0:T(8,128)S(1)} %get-tuple-element.17), channel_id=1, source_target_pairs={{0,8},{1,9}} | collective-permute-start | bytes 589832 | tf_op jit(solution)/shard_map/ppermute | solution.py:538
  20.4 7.4 %collective-permute-start.10 = (f32[256,256]{1,0:T(8,128)S(1)}, f32[256,256]{1,0:T(8,128)S(1)}, u32[]{:S(2)}, u32[]{:S(2)}) collective-permute-start(f32[256,256]{1,0:T(8,128)S(1)} %pick.3), channel_id=1, source_target_pairs={{24,28},{28,24},{26,30},{30,26},{9,13},{13,9},{11,15},{15,11},{17,... | collective-permute-start | bytes 786440 | tf_op jit(solution)/shard_map/ppermute | solution.py:538
  27.9 1.3 %collective-permute-start.20 = (f32[192,256]{1,0:T(8,128)S(1)}, f32[192,256]{1,0:T(8,128)S(1)}, u32[]{:S(2)}, u32[]{:S(2)}) collective-permute-start(f32[192,256]{1,0:T(8,128)S(1)} %add_add_fusion.1), channel_id=1, source_target_pairs={{2,6},{3,7},{10,14},{11,15},{18,22},{19,23},{26,30},{27,31}} | collective-permute-start | bytes 589832 | tf_op jit(solution)/shard_map/ppermute | solution.py:538
  29.3 0.7 %collective-permute-start.6 = (f32[2,256,256]{2,1,0:T(8,128)S(1)}, f32[2,256,256]{2,1,0:T(8,128)S(1)}, u32[]{:S(2)}, u32[]{:S(2)}) collective-permute-start(f32[2,256,256]{2,1,0:T(8,128)S(1)} %get-tuple-element.18), channel_id=1, source_target_pairs={{0,4},{1,5},{2,6},{3,7}} | collective-permute-start | bytes 1572872 | tf_op jit(solution)/shard_map/ppermute | solution.py:538
  30.0 4.2 %collective-permute-start.9 = (f32[256,256]{1,0:T(8,128)S(1)}, f32[256,256]{1,0:T(8,128)S(1)}, u32[]{:S(2)}, u32[]{:S(2)}) collective-permute-start(f32[256,256]{1,0:T(8,128)S(1)} %pick.2), channel_id=1, source_target_pairs={{8,12},{12,8},{10,14},{14,10},{16,20},{20,16},{18,22},{22,18},{9,1... | collective-permute-start | bytes 786440 | tf_op jit(solution)/shard_map/ppermute | solution.py:538
  34.3 2.0 %collective-permute-start.11 = (f32[256,256]{1,0:T(8,128)S(1)}, f32[256,256]{1,0:T(8,128)S(1)}, u32[]{:S(2)}, u32[]{:S(2)}) collective-permute-start(f32[256,256]{1,0:T(8,128)S(1)} %collective-permute-done.1.w11.refs_1_), channel_id=1, source_target_pairs={{0,2},{2,0},{1,3},{3,1},{4,6},{6,4},{5,7},{7,5},{8,10},{10,8},{9,1... | collective-permute-start | bytes 786440 | tf_op jit(solution)/shard_map/ppermute | solution.py:547
  36.3 1.5 %collective-permute-done.20 = f32[192,256]{1,0:T(8,128)S(1)} collective-permute-done((f32[192,256]{1,0:T(8,128)S(1)}, f32[192,256]{1,0:T(8,128)S(1)}, u32[]{:S(2)}, u32[]{:S(2)}) %collective-permute-start.20) | collective-permute-done | bytes 196640 | tf_op jit(solution)/shard_map/ppermute | solution.py:538
  37.8 4.4 %collective-permute-done.9.refs_4_ = f32[256,256]{1,0:T(8,128)S(1)} collective-permute-done((f32[256,256]{1,0:T(8,128)S(1)}, f32[256,256]{1,0:T(8,128)S(1)}, u32[]{:S(2)}, u32[]{:S(2)}) %collective-permute-start.9) | collective-permute-done | bytes 262176 | tf_op jit(solution)/shard_map/ppermute | solution.py:538
  42.2 0.7 %collective-permute-start.5 = (f32[192,256]{1,0:T(8,128)S(1)}, f32[192,256]{1,0:T(8,128)S(1)}, u32[]{:S(2)}, u32[]{:S(2)}) collective-permute-start(f32[192,256]{1,0:T(8,128)S(1)} %get-tuple-element.17), channel_id=1, source_target_pairs={{0,4},{1,5}} | collective-permute-start | bytes 589832 | tf_op jit(solution)/shard_map/ppermute | solution.py:538
  42.9 0.5 collective-permute-start.14
  43.4 0.1 collective-permute-start.21
  43.6 0.7 %collective-permute-start.22 = (f32[192,256]{1,0:T(8,128)S(1)}, f32[192,256]{1,0:T(8,128)S(1)}, u32[]{:S(2)}, u32[]{:S(2)}) collective-permute-start(f32[192,256]{1,0:T(8,128)S(1)} %add_add_fusion.2), channel_id=1, source_target_pairs={{8,12},{9,13},{16,20},{17,21},{24,28},{25,29}} | collective-permute-start | bytes 589832 | tf_op jit(solution)/shard_map/ppermute | solution.py:538
  44.2 0.2 collective-permute-done.15.refs_11_
  44.4 0.4 collective-permute-done.14.refs_10_
  44.8 0.3 collective-permute-done.21.refs_13_
  45.1 3.5 %early.1 = (f32[256,256]{1,0:T(8,128)S(1)}, f32[256,256]{1,0:T(8,128)S(1)}, f32[2,256,256]{2,1,0:T(8,128)S(1)}, f32[2,256,256]{2,1,0:T(8,128)S(1)}) custom-call(s32[40]{0:T(128)S(1)} %copy-done.1, f32[1,1,256,4,1,256]{5,4,3,2,1,0:T(1,128)S(1)} %copy-done, f32[2,256,256]{2,1,0:T(8,128)S(1)} %collective-permute-done.6.above, f32[256,256]{1,0:T(8,128)S(1)} %bitcast.9, ...), custom_call_target="tpu_custom_call" | custom-call | flops 1006632960 | bytes 8388608 | tf_op jit(solution)/shard_map/early/pallas_call | solution.py:425
  48.7 3.0 %collective-permute-start.23 = (f32[192,256]{1,0:T(8,128)S(1)}, f32[192,256]{1,0:T(8,128)S(1)}, u32[]{:S(2)}, u32[]{:S(2)}) collective-permute-start(f32[192,256]{1,0:T(8,128)S(1)} %add_add_fusion.inv_own), channel_id=1, source_target_pairs={{0,2},{2,0},{1,3},{3,1},{4,6},{6,4},{5,7},{7,5},{8,10},{10,8},{9,1... | collective-permute-start | bytes 589832 | tf_op jit(solution)/shard_map/ppermute | solution.py:547
  51.7 1.1 %collective-permute-done.23.inv_sib = f32[192,256]{1,0:T(8,128)S(1)} collective-permute-done((f32[192,256]{1,0:T(8,128)S(1)}, f32[192,256]{1,0:T(8,128)S(1)}, u32[]{:S(2)}, u32[]{:S(2)}) %collective-permute-start.23) | collective-permute-done | bytes 196640 | tf_op jit(solution)/shard_map/ppermute | solution.py:547
  52.7 2.5 %late.1 = f32[1,1,256,2,1,256]{5,4,3,2,1,0:T(1,128)} custom-call(f32[256,256]{1,0:T(8,128)S(1)} %get-tuple-element.21.p0, f32[256,256]{1,0:T(8,128)S(1)} %get-tuple-element.22.t1r, f32[2,256,256]{2,1,0:T(8,128)S(1)} %get-tuple-element.23.t1g, f32[2,256,256]{2,1,0:T(8,128)S(1)} %get-tuple-element.24.acc, f32[192,256]{1,0:T(8,128)S(1)} %add_add_fusion.inv_own, ...), custom_call_target="tpu_custom_call" | custom-call | flops 503316480 | bytes 4194304 | tf_op jit(solution)/shard_map/late/pallas_call | solution.py:445
  (33 shorter events, 0.6 us)
Async XLA Ops:
  0.0 0.9 %slice-start = ((f32[1,1,256,4,1,256]{5,4,3,2,1,0:T(1,128)}), f32[1,1,256,1,1,256]{5,4,3,2,1,0:T(1,128)S(1)}, s32[]{:S(2)}) async-start(f32[1,1,256,4,1,256]{5,4,3,2,1,0:T(1,128)} %matrix.3), calls=%async_computation | async-start | bytes 524288 | tf_op jit(solution)/shard_map/slice | solution.py:553
  1.0 9.2 %copy-start = (f32[1,1,256,4,1,256]{5,4,3,2,1,0:T(1,128)S(1)}, f32[1,1,256,4,1,256]{5,4,3,2,1,0:T(1,128)}, u32[]{:S(2)}) copy-start(f32[1,1,256,4,1,256]{5,4,3,2,1,0:T(1,128)} %matrix.3) | copy-start | bytes 3145732
  1.0 7.8 %collective-permute-start.1 = (f32[256,256]{1,0:T(8,128)S(1)}, f32[256,256]{1,0:T(8,128)S(1)}, u32[]{:S(2)}, u32[]{:S(2)}) collective-permute-start(f32[256,256]{1,0:T(8,128)S(1)} %bitcast.3), channel_id=1, source_target_pairs={{6,0},{7,1},{2,10},{4,12},{3,11},{5,13}} | collective-permute-start | bytes 786440 | tf_op jit(solution)/shard_map/ppermute | solution.py:538
  1.8 7.7 %collective-permute-start = (f32[256,256]{1,0:T(8,128)S(1)}, f32[256,256]{1,0:T(8,128)S(1)}, u32[]{:S(2)}, u32[]{:S(2)}) collective-permute-start(f32[256,256]{1,0:T(8,128)S(1)} %bitcast.4), channel_id=1, source_target_pairs={{0,2},{2,0},{1,3},{3,1},{4,6},{6,4},{5,7},{7,5},{8,10},{10,8},{9,1... | collective-permute-start | bytes 786440 | tf_op jit(solution)/shard_map/ppermute | solution.py:547
  3.2 5.0 %collective-permute-start.16 = (f32[192,256]{1,0:T(8,128)S(1)}, f32[192,256]{1,0:T(8,128)S(1)}, u32[]{:S(2)}, u32[]{:S(2)}) collective-permute-start(f32[192,256]{1,0:T(8,128)S(1)} %get-tuple-element.19), channel_id=1, source_target_pairs={{0,2},{1,3}} | collective-permute-start | bytes 589832 | tf_op jit(solution)/shard_map/ppermute | solution.py:538
  3.9 9.7 %collective-permute-start.7 = (f32[256,256]{1,0:T(8,128)S(1)}, f32[256,256]{1,0:T(8,128)S(1)}, u32[]{:S(2)}, u32[]{:S(2)}) collective-permute-start(f32[256,256]{1,0:T(8,128)S(1)} %bitcast.6), channel_id=1, source_target_pairs={{2,26},{4,28},{3,27},{5,29},{8,16},{10,18},{12,20},{14,22},{17,9},... | collective-permute-start | bytes 786440 | tf_op jit(solution)/shard_map/ppermute | solution.py:538
  5.2 13.8 %collective-permute-start.8 = (f32[256,256]{1,0:T(8,128)S(1)}, f32[256,256]{1,0:T(8,128)S(1)}, u32[]{:S(2)}, u32[]{:S(2)}) collective-permute-start(f32[256,256]{1,0:T(8,128)S(1)} %bitcast.7), channel_id=1, source_target_pairs={{2,18},{4,20},{3,19},{5,21},{9,24},{11,26},{13,28},{15,30},{16,25}... | collective-permute-start | bytes 786440 | tf_op jit(solution)/shard_map/ppermute | solution.py:538
  8.1 11.6 %collective-permute-start.17 = (f32[192,256]{1,0:T(8,128)S(1)}, f32[192,256]{1,0:T(8,128)S(1)}, u32[]{:S(2)}, u32[]{:S(2)}) collective-permute-start(f32[192,256]{1,0:T(8,128)S(1)} %collective-permute-done.16), channel_id=1, source_target_pairs={{2,26},{3,27}} | collective-permute-start | bytes 589832 | tf_op jit(solution)/shard_map/ppermute | solution.py:538
  8.8 11.6 %collective-permute-start.18 = (f32[192,256]{1,0:T(8,128)S(1)}, f32[192,256]{1,0:T(8,128)S(1)}, u32[]{:S(2)}, u32[]{:S(2)}) collective-permute-start(f32[192,256]{1,0:T(8,128)S(1)} %collective-permute-done.16), channel_id=1, source_target_pairs={{2,18},{3,19}} | collective-permute-start | bytes 589832 | tf_op jit(solution)/shard_map/ppermute | solution.py:538
  9.5 18.4 %collective-permute-start.19 = (f32[192,256]{1,0:T(8,128)S(1)}, f32[192,256]{1,0:T(8,128)S(1)}, u32[]{:S(2)}, u32[]{:S(2)}) collective-permute-start(f32[192,256]{1,0:T(8,128)S(1)} %collective-permute-done.16), channel_id=1, source_target_pairs={{2,10},{3,11}} | collective-permute-start | bytes 589832 | tf_op jit(solution)/shard_map/ppermute | solution.py:538
  13.6 15.7 %collective-permute-start.2 = (f32[192,256]{1,0:T(8,128)S(1)}, f32[192,256]{1,0:T(8,128)S(1)}, u32[]{:S(2)}, u32[]{:S(2)}) collective-permute-start(f32[192,256]{1,0:T(8,128)S(1)} %get-tuple-element.17), channel_id=1, source_target_pairs={{0,24},{1,25}} | collective-permute-start | bytes 589832 | tf_op jit(solution)/shard_map/ppermute | solution.py:538
  19.0 11.0 %collective-permute-start.3 = (f32[192,256]{1,0:T(8,128)S(1)}, f32[192,256]{1,0:T(8,128)S(1)}, u32[]{:S(2)}, u32[]{:S(2)}) collective-permute-start(f32[192,256]{1,0:T(8,128)S(1)} %get-tuple-element.17), channel_id=1, source_target_pairs={{0,16},{1,17}} | collective-permute-start | bytes 589832 | tf_op jit(solution)/shard_map/ppermute | solution.py:538
  19.7 14.5 %collective-permute-start.4 = (f32[192,256]{1,0:T(8,128)S(1)}, f32[192,256]{1,0:T(8,128)S(1)}, u32[]{:S(2)}, u32[]{:S(2)}) collective-permute-start(f32[192,256]{1,0:T(8,128)S(1)} %get-tuple-element.17), channel_id=1, source_target_pairs={{0,8},{1,9}} | collective-permute-start | bytes 589832 | tf_op jit(solution)/shard_map/ppermute | solution.py:538
  20.4 13.9 %collective-permute-start.10 = (f32[256,256]{1,0:T(8,128)S(1)}, f32[256,256]{1,0:T(8,128)S(1)}, u32[]{:S(2)}, u32[]{:S(2)}) collective-permute-start(f32[256,256]{1,0:T(8,128)S(1)} %pick.3), channel_id=1, source_target_pairs={{24,28},{28,24},{26,30},{30,26},{9,13},{13,9},{11,15},{15,11},{17,... | collective-permute-start | bytes 786440 | tf_op jit(solution)/shard_map/ppermute | solution.py:538
  27.9 9.8 %collective-permute-start.20 = (f32[192,256]{1,0:T(8,128)S(1)}, f32[192,256]{1,0:T(8,128)S(1)}, u32[]{:S(2)}, u32[]{:S(2)}) collective-permute-start(f32[192,256]{1,0:T(8,128)S(1)} %add_add_fusion.1), channel_id=1, source_target_pairs={{2,6},{3,7},{10,14},{11,15},{18,22},{19,23},{26,30},{27,31}} | collective-permute-start | bytes 589832 | tf_op jit(solution)/shard_map/ppermute | solution.py:538
  29.3 14.3 %collective-permute-start.6 = (f32[2,256,256]{2,1,0:T(8,128)S(1)}, f32[2,256,256]{2,1,0:T(8,128)S(1)}, u32[]{:S(2)}, u32[]{:S(2)}) collective-permute-start(f32[2,256,256]{2,1,0:T(8,128)S(1)} %get-tuple-element.18), channel_id=1, source_target_pairs={{0,4},{1,5},{2,6},{3,7}} | collective-permute-start | bytes 1572872 | tf_op jit(solution)/shard_map/ppermute | solution.py:538
  30.0 12.1 %collective-permute-start.9 = (f32[256,256]{1,0:T(8,128)S(1)}, f32[256,256]{1,0:T(8,128)S(1)}, u32[]{:S(2)}, u32[]{:S(2)}) collective-permute-start(f32[256,256]{1,0:T(8,128)S(1)} %pick.2), channel_id=1, source_target_pairs={{8,12},{12,8},{10,14},{14,10},{16,20},{20,16},{18,22},{22,18},{9,1... | collective-permute-start | bytes 786440 | tf_op jit(solution)/shard_map/ppermute | solution.py:538
  34.2 8.6 %collective-permute-start.12 = (f32[256,256]{1,0:T(8,128)S(1)}, f32[256,256]{1,0:T(8,128)S(1)}, u32[]{:S(2)}, u32[]{:S(2)}) collective-permute-start(f32[256,256]{1,0:T(8,128)S(1)} %collective-permute-done.7.refs_1_.refs_0_.refs_2_), channel_id=1, source_target_pairs={{0,2},{2,0},{1,3},{3,1},{4,6},{6,4},{5,7},{7,5},{8,10},{10,8},{9,1... | collective-permute-start | bytes 786440 | tf_op jit(solution)/shard_map/ppermute | solution.py:547
  34.3 8.6 %collective-permute-start.11 = (f32[256,256]{1,0:T(8,128)S(1)}, f32[256,256]{1,0:T(8,128)S(1)}, u32[]{:S(2)}, u32[]{:S(2)}) collective-permute-start(f32[256,256]{1,0:T(8,128)S(1)} %collective-permute-done.1.w11.refs_1_), channel_id=1, source_target_pairs={{0,2},{2,0},{1,3},{3,1},{4,6},{6,4},{5,7},{7,5},{8,10},{10,8},{9,1... | collective-permute-start | bytes 786440 | tf_op jit(solution)/shard_map/ppermute | solution.py:547
  37.8 5.7 %collective-permute-start.13 = (f32[256,256]{1,0:T(8,128)S(1)}, f32[256,256]{1,0:T(8,128)S(1)}, u32[]{:S(2)}, u32[]{:S(2)}) collective-permute-start(f32[256,256]{1,0:T(8,128)S(1)} %collective-permute-done.8.refs_1_.refs_3_), channel_id=1, source_target_pairs={{0,2},{2,0},{1,3},{3,1},{4,6},{6,4},{5,7},{7,5},{8,10},{10,8},{9,1... | collective-permute-start | bytes 786440 | tf_op jit(solution)/shard_map/ppermute | solution.py:547
  37.8 7.3 %copy-start.1 = (s32[40]{0:T(128)S(1)}, s32[40]{0:T(128)}, u32[]{:S(2)}) copy-start(s32[40]{0:T(128)} %constant.2.clone.table) | copy-start | bytes 484
  42.2 6.5 %collective-permute-start.5 = (f32[192,256]{1,0:T(8,128)S(1)}, f32[192,256]{1,0:T(8,128)S(1)}, u32[]{:S(2)}, u32[]{:S(2)}) collective-permute-start(f32[192,256]{1,0:T(8,128)S(1)} %get-tuple-element.17), channel_id=1, source_target_pairs={{0,4},{1,5}} | collective-permute-start | bytes 589832 | tf_op jit(solution)/shard_map/ppermute | solution.py:538
  42.8 1.6 %collective-permute-start.15 = (f32[256,256]{1,0:T(8,128)S(1)}, f32[256,256]{1,0:T(8,128)S(1)}, u32[]{:S(2)}, u32[]{:S(2)}) collective-permute-start(f32[256,256]{1,0:T(8,128)S(1)} %collective-permute-done.10.refs_5_), channel_id=1, source_target_pairs={{0,2},{2,0},{1,3},{3,1},{4,6},{6,4},{5,7},{7,5},{8,10},{10,8},{9,1... | collective-permute-start | bytes 786440 | tf_op jit(solution)/shard_map/ppermute | solution.py:547
  42.9 1.9 %collective-permute-start.14 = (f32[256,256]{1,0:T(8,128)S(1)}, f32[256,256]{1,0:T(8,128)S(1)}, u32[]{:S(2)}, u32[]{:S(2)}) collective-permute-start(f32[256,256]{1,0:T(8,128)S(1)} %collective-permute-done.9.refs_4_), channel_id=1, source_target_pairs={{0,2},{2,0},{1,3},{3,1},{4,6},{6,4},{5,7},{7,5},{8,10},{10,8},{9,1... | collective-permute-start | bytes 786440 | tf_op jit(solution)/shard_map/ppermute | solution.py:547
  43.4 1.7 %collective-permute-start.21 = (f32[192,256]{1,0:T(8,128)S(1)}, f32[192,256]{1,0:T(8,128)S(1)}, u32[]{:S(2)}, u32[]{:S(2)}) collective-permute-start(f32[192,256]{1,0:T(8,128)S(1)} %add.33.refs_12_), channel_id=1, source_target_pairs={{0,2},{2,0},{1,3},{3,1},{4,6},{6,4},{5,7},{7,5},{8,10},{10,8},{9,1... | collective-permute-start | bytes 589832 | tf_op jit(solution)/shard_map/ppermute | solution.py:547
  43.6 5.1 %collective-permute-start.22 = (f32[192,256]{1,0:T(8,128)S(1)}, f32[192,256]{1,0:T(8,128)S(1)}, u32[]{:S(2)}, u32[]{:S(2)}) collective-permute-start(f32[192,256]{1,0:T(8,128)S(1)} %add_add_fusion.2), channel_id=1, source_target_pairs={{8,12},{9,13},{16,20},{17,21},{24,28},{25,29}} | collective-permute-start | bytes 589832 | tf_op jit(solution)/shard_map/ppermute | solution.py:538
  48.7 4.0 %collective-permute-start.23 = (f32[192,256]{1,0:T(8,128)S(1)}, f32[192,256]{1,0:T(8,128)S(1)}, u32[]{:S(2)}, u32[]{:S(2)}) collective-permute-start(f32[192,256]{1,0:T(8,128)S(1)} %add_add_fusion.inv_own), channel_id=1, source_target_pairs={{0,2},{2,0},{1,3},{3,1},{4,6},{6,4},{5,7},{7,5},{8,10},{10,8},{9,1... | collective-permute-start | bytes 589832 | tf_op jit(solution)/shard_map/ppermute | solution.py:547
